TPU v7x, 512 devices: a whole 4x4x16 slice. The times are simulated.
512 devices in a mesh: frames: 128 (over z, y, core), bins: 4 (over x).
Axes of the slice: x: 4, y: 4, z: 16, core: 2. Of those that a mesh axis runs over, the one named last changes fastest.
Arguments:
- spectrum: float32 [262144, 1024], P('frames', 'bins'), may hold values from 0.01 to 4
- sign_bits: int32 [262144], P('frames'), may hold values from 0 to 1
- kept_rows: int32 [4096], replicated, may hold values from 0 to 2047, as said below
- mask: int32 [352, 1024], P(None, 'bins'), may hold values 0 or 1
- w_init: float32 [4096, 352], P('frames'), may hold values from 0.02 to 0.2
- h_init: float32 [352, 1024], P(None, 'bins'), may hold values from 0.02 to 0.2
Outputs:
- activations: float32 [4096, 352], P('frames')
- templates: float32 [352, 1024], P(None, 'bins')
Inputs may be any that keep to these rules, and one draw needn't show every extreme that they name: `kept_rows`: rows i * 32 to (i + 1) * 32 - 1 hold distinct positions, so each block of 2048 frames gives exactly 32 distinct sketch rows.
All inputs are finite; a program needn't handle non-finite values. No bound on the sum of `mask` on one device may be relied on, other than what follows from the above.
Results may differ from a plain program's by a relative error of at most 0.0001.
Values sent between devices are 32-bit elements; how exact they have to be, the bound alone decides.
No kernel may reach another device: no remote copies, remote signals or barrier semaphores. Data moves between devices by JAX's collectives and lax.ppermute only.
A program may use at most 64 MiB of HBM per device.

v0:
```python
import jax
import jax.numpy as jnp
from jax import lax
from jax.sharding import PartitionSpec as P

ITERS = 2


def partner_2(value, axis, apart):
    return lax.ppermute(value, axis, [(i, i ^ 1 << apart) for i in range(lax.axis_size(axis))])


def parity_bits(left, right, width):
    joint = jnp.bitwise_and(left, right)
    total = jnp.zeros(joint.shape, jnp.int32)
    for position in range(width):
        total = jnp.bitwise_xor(total, jnp.bitwise_and(jnp.right_shift(joint, position), 1))
    return total


def hadamard(count):
    index = jnp.arange(count, dtype=jnp.int32)
    bits = parity_bits(index[:, None], index[None, :], max(count.bit_length(), 1))
    return (1 - 2 * bits).astype(jnp.float32)


def body(spectrum, sign_bits, kept_rows, mask, w_init, h_init):
    damping = 1.0
    high = lax.Precision.HIGHEST
    block_count = lax.axis_size("frames")
    position = lax.axis_index("frames")
    frame_rows = spectrum.shape[0]
    sketch_rows = kept_rows.shape[0]
    per_block = sketch_rows // block_count
    signed = spectrum * (1 - 2 * sign_bits).astype(jnp.float32)[:, None]
    local = jnp.dot(hadamard(frame_rows), signed, precision=high)
    partial_value = local
    for level in range(block_count.bit_length() - 1):
        partner = partner_2(partial_value, "frames", level)
        upper = jnp.bitwise_and(jnp.right_shift(position, level), 1) == 1
        partial_value = jnp.where(upper, partner - partial_value, partial_value + partner)
    own_rows = lax.dynamic_slice_in_dim(kept_rows, position * per_block, per_block)
    sketch = jnp.take(partial_value, own_rows, axis=0)
    sketch = sketch / jnp.sqrt(jnp.float32(frame_rows * block_count))
    templates = h_init * mask.astype(jnp.float32)
    activations = w_init
    for round_index in range(ITERS):
        gram_h, proj = lax.psum(
            (
                jnp.dot(templates, templates.T, precision=high),
                jnp.dot(sketch, templates.T, precision=high),
            ),
            "bins",
        )
        lower = jnp.maximum(-proj, 0.0) + jnp.dot(activations, gram_h, precision=high) + damping
        activations = activations * jnp.sqrt((jnp.maximum(proj, 0.0) + damping) / lower)
        cross, gram_w = lax.psum(
            (
                jnp.dot(activations.T, sketch, precision=high),
                jnp.dot(activations.T, activations, precision=high),
            ),
            "frames",
        )
        lower = jnp.maximum(-cross, 0.0) + jnp.dot(gram_w, templates, precision=high) + damping
        templates = templates * jnp.sqrt((jnp.maximum(cross, 0.0) + damping) / lower)
    return (activations, templates)


def solution(mesh):
    in_specs = (
        P("frames", "bins"),
        P("frames"),
        P(),
        P(None, "bins"),
        P("frames", None),
        P(None, "bins"),
    )
    out_specs = (P("frames", None), P(None, "bins"))
    return jax.shard_map(body, mesh=mesh, in_specs=in_specs, out_specs=out_specs, check_vma=False)
```

profile of v0, /device:TPU:1, one launch (start us, length us, event | category | flops | bytes accessed | tf_op | source)
XLA Modules:
  0.0 1724.5 jit_solution(9883276830763627282)
XLA Ops:
  7.2 0.0 all-reduce.7.cloned.1.call-start
  7.2 0.7 subtract_convert_fusion
  7.9 254.3 %fusion = f32[2048,256]{1,0:T(8,128)S(1)} fusion(f32[2048,256]{1,0:T(8,128)} %param.6, f32[2048]{0:T(1024)S(1)} %subtract_convert_fusion), kind=kOutput, calls=%fused_computation.1 | convolution fusion | flops 13049004032 | bytes 4202496 | tf_op jit(solution)/shard_map/dot_general | solution.py:36
  262.2 0.0 copy-start.1
  262.2 8.8 collective-permute-start
  271.0 0.0 copy-done.1
  271.0 3.9 collective-permute-done
  274.9 2.5 add_select_fusion.6
  277.4 0.0 copy-start
  277.4 1.9 collective-permute-start.1
  279.4 0.0 copy-done
  279.4 46.9 %collective-permute-done.1 = f32[2048,256]{1,0:T(8,128)} collective-permute-done((f32[2048,256]{1,0:T(8,128)S(1)}, f32[2048,256]{1,0:T(8,128)}, u32[]{:S(2)}, u32[]{:S(2)}) %collective-permute-start.1) | collective-permute-done | bytes 2097184 | tf_op jit(solution)/shard_map/ppermute | solution.py:10
  326.3 2.5 add_select_fusion.5
  328.8 1.9 collective-permute-start.2
  330.7 47.5 %collective-permute-done.2 = f32[2048,256]{1,0:T(8,128)} collective-permute-done((f32[2048,256]{1,0:T(8,128)S(1)}, f32[2048,256]{1,0:T(8,128)}, u32[]{:S(2)}, u32[]{:S(2)}) %collective-permute-start.2) | collective-permute-done | bytes 2097184 | tf_op jit(solution)/shard_map/ppermute | solution.py:10
  378.2 3.2 add_select_fusion.4
  381.4 1.9 collective-permute-start.3
  383.3 45.3 %collective-permute-done.3 = f32[2048,256]{1,0:T(8,128)} collective-permute-done((f32[2048,256]{1,0:T(8,128)}, f32[2048,256]{1,0:T(8,128)}, u32[]{:S(2)}, u32[]{:S(2)}) %collective-permute-start.3) | collective-permute-done | bytes 2097184 | tf_op jit(solution)/shard_map/ppermute | solution.py:10
  428.6 2.5 add_select_fusion.3
  431.1 1.9 collective-permute-start.4
  433.0 93.4 %collective-permute-done.4 = f32[2048,256]{1,0:T(8,128)} collective-permute-done((f32[2048,256]{1,0:T(8,128)S(1)}, f32[2048,256]{1,0:T(8,128)}, u32[]{:S(2)}, u32[]{:S(2)}) %collective-permute-start.4) | collective-permute-done | bytes 2097184 | tf_op jit(solution)/shard_map/ppermute | solution.py:10
  526.5 3.2 add_select_fusion.2
  529.6 3.4 collective-permute-start.5
  533.0 0.0 copy-start.2
  533.1 0.0 copy-start.3
  533.1 227.6 %collective-permute-done.5 = f32[2048,256]{1,0:T(8,128)} collective-permute-done((f32[2048,256]{1,0:T(8,128)}, f32[2048,256]{1,0:T(8,128)}, u32[]{:S(2)}, u32[]{:S(2)}) %collective-permute-start.5) | collective-permute-done | bytes 2097184 | tf_op jit(solution)/shard_map/ppermute | solution.py:10
  760.7 2.5 add_select_fusion.1
  763.2 10.8 collective-permute-start.6
  774.0 0.0 copy-done.2
  774.0 0.0 copy-done.3
  774.0 1.5 fusion.109
  775.6 0.0 all-reduce.7.cloned.1.call-update
  775.6 0.0 all-reduce.13.cloned.1.call-start
  775.6 0.8 compare_and_fusion
  776.4 0.0 copy-start.5
  776.4 80.0 %collective-permute-done.6 = f32[2048,256]{1,0:T(8,128)} collective-permute-done((f32[2048,256]{1,0:T(8,128)S(1)}, f32[2048,256]{1,0:T(8,128)}, u32[]{:S(2)}, u32[]{:S(2)}) %collective-permute-start.6) | collective-permute-done | bytes 2097184 | tf_op jit(solution)/shard_map/ppermute | solution.py:10
  856.5 3.2 add_select_fusion
  859.6 2.2 gather_fusion
  861.8 0.4 fusion.76
  862.3 111.7 %psum.56 = f32[32,352]{1,0:T(8,128)S(1)} all-reduce(f32[32,352]{1,0:T(8,128)S(1)} %fusion.76), channel_id=1, replica_groups=mesh['frames'=128,'bins'=4] {'bins'}, use_global_device_ids=true, to_apply=%region_0.1 | all-reduce | flops 11264 | bytes 90112 | tf_op jit(solution)/shard_map/psum | solution.py:48
  974.0 0.0 all-reduce.7.cloned.1.call-done
  974.0 0.0 copy-done.5
  974.0 1.5 fusion.67
  975.6 1.3 fusion.75
  976.8 1.4 fusion.110
  978.3 0.0 all-reduce.13.cloned.1.call-update
  978.3 0.0 all-reduce.9.cloned.1.call-start
  978.3 334.9 %all-reduce.13.cloned.1.call-done = (f32[352,352]{1,0:T(8,128)}, f32[352,256]{1,0:T(8,128)}) async-done(((f32[352,352]{1,0:T(8,128)}, f32[352,256]{1,0:T(8,128)}), (f32[352,352]{1,0:T(8,128)}, f32[352,256]{1,0:T(8,128)})) %all-reduce.13.cloned.1.call-update) | async-done | bytes 856080 | tf_op jit(solution)/shard_map/psum | solution.py:57
  1313.2 2.0 fusion.58
  1315.3 1.5 fusion.111
  1316.8 0.0 all-reduce.9.cloned.1.call-update
  1316.8 0.0 all-reduce.11.cloned.1.call-start
  1316.9 0.4 fusion.74
  1317.3 13.6 psum.60
  1330.9 40.4 %all-reduce.9.cloned.1.call-done = f32[352,352]{1,0:T(8,128)} async-done(((f32[352,352]{1,0:T(8,128)}), f32[352,352]{1,0:T(8,128)}) %all-reduce.9.cloned.1.call-update) | async-done | bytes 495632 | tf_op jit(solution)/shard_map/psum | solution.py:48
  1371.3 1.5 fusion.71
  1372.8 0.0 copy-start.4
  1372.8 1.3 fusion.73
  1374.0 1.4 fusion.112
  1375.5 0.0 all-reduce.11.cloned.1.call-update
  1375.5 339.7 %all-reduce.11.cloned.1.call-done = (f32[352,352]{1,0:T(8,128)}, f32[352,256]{1,0:T(8,128)}) async-done(((f32[352,352]{1,0:T(8,128)}, f32[352,256]{1,0:T(8,128)}), (f32[352,352]{1,0:T(8,128)}, f32[352,256]{1,0:T(8,128)})) %all-reduce.11.cloned.1.call-update) | async-done | bytes 856080 | tf_op jit(solution)/shard_map/psum | solution.py:57
  1715.2 2.8 fusion.62
  1718.0 0.0 copy-done.4
  (1 shorter events, 0.0 us)
Async XLA Ops:
  7.2 966.9 %all-reduce.7.cloned.1.call-start = ((), (), s32[]{:S(2)}) async-start(), calls=%async_computation | async-start | bytes 1081344 | tf_op jit(solution)/shard_map/psum | solution.py:48
  262.2 8.8 copy-start.1
  262.2 12.7 collective-permute-start
  277.4 1.9 copy-start
  277.4 48.8 %collective-permute-start.1 = (f32[2048,256]{1,0:T(8,128)S(1)}, f32[2048,256]{1,0:T(8,128)}, u32[]{:S(2)}, u32[]{:S(2)}) collective-permute-start(f32[2048,256]{1,0:T(8,128)S(1)} %add_select_fusion.6), channel_id=1, source_target_pairs={{0,8},{4,12},{8,0},{12,4},{16,24},{20,28},{24,16},{28,20},{32,40},... | collective-permute-start | bytes 6291464 | tf_op jit(solution)/shard_map/ppermute | solution.py:10
  328.8 49.4 %collective-permute-start.2 = (f32[2048,256]{1,0:T(8,128)S(1)}, f32[2048,256]{1,0:T(8,128)}, u32[]{:S(2)}, u32[]{:S(2)}) collective-permute-start(f32[2048,256]{1,0:T(8,128)S(1)} %add_select_fusion.5), channel_id=1, source_target_pairs={{0,16},{4,20},{8,24},{12,28},{16,0},{20,4},{24,8},{28,12},{32,48},... | collective-permute-start | bytes 6291464 | tf_op jit(solution)/shard_map/ppermute | solution.py:10
  381.4 47.2 %collective-permute-start.3 = (f32[2048,256]{1,0:T(8,128)}, f32[2048,256]{1,0:T(8,128)}, u32[]{:S(2)}, u32[]{:S(2)}) collective-permute-start(f32[2048,256]{1,0:T(8,128)} %add_select_fusion.4), channel_id=1, source_target_pairs={{0,32},{4,36},{8,40},{12,44},{16,48},{20,52},{24,56},{28,60},{32,0... | collective-permute-start | bytes 6291464 | tf_op jit(solution)/shard_map/ppermute | solution.py:10
  431.1 95.4 %collective-permute-start.4 = (f32[2048,256]{1,0:T(8,128)S(1)}, f32[2048,256]{1,0:T(8,128)}, u32[]{:S(2)}, u32[]{:S(2)}) collective-permute-start(f32[2048,256]{1,0:T(8,128)S(1)} %add_select_fusion.3), channel_id=1, source_target_pairs={{0,64},{4,68},{8,72},{12,76},{16,80},{20,84},{24,88},{28,92},{32,9... | collective-permute-start | bytes 6291464 | tf_op jit(solution)/shard_map/ppermute | solution.py:10
  529.6 231.1 %collective-permute-start.5 = (f32[2048,256]{1,0:T(8,128)}, f32[2048,256]{1,0:T(8,128)}, u32[]{:S(2)}, u32[]{:S(2)}) collective-permute-start(f32[2048,256]{1,0:T(8,128)} %add_select_fusion.2), channel_id=1, source_target_pairs={{0,128},{4,132},{8,136},{12,140},{16,144},{20,148},{24,152},{28,15... | collective-permute-start | bytes 6291464 | tf_op jit(solution)/shard_map/ppermute | solution.py:10
  533.0 240.9 %copy-start.2 = (f32[352,256]{1,0:T(8,128)S(1)}, f32[352,256]{1,0:T(8,128)}, u32[]{:S(2)}) copy-start(f32[352,256]{1,0:T(8,128)} %param.11) | copy-start | bytes 1081348
  533.1 240.9 %copy-start.3 = (s32[352,256]{1,0:T(8,128)S(1)}, s32[352,256]{1,0:T(8,128)}, u32[]{:S(2)}) copy-start(s32[352,256]{1,0:T(8,128)} %param.9) | copy-start | bytes 1081348
  763.2 93.2 %collective-permute-start.6 = (f32[2048,256]{1,0:T(8,128)S(1)}, f32[2048,256]{1,0:T(8,128)}, u32[]{:S(2)}, u32[]{:S(2)}) collective-permute-start(f32[2048,256]{1,0:T(8,128)S(1)} %add_select_fusion.1), channel_id=1, source_target_pairs={{0,256},{4,260},{8,264},{12,268},{16,272},{20,276},{24,280},{28,28... | collective-permute-start | bytes 6291464 | tf_op jit(solution)/shard_map/ppermute | solution.py:10
  775.6 537.6 %all-reduce.13.cloned.1.call-start = ((), (), s32[]{:S(2)}) async-start(), calls=%async_computation.3 | async-start | bytes 1802240 | tf_op jit(solution)/shard_map/psum | solution.py:57
  776.4 197.6 %copy-start.5 = (f32[32,352]{1,0:T(8,128)S(1)}, f32[32,352]{1,0:T(8,128)}, u32[]{:S(2)}) copy-start(f32[32,352]{1,0:T(8,128)} %param.10) | copy-start | bytes 135172
  978.3 393.0 %all-reduce.9.cloned.1.call-start = ((), (), s32[]{:S(2)}) async-start(), calls=%async_computation.1 | async-start | bytes 1081344 | tf_op jit(solution)/shard_map/psum | solution.py:48
  1316.8 398.4 %all-reduce.11.cloned.1.call-start = ((), (), s32[]{:S(2)}) async-start(), calls=%async_computation.2 | async-start | bytes 1802240 | tf_op jit(solution)/shard_map/psum | solution.py:57
  1372.8 345.2 %copy-start.4 = (f32[32,352]{1,0:T(8,128)}, f32[32,352]{1,0:T(8,128)S(1)}, u32[]{:S(2)}) copy-start(f32[32,352]{1,0:T(8,128)S(1)} %fusion.71) | copy-start | bytes 135172
Sparse Core Ops, SparseCore 0:
  775.7 138.5 all-reduce.6
  978.4 334.7 all-reduce.12
  1316.9 54.2 all-reduce.8
  1375.6 339.5 all-reduce.10
where the time goes:
time: 1740 us; the launch traced here: 1720 us
  waiting for transfers between devices  1260 us (72%)
  matrix products  271 us (16%)
  blocking collectives  125 us (7%)
  starting transfers between devices  30.8 us (2%)
  other arithmetic  21 us (1%)
    psum x2, waiting for transfers between devices, body(): lax.psum((jnp.dot(activations.T, sketch, precision=high), jnp.dot(activat...  675 us
    ppermute x7, waiting for transfers between devices, partner_2(): lax.ppermute(value, axis, [(i, i ^ 1 << apart) for i in range(lax.axis_si...  545 us
    dot_general x1, matrix products, body(): local = jnp.dot(hadamard(frame_rows), signed, precision=high)  254 us
    psum x2, blocking collectives, body(): lax.psum((jnp.dot(templates, templates.T, precision=high), jnp.dot(sketch...  125 us
    psum x2, waiting for transfers between devices, body(): lax.psum((jnp.dot(templates, templates.T, precision=high), jnp.dot(sketch...  40.4 us
  transfers between devices with their start and end apart: 11, of which 10 were waited for; matrix products, arithmetic and copies ran while one was open for 0% of the time, Pallas kernels for 0%

commit v1 on v0

v1 whole, which is shorter than its diff:
```python
import numpy as np
import jax
import jax.numpy as jnp
from jax import lax
from jax.experimental import pallas as pl
from jax.experimental.pallas import tpu as pltpu
from jax.sharding import Mesh
from jax.sharding import PartitionSpec as P

ITERS = 2
FINE = 256
SHARE = 128


def sylvester(count):
    matrix = np.ones((1, 1), np.float32)
    while matrix.shape[0] < count:
        matrix = np.block([[matrix, matrix], [matrix, -matrix]])
    return matrix


def shift(axis, by):
    count = lax.axis_size(axis)
    return [(i, (i + by) % count) for i in range(count)]


def signs_of(position, count):
    rows = jnp.asarray(sylvester(count))
    row = lax.dynamic_slice_in_dim(rows, position, 1, axis=0)[0]
    return [row[i] for i in range(count)]


def split2(value):
    high = value.astype(jnp.bfloat16)
    low = (value - high.astype(jnp.float32)).astype(jnp.bfloat16)
    return high, low


def mix_kernel(rows_ref, sign_ref, own_ref, other_ref, fine_ref, out_ref, work_ref):
    frames = own_ref.shape[0]
    coarse = frames // FINE
    sign = sign_ref[0]
    for part in range(coarse):
        here = pl.ds(part * FINE, FINE)
        own = own_ref[here, :]
        other = other_ref[here, :]
        upper = own + other
        lower = (own - other) * sign
        pieces = jnp.concatenate([*split2(upper), *split2(lower)], axis=1)
        done = jnp.dot(fine_ref[...], pieces, preferred_element_type=jnp.float32)
        work_ref[here, :] = done[:, :SHARE] + done[:, SHARE : 2 * SHARE]
        work_ref[pl.ds(frames + part * FINE, FINE), :] = done[:, 2 * SHARE : 3 * SHARE] + done[:, 3 * SHARE :]
    step = 32
    for base in (0, frames):
        def stage(i, carry, base=base):
            at = [pl.ds(pl.multiple_of(base + part * FINE + i * step, 8), step) for part in range(coarse)]
            values = [work_ref[a, :] for a in at]
            apart = 1
            while apart < coarse:
                new = list(values)
                for j in range(coarse):
                    if not j & apart:
                        new[j] = values[j] + values[j | apart]
                        new[j | apart] = values[j] - values[j | apart]
                values = new
                apart *= 2
            for a, v in zip(at, values):
                work_ref[a, :] = v
            return carry

        lax.fori_loop(0, FINE // step, stage, 0)
    group = 16

    def pick(i, carry):
        first = pl.multiple_of(i * group, group)
        found = [work_ref[pl.ds(rows_ref[first + j], 1), :] for j in range(group)]
        out_ref[pl.ds(first, group), :] = jnp.concatenate(found, axis=0)
        return carry

    lax.fori_loop(0, out_ref.shape[0] // group, pick, 0)


def mix(own, other, sign, rows):
    frames = own.shape[0]
    count = rows.shape[0]
    vmem = pl.BlockSpec(memory_space=pltpu.VMEM)
    smem = pl.BlockSpec(memory_space=pltpu.SMEM)
    return pl.pallas_call(
        mix_kernel,
        out_shape=jax.ShapeDtypeStruct((count, SHARE), jnp.float32),
        in_specs=[smem, smem, vmem, vmem, vmem],
        out_specs=vmem,
        scratch_shapes=[pltpu.VMEM((2 * frames, SHARE), jnp.float32)],
        compiler_params=pltpu.CompilerParams(vmem_limit_bytes=24 << 20),
    )(rows, sign, own, other, jnp.asarray(sylvester(FINE), jnp.bfloat16))


def times(a, b, dims):
    return lax.dot_general(a, b, (dims, ((), ())), precision=lax.Precision.HIGH, preferred_element_type=jnp.float32)


def ratio(signed, total):
    damping = 1.0
    return jnp.sqrt((jnp.maximum(signed, 0.0) + damping) / (jnp.maximum(-signed, 0.0) + total + damping))


def by_core(core, own, other):
    return jnp.where(core == 0, jnp.concatenate([own, other], axis=-1), jnp.concatenate([other, own], axis=-1))


def body(spectrum, sign_bits, kept_rows, mask, w_init, h_init):
    n_z, n_y = lax.axis_size("z"), lax.axis_size("y")
    at_y, at_z, core = lax.axis_index("y"), lax.axis_index("z"), lax.axis_index("core")
    swap = [(0, 1), (1, 0)]
    frames = spectrum.shape[0]
    per_block = kept_rows.shape[0] // (n_z * n_y * 2)
    k = h_init.shape[0]
    mine, theirs = core * SHARE, (1 - core) * SHARE

    def across(value):
        return [value] + [lax.ppermute(value, "x", shift("x", by)) for by in range(1, lax.axis_size("x"))]

    signed = spectrum * (1 - 2 * sign_bits).astype(jnp.float32)[:, None]
    own = lax.dynamic_slice_in_dim(signed, mine, SHARE, axis=1)
    other = lax.ppermute(lax.dynamic_slice_in_dim(signed, theirs, SHARE, axis=1), "core", swap)
    rows = kept_rows.reshape(n_z, n_y, 2, per_block) + (jnp.arange(2, dtype=jnp.int32) * frames)[:, None]
    rows = rows.transpose(1, 0, 2, 3).reshape(-1)
    partial_rows = mix(own, other, (1 - 2 * core).astype(jnp.float32).reshape(1), rows)

    got = lax.all_to_all(partial_rows.reshape(n_y, -1, SHARE), "y", 0, 0)
    partial_rows = sum(s * got[i] for i, s in enumerate(signs_of(at_y, n_y)))
    got = lax.all_to_all(partial_rows.reshape(n_z, -1, SHARE), "z", 0, 0)
    z_signs = lax.dynamic_slice_in_dim(jnp.asarray(sylvester(n_z)), at_z, 1, axis=0)[0]
    sketch = jnp.sum(got * z_signs[:, None, None], axis=0)
    sketch = sketch / jnp.sqrt(jnp.float32(frames * n_z * n_y * 2))
    keep = lax.dynamic_slice_in_dim(sketch, core * per_block, per_block)
    give = lax.dynamic_slice_in_dim(sketch, (1 - core) * per_block, per_block)
    sketch = by_core(core, keep, lax.ppermute(give, "core", swap))

    gathered = lax.all_gather(jnp.concatenate([sketch, w_init], axis=1), "z", tiled=True)
    sketch = across(gathered[:, : sketch.shape[1]])
    activations = gathered[:, sketch[0].shape[1] :]
    templates = across(h_init * mask.astype(jnp.float32))
    for round_index in range(ITERS):
        sketch_all = jnp.concatenate(sketch, axis=1)
        templates_all = jnp.concatenate(templates, axis=1)
        proj = times(sketch_all, templates_all, ((1,), (1,)))
        model = times(activations, templates_all, ((1,), (0,)))
        activations = activations * ratio(proj, times(model, templates_all, ((1,), (1,))))
        cross = times(activations, sketch[0], ((0,), (0,)))
        model = times(activations, templates[0], ((1,), (0,)))
        total = times(activations, model, ((0,), (0,)))

        def half(at):
            return jnp.concatenate([lax.dynamic_slice_in_dim(v, at, SHARE, axis=1) for v in (cross, total)], axis=1)

        both = half(mine) + lax.ppermute(half(theirs), "core", swap)
        both = jnp.sum(lax.all_to_all(both.reshape(n_y, k // n_y, 2 * SHARE), "y", 0, 0), axis=0)
        piece = lax.dynamic_slice(templates[0], (at_y * (k // n_y), mine), (k // n_y, SHARE))
        piece = piece * ratio(both[:, :SHARE], both[:, SHARE:])
        piece = lax.all_gather(piece, "y", tiled=True)
        if round_index == ITERS - 1:
            templates = [by_core(core, piece, lax.ppermute(piece, "core", swap))]
        else:
            pieces = jnp.stack(across(piece))
            other = lax.ppermute(pieces, "core", swap)
            templates = [by_core(core, pieces[i], other[i]) for i in range(pieces.shape[0])]
    activations = lax.dynamic_slice_in_dim(activations, at_z * per_block, per_block)
    return (activations, templates[0])


def solution(mesh):
    torus = Mesh(mesh.devices.reshape(16, 4, 2, 4), ("z", "y", "core", "x"))
    frames = ("z", "y", "core")
    in_specs = (P(frames, "x"), P(frames), P(), P(None, "x"), P(frames, None), P(None, "x"))
    out_specs = (P(frames, None), P(None, "x"))
    return jax.shard_map(body, mesh=torus, in_specs=in_specs, out_specs=out_specs, check_vma=False)
```

time: 1740 us -> 298 us (0.17)
  waiting for transfers between devices: 1260 us -> 122 us
  matrix products: 271 us -> 18.4 us
  blocking collectives: 125 us -> 28.2 us
  starting transfers between devices: 30.8 us -> 90 us
    psum x4 -> x0, waiting for transfers between devices: 715 us -> none  [the longest x2 675 us: body(): lax.psum((jnp.dot(activations.T, sketch, precision=high), jnp.dot(activat...]
    ppermute x7 -> x15, waiting for transfers between devices: 545 us -> 21.8 us  [the longest x9 14.7 us: across(): lax.ppermute(value, 'x', shift('x', by))]
    dot_general x13 -> x12, matrix products: 271 us -> 18.4 us  [times(): lax.dot_general(a, b, (dims, ((), ())), precision=lax.Precision.HIGH, pre...]
    psum x2 -> x0, blocking collectives: 125 us -> none  [body(): lax.psum((jnp.dot(templates, templates.T, precision=high), jnp.dot(sketch...]
    all_to_all x0 -> x3, waiting for transfers between devices: none -> 53.3 us  [the longest x1 24.7 us: body(): got = lax.all_to_all(partial_rows.reshape(n_y, -1, SHARE), 'y', 0, 0)]
    all_gather x0 -> x1, waiting for transfers between devices: none -> 47.3 us  [body(): lax.all_gather(jnp.concatenate([sketch, w_init], axis=1), 'z', tiled=True)]
    ppermute x7 -> x15, starting transfers between devices: 30.6 us -> 72.4 us  [the longest x9 25.4 us: across(): lax.ppermute(value, 'x', shift('x', by))]
    all_gather x0 -> x2, blocking collectives: none -> 18.8 us  [body(): piece = lax.all_gather(piece, 'y', tiled=True)]
  transfers between devices with their start and end apart: 11 -> 19, of which waited for: 10 -> 14; matrix products, arithmetic and copies ran while one was open for 0% -> 3% of each run, Pallas kernels for 0% -> 0%
where the time goes in v1:
time: 298 us; the launch traced here: 296 us
  waiting for transfers between devices  122 us (41%)
  starting transfers between devices  90 us (30%)
  blocking collectives  28.2 us (9%)
  matrix products  18.4 us (6%)
  between operations  14.6 us (5%)
  other arithmetic  9.03 us (3%)
  Pallas kernels  7.92 us (3%)
  local copies, waits for them, and re-layouts  5.82 us (2%)
    all_gather x1, waiting for transfers between devices, body(): lax.all_gather(jnp.concatenate([sketch, w_init], axis=1), 'z', tiled=True)  47.3 us
    ppermute x9, starting transfers between devices, across(): lax.ppermute(value, 'x', shift('x', by))  25.4 us
    all_to_all x1, waiting for transfers between devices, body(): got = lax.all_to_all(partial_rows.reshape(n_y, -1, SHARE), 'y', 0, 0)  24.7 us
    all_to_all x1, waiting for transfers between devices, body(): got = lax.all_to_all(partial_rows.reshape(n_z, -1, SHARE), 'z', 0, 0)  21.8 us
    all_gather x2, blocking collectives, body(): piece = lax.all_gather(piece, 'y', tiled=True)  18.8 us
    dot_general x12, matrix products, times(): lax.dot_general(a, b, (dims, ((), ())), precision=lax.Precision.HIGH, pre...  18.4 us
    ppermute x2, starting transfers between devices, body(): both = half(mine) + lax.ppermute(half(theirs), 'core', swap)  15.3 us
    ppermute x9, waiting for transfers between devices, across(): lax.ppermute(value, 'x', shift('x', by))  14.7 us
  transfers between devices with their start and end apart: 19, of which 14 were waited for; matrix products, arithmetic and copies ran while one was open for 3% of the time, Pallas kernels for 0%

profile of v1, /device:TPU:1, one launch (start us, length us, event | category | flops | bytes accessed | tf_op | source)
XLA Modules:
  0.0 296.4 jit_solution(13702519381585351411)
XLA Ops:
  7.2 0.7 subtract_convert_fusion
  7.9 1.9 broadcast_multiply_fusion
  9.8 0.1 constant_dynamic-slice_fusion.12
  10.0 8.8 %collective-permute-start = (f32[2048,128]{1,0:T(8,128)S(1)}, f32[2048,128]{1,0:T(8,128)S(1)}, u32[]{:S(2)}, u32[]{:S(2)}) collective-permute-start(f32[2048,128]{1,0:T(8,128)S(1)} %get-tuple-element.10), channel_id=1, source_target_pairs={{0,4},{4,0},{1,5},{5,1},{2,6},{6,2},{3,7},{7,3},{8,12},{12,8},{9,1... | collective-permute-start | bytes 3145736 | tf_op jit(solution)/shard_map/ppermute | solution.py:125
  18.8 0.1 reshape.52
  19.0 0.1 reshape.53.rows_ref
  19.2 1.9 collective-permute-done.other_ref
  21.0 7.9 %shard_map.104 = f32[4096,128]{1,0:T(8,128)} custom-call(s32[4096]{0:T(1024)S(1)} %reshape.53.rows_ref, f32[1]{0:T(128)} %bitcast.2.sign_ref, f32[2048,128]{1,0:T(8,128)S(1)} %get-tuple-element.11.own_ref, f32[2048,128]{1,0:T(8,128)S(1)} %collective-permute-done.other_ref, bf16[256,256]{1,0:T(8,128)(2,1)S(1)} %copy-done), custom_call_target="tpu_custom_call" | custom-call | tf_op jit(solution)/shard_map/pallas_call | solution.py:88
  29.0 3.6 %all-to-all-start = ((f32[4,1024,128]{2,1,0:T(8,128)}), f32[4,1024,128]{2,1,0:T(8,128)S(1)}, u32[]{:S(2)}, u32[]{:S(2)}) async-start(f32[4,1024,128]{2,1,0:T(8,128)} %bitcast.3), calls=%async_computation | async-start | bytes 4194304 | tf_op jit(solution)/shard_map/all_to_all | solution.py:130
  32.6 0.7 constant_dynamic-slice_fusion.14
  33.3 0.7 fusion.29
  34.0 24.7 %all-to-all-done = f32[4,1024,128]{2,1,0:T(8,128)S(1)} async-done(((f32[4,1024,128]{2,1,0:T(8,128)}), f32[4,1024,128]{2,1,0:T(8,128)S(1)}, u32[]{:S(2)}, u32[]{:S(2)}) %all-to-all-start) | async-done | bytes 2097184 | tf_op jit(solution)/shard_map/all_to_all | solution.py:130
  58.6 3.6 %fusion.2 = f32[1,1024,128]{2,1,0:T(8,128)} fusion(f32[4,1024,128]{2,1,0:T(8,128)S(1)} %all-to-all-done, f32[]{:T(128)} %bitcast.6, f32[]{:T(128)} %bitcast.5, f32[]{:T(128)} %bitcast.4, f32[]{:T(128)} %bitcast), kind=kLoop, calls=%fused_computation.10 | loop fusion | flops 917504 | bytes 2621456 | tf_op jit(solution)/shard_map/add | solution.py:131
  62.2 9.9 %all-to-all-start.1 = ((f32[16,64,128]{2,1,0:T(8,128)}), f32[16,64,128]{2,1,0:T(8,128)S(1)}, u32[]{:S(2)}, u32[]{:S(2)}) async-start(f32[16,64,128]{2,1,0:T(8,128)} %bitcast.7), calls=%async_computation.1 | async-start | bytes 1048576 | tf_op jit(solution)/shard_map/all_to_all | solution.py:132
  72.2 0.7 fusion.17
  72.9 21.8 %all-to-all-done.1 = f32[16,64,128]{2,1,0:T(8,128)S(1)} async-done(((f32[16,64,128]{2,1,0:T(8,128)}), f32[16,64,128]{2,1,0:T(8,128)S(1)}, u32[]{:S(2)}, u32[]{:S(2)}) %all-to-all-start.1) | async-done | bytes 524320 | tf_op jit(solution)/shard_map/all_to_all | solution.py:132
  94.9 8.7 %collective-permute-start.1 = (f32[32,128]{1,0:T(8,128)S(1)}, f32[32,128]{1,0:T(8,128)S(1)}, u32[]{:S(2)}, u32[]{:S(2)}) collective-permute-start(f32[32,128]{1,0:T(8,128)S(1)} %get-tuple-element.25), channel_id=1, source_target_pairs={{0,4},{4,0},{1,5},{5,1},{2,6},{6,2},{3,7},{7,3},{8,12},{12,8},{9,1... | collective-permute-start | bytes 49160 | tf_op jit(solution)/shard_map/ppermute | solution.py:138
  103.5 0.8 collective-permute-done.1
  104.4 0.6 pad_maximum_fusion.18
  105.1 4.4 %collective-permute-start.7 = (f32[352,256]{1,0:T(8,128)S(1)}, f32[352,256]{1,0:T(8,128)S(1)}, u32[]{:S(2)}, u32[]{:S(2)}) collective-permute-start(f32[352,256]{1,0:T(8,128)S(1)} %convert_multiply_fusion), channel_id=1, source_target_pairs={{0,3},{1,0},{2,1},{3,2},{4,7},{5,4},{6,5},{7,6},{8,11},{9,8},{10,9... | collective-permute-start | bytes 1081352 | tf_op jit(solution)/shard_map/ppermute | solution.py:121
  109.5 2.4 collective-permute-start.6
  112.0 2.5 collective-permute-start.5
  114.5 47.3 %all-gather.2.cloned.1.call-done = f32[512,608]{1,0:T(8,128)} async-done(((f32[32,608]{1,0:T(8,128)}), f32[512,608]{1,0:T(8,128)}) %all-gather.2.cloned.1.call-update) | async-done | bytes 1245200 | tf_op jit(solution)/shard_map/all_gather | solution.py:140
  161.8 1.1 slice.81
  163.0 4.4 %collective-permute-start.4 = (f32[512,256]{1,0:T(8,128)S(1)}, f32[512,256]{1,0:T(8,128)}, u32[]{:S(2)}, u32[]{:S(2)}) collective-permute-start(f32[512,256]{1,0:T(8,128)S(1)} %slice.81), channel_id=1, source_target_pairs={{0,3},{1,0},{2,1},{3,2},{4,7},{5,4},{6,5},{7,6},{8,11},{9,8},{10,9... | collective-permute-start | bytes 1572872 | tf_op jit(solution)/shard_map/ppermute | solution.py:121
  167.4 2.1 collective-permute-start.3
  169.5 2.4 collective-permute-start.2
  171.9 1.1 copy.21
  173.0 2.9 fusion.8
  176.0 3.5 %collective-permute-done.4 = f32[512,256]{1,0:T(8,128)} collective-permute-done((f32[512,256]{1,0:T(8,128)S(1)}, f32[512,256]{1,0:T(8,128)}, u32[]{:S(2)}, u32[]{:S(2)}) %collective-permute-start.4) | collective-permute-done | bytes 524320 | tf_op jit(solution)/shard_map/ppermute | solution.py:121
  179.5 6.0 %collective-permute-done.2 = f32[512,256]{1,0:T(8,128)} collective-permute-done((f32[512,256]{1,0:T(8,128)S(1)}, f32[512,256]{1,0:T(8,128)}, u32[]{:S(2)}, u32[]{:S(2)}) %collective-permute-start.2) | collective-permute-done | bytes 524320 | tf_op jit(solution)/shard_map/ppermute | solution.py:121
  185.5 3.0 %fusion.1 = f32[512,352]{0,1:T(8,128)S(1)} fusion(f32[512,256]{1,0:T(8,128)} %collective-permute-done.4, f32[512,256]{1,0:T(8,128)} %collective-permute-done.3, f32[512,256]{1,0:T(8,128)} %collective-permute-done.2, f32[512,256]{1,0:T(8,128)S(1)} %slice.81, f32[352,256]{1,0:T(8,128)} %copy-done.7, f32[352,256]{1,0:T(8,128)} %collective-permute-done.6, ...), kind=kOutput, calls=%fused_computation.4 | convolution fusion | flops 1109950464 | bytes 4259840 | tf_op jit(solution)/shard_map/dot_general | solution.py:99
  188.5 2.7 sqrt_multiply_fusion.1
  191.2 0.8 fusion.30
  192.1 0.5 fusion.27
  192.6 0.5 fusion.31
  193.1 13.0 %collective-permute-start.8 = (f32[352,256]{1,0:T(8,128)S(1)}, f32[352,256]{1,0:T(8,128)S(1)}, u32[]{:S(2)}, u32[]{:S(2)}) collective-permute-start(f32[352,256]{1,0:T(8,128)S(1)} %pad_maximum_fusion.6), channel_id=1, source_target_pairs={{0,4},{4,0},{1,5},{5,1},{2,6},{6,2},{3,7},{7,3},{8,12},{12,8},{9,1... | collective-permute-start | bytes 1081352 | tf_op jit(solution)/shard_map/ppermute | solution.py:157
  206.1 1.3 collective-permute-done.8
  207.4 0.8 maximum_add_fusion
  208.2 4.0 %all-to-all-start.2 = ((f32[4,88,256]{2,1,0:T(8,128)}), f32[4,88,256]{2,1,0:T(8,128)S(1)}, u32[]{:S(2)}, u32[]{:S(2)}) async-start(f32[4,88,256]{2,1,0:T(8,128)} %bitcast.9), calls=%async_computation.2 | async-start | bytes 720896 | tf_op jit(solution)/shard_map/all_to_all | solution.py:158
  212.2 6.9 %all-to-all-done.2 = f32[4,88,256]{2,1,0:T(8,128)S(1)} async-done(((f32[4,88,256]{2,1,0:T(8,128)}), f32[4,88,256]{2,1,0:T(8,128)S(1)}, u32[]{:S(2)}, u32[]{:S(2)}) %all-to-all-start.2) | async-done | bytes 360480 | tf_op jit(solution)/shard_map/all_to_all | solution.py:158
  219.1 9.2 %all_gather.10 = f32[352,128]{1,0:T(8,128)S(1)} all-gather(f32[88,128]{1,0:T(8,128)S(1)} %fusion.16), channel_id=1, replica_groups=mesh['z'=16,'y'=4,'core'=2,'x'=4] {'y'}, dimensions={0}, use_global_device_ids=true | all-gather | bytes 225280 | tf_op jit(solution)/shard_map/all_gather | solution.py:161
  228.3 2.2 collective-permute-start.11
  230.6 2.0 collective-permute-start.10
  232.5 3.0 %collective-permute-start.9 = (f32[352,128]{1,0:T(8,128)S(1)}, f32[352,128]{1,0:T(8,128)S(1)}, u32[]{:S(2)}, u32[]{:S(2)}) collective-permute-start(f32[352,128]{1,0:T(8,128)S(1)} %all_gather.10), channel_id=1, source_target_pairs={{0,1},{1,2},{2,3},{3,0},{4,5},{5,6},{6,7},{7,4},{8,9},{9,10},{10,1... | collective-permute-start | bytes 540680 | tf_op jit(solution)/shard_map/ppermute | solution.py:121
  235.5 2.8 collective-permute-done.10
  238.3 2.5 collective-permute-done.9
  240.8 8.2 %collective-permute-start.12 = (f32[4,352,128]{2,1,0:T(8,128)S(1)}, f32[4,352,128]{2,1,0:T(8,128)S(1)}, u32[]{:S(2)}, u32[]{:S(2)}) collective-permute-start(f32[4,352,128]{2,1,0:T(8,128)S(1)} %pad_maximum_fusion.5), channel_id=1, source_target_pairs={{0,4},{4,0},{1,5},{5,1},{2,6},{6,2},{3,7},{7,3},{8,12},{12,8},{9,1... | collective-permute-start | bytes 2162696 | tf_op jit(solution)/shard_map/ppermute | solution.py:166
  249.1 1.6 collective-permute-done.12
  250.9 1.9 fusion.6
  252.8 2.7 fusion
  255.5 1.6 sqrt_multiply_fusion
  257.2 0.8 fusion.32
  258.0 0.5 fusion.33
  258.5 0.5 fusion.25
  259.1 2.3 collective-permute-start.13
  261.3 1.3 collective-permute-done.13
  262.7 9.4 %all_to_all.20 = f32[4,88,256]{2,1,0:T(8,128)S(1)} all-to-all(f32[4,88,256]{2,1,0:T(8,128)S(1)} %bitcast.39), channel_id=1, replica_groups=mesh['z'=16,'y'=4,'core'=2,'x'=4] {'y'}, dimensions={0} | all-to-all | bytes 720896 | tf_op jit(solution)/shard_map/all_to_all | solution.py:158
  272.1 9.6 %all_gather.11 = f32[352,128]{1,0:T(8,128)S(1)} all-gather(f32[88,128]{1,0:T(8,128)S(1)} %fusion.12), channel_id=1, replica_groups=mesh['z'=16,'y'=4,'core'=2,'x'=4] {'y'}, dimensions={0}, use_global_device_ids=true | all-gather | bytes 225280 | tf_op jit(solution)/shard_map/all_gather | solution.py:161
  281.7 6.1 %collective-permute-start.14 = (f32[352,128]{1,0:T(8,128)S(1)}, f32[352,128]{1,0:T(8,128)S(1)}, u32[]{:S(2)}, u32[]{:S(2)}) collective-permute-start(f32[352,128]{1,0:T(8,128)S(1)} %all_gather.11), channel_id=1, source_target_pairs={{0,4},{4,0},{1,5},{5,1},{2,6},{6,2},{3,7},{7,3},{8,12},{12,8},{9,1... | collective-permute-start | bytes 540680 | tf_op jit(solution)/shard_map/ppermute | solution.py:163
  287.8 0.1 constant_dynamic-slice_fusion.4
  287.9 0.7 copy.20
  288.7 0.2 collective-permute-done.14
  288.8 0.8 maximum_select_fusion.4
  (55 shorter events, 1.0 us)
Async XLA Ops:
  9.8 9.0 %copy-start.10 = (s32[4096]{0:T(1024)S(1)}, s32[4096]{0:T(1024)}, u32[]{:S(2)}) copy-start(s32[4096]{0:T(1024)} %param.11) | copy-start | bytes 49156
  9.8 11.2 %copy-start = (bf16[256,256]{1,0:T(8,128)(2,1)S(1)}, bf16[256,256]{1,0:T(8,128)(2,1)}, u32[]{:S(2)}) copy-start(bf16[256,256]{1,0:T(8,128)(2,1)} %constant.60.clone.fine_ref) | copy-start | bytes 393220
  10.0 11.1 %collective-permute-start = (f32[2048,128]{1,0:T(8,128)S(1)}, f32[2048,128]{1,0:T(8,128)S(1)}, u32[]{:S(2)}, u32[]{:S(2)}) collective-permute-start(f32[2048,128]{1,0:T(8,128)S(1)} %get-tuple-element.10), channel_id=1, source_target_pairs={{0,4},{4,0},{1,5},{5,1},{2,6},{6,2},{3,7},{7,3},{8,12},{12,8},{9,1... | collective-permute-start | bytes 3145736 | tf_op jit(solution)/shard_map/ppermute | solution.py:125
  29.0 29.7 %all-to-all-start = ((f32[4,1024,128]{2,1,0:T(8,128)}), f32[4,1024,128]{2,1,0:T(8,128)S(1)}, u32[]{:S(2)}, u32[]{:S(2)}) async-start(f32[4,1024,128]{2,1,0:T(8,128)} %bitcast.3), calls=%async_computation | async-start | bytes 4194304 | tf_op jit(solution)/shard_map/all_to_all | solution.py:130
  62.2 42.2 %copy-start.9 = (f32[32,352]{1,0:T(8,128)S(1)}, f32[32,352]{1,0:T(8,128)}, u32[]{:S(2)}) copy-start(f32[32,352]{1,0:T(8,128)} %param.13) | copy-start | bytes 135172
  62.2 42.8 %copy-start.5 = (f32[352,256]{1,0:T(8,128)S(1)}, f32[352,256]{1,0:T(8,128)}, u32[]{:S(2)}) copy-start(f32[352,256]{1,0:T(8,128)} %param.14) | copy-start | bytes 1081348
  62.2 42.8 %copy-start.6 = (s32[352,256]{1,0:T(8,128)S(1)}, s32[352,256]{1,0:T(8,128)}, u32[]{:S(2)}) copy-start(s32[352,256]{1,0:T(8,128)} %param.12) | copy-start | bytes 1081348
  62.2 32.5 %all-to-all-start.1 = ((f32[16,64,128]{2,1,0:T(8,128)}), f32[16,64,128]{2,1,0:T(8,128)S(1)}, u32[]{:S(2)}, u32[]{:S(2)}) async-start(f32[16,64,128]{2,1,0:T(8,128)} %bitcast.7), calls=%async_computation.1 | async-start | bytes 1048576 | tf_op jit(solution)/shard_map/all_to_all | solution.py:132
  72.2 89.6 %all-gather.2.cloned.1.call-start = ((), (), s32[]{:S(2)}) async-start(), calls=%async_computation.4 | async-start | bytes 1392640 | tf_op jit(solution)/shard_map/all_gather | solution.py:140
  94.9 9.5 %collective-permute-start.1 = (f32[32,128]{1,0:T(8,128)S(1)}, f32[32,128]{1,0:T(8,128)S(1)}, u32[]{:S(2)}, u32[]{:S(2)}) collective-permute-start(f32[32,128]{1,0:T(8,128)S(1)} %get-tuple-element.25), channel_id=1, source_target_pairs={{0,4},{4,0},{1,5},{5,1},{2,6},{6,2},{3,7},{7,3},{8,12},{12,8},{9,1... | collective-permute-start | bytes 49160 | tf_op jit(solution)/shard_map/ppermute | solution.py:138
  105.1 64.4 %collective-permute-start.7 = (f32[352,256]{1,0:T(8,128)S(1)}, f32[352,256]{1,0:T(8,128)S(1)}, u32[]{:S(2)}, u32[]{:S(2)}) collective-permute-start(f32[352,256]{1,0:T(8,128)S(1)} %convert_multiply_fusion), channel_id=1, source_target_pairs={{0,3},{1,0},{2,1},{3,2},{4,7},{5,4},{6,5},{7,6},{8,11},{9,8},{10,9... | collective-permute-start | bytes 1081352 | tf_op jit(solution)/shard_map/ppermute | solution.py:121
  109.5 63.5 %collective-permute-start.6 = (f32[352,256]{1,0:T(8,128)S(1)}, f32[352,256]{1,0:T(8,128)}, u32[]{:S(2)}, u32[]{:S(2)}) collective-permute-start(f32[352,256]{1,0:T(8,128)S(1)} %convert_multiply_fusion), channel_id=1, source_target_pairs={{0,2},{1,3},{2,0},{3,1},{4,6},{5,7},{6,4},{7,5},{8,10},{9,11},{10,... | collective-permute-start | bytes 1081352 | tf_op jit(solution)/shard_map/ppermute | solution.py:121
  112.0 61.1 %collective-permute-start.5 = (f32[352,256]{1,0:T(8,128)S(1)}, f32[352,256]{1,0:T(8,128)}, u32[]{:S(2)}, u32[]{:S(2)}) collective-permute-start(f32[352,256]{1,0:T(8,128)S(1)} %convert_multiply_fusion), channel_id=1, source_target_pairs={{0,1},{1,2},{2,3},{3,0},{4,5},{5,6},{6,7},{7,4},{8,9},{9,10},{10,1... | collective-permute-start | bytes 1081352 | tf_op jit(solution)/shard_map/ppermute | solution.py:121
  161.8 10.1 %slice-start = ((f32[512,608]{1,0:T(8,128)}), f32[512,352]{1,0:T(8,128)S(1)}, s32[]{:S(2)}) async-start(f32[512,608]{1,0:T(8,128)} %all-gather.2.cloned.1.call-done), calls=%async_computation.5 | async-start | bytes 1572864
  163.0 22.5 %copy-start.3 = (f32[512,256]{1,0:T(8,128)}, f32[512,256]{1,0:T(8,128)S(1)}, u32[]{:S(2)}) copy-start(f32[512,256]{1,0:T(8,128)S(1)} %slice.81) | copy-start | bytes 1572868
  163.0 10.1 %copy-start.1 = (f32[512,608]{1,0:T(8,128)S(1)}, f32[512,608]{1,0:T(8,128)}, u32[]{:S(2)}) copy-start(f32[512,608]{1,0:T(8,128)} %all-gather.2.cloned.1.call-done) | copy-start | bytes 3735556
  163.0 16.5 %collective-permute-start.4 = (f32[512,256]{1,0:T(8,128)S(1)}, f32[512,256]{1,0:T(8,128)}, u32[]{:S(2)}, u32[]{:S(2)}) collective-permute-start(f32[512,256]{1,0:T(8,128)S(1)} %slice.81), channel_id=1, source_target_pairs={{0,3},{1,0},{2,1},{3,2},{4,7},{5,4},{6,5},{7,6},{8,11},{9,8},{10,9... | collective-permute-start | bytes 1572872 | tf_op jit(solution)/shard_map/ppermute | solution.py:121
  167.4 12.0 %collective-permute-start.3 = (f32[512,256]{1,0:T(8,128)S(1)}, f32[512,256]{1,0:T(8,128)}, u32[]{:S(2)}, u32[]{:S(2)}) collective-permute-start(f32[512,256]{1,0:T(8,128)S(1)} %slice.81), channel_id=1, source_target_pairs={{0,2},{1,3},{2,0},{3,1},{4,6},{5,7},{6,4},{7,5},{8,10},{9,11},{10,... | collective-permute-start | bytes 1572872 | tf_op jit(solution)/shard_map/ppermute | solution.py:121
  169.5 3.5 %copy-start.7 = (f32[352,256]{1,0:T(8,128)}, f32[352,256]{1,0:T(8,128)S(1)}, u32[]{:S(2)}) copy-start(f32[352,256]{1,0:T(8,128)S(1)} %collective-permute-done.7) | copy-start | bytes 1081348
  169.5 15.9 %collective-permute-start.2 = (f32[512,256]{1,0:T(8,128)S(1)}, f32[512,256]{1,0:T(8,128)}, u32[]{:S(2)}, u32[]{:S(2)}) collective-permute-start(f32[512,256]{1,0:T(8,128)S(1)} %slice.81), channel_id=1, source_target_pairs={{0,1},{1,2},{2,3},{3,0},{4,5},{5,6},{6,7},{7,4},{8,9},{9,10},{10,1... | collective-permute-start | bytes 1572872 | tf_op jit(solution)/shard_map/ppermute | solution.py:121
  176.0 12.5 %copy-start.2 = (f32[512,352]{0,1:T(8,128)S(1)}, f32[512,352]{0,1:T(8,128)}, u32[]{:S(2)}) copy-start(f32[512,352]{0,1:T(8,128)} %copy.21) | copy-start | bytes 2162692
  176.0 12.5 %copy-start.8 = (f32[352,256]{1,0:T(8,128)S(1)}, f32[352,256]{1,0:T(8,128)}, u32[]{:S(2)}) copy-start(f32[352,256]{1,0:T(8,128)} %copy-done.7) | copy-start | bytes 1081348
  193.1 14.3 %collective-permute-start.8 = (f32[352,256]{1,0:T(8,128)S(1)}, f32[352,256]{1,0:T(8,128)S(1)}, u32[]{:S(2)}, u32[]{:S(2)}) collective-permute-start(f32[352,256]{1,0:T(8,128)S(1)} %pad_maximum_fusion.6), channel_id=1, source_target_pairs={{0,4},{4,0},{1,5},{5,1},{2,6},{6,2},{3,7},{7,3},{8,12},{12,8},{9,1... | collective-permute-start | bytes 1081352 | tf_op jit(solution)/shard_map/ppermute | solution.py:157
  208.2 10.9 %all-to-all-start.2 = ((f32[4,88,256]{2,1,0:T(8,128)}), f32[4,88,256]{2,1,0:T(8,128)S(1)}, u32[]{:S(2)}, u32[]{:S(2)}) async-start(f32[4,88,256]{2,1,0:T(8,128)} %bitcast.9), calls=%async_computation.2 | async-start | bytes 720896 | tf_op jit(solution)/shard_map/all_to_all | solution.py:158
  228.3 7.2 %collective-permute-start.11 = (f32[352,128]{1,0:T(8,128)S(1)}, f32[352,128]{1,0:T(8,128)S(1)}, u32[]{:S(2)}, u32[]{:S(2)}) collective-permute-start(f32[352,128]{1,0:T(8,128)S(1)} %all_gather.10), channel_id=1, source_target_pairs={{0,3},{1,0},{2,1},{3,2},{4,7},{5,4},{6,5},{7,6},{8,11},{9,8},{10,9... | collective-permute-start | bytes 540680 | tf_op jit(solution)/shard_map/ppermute | solution.py:121
  230.6 7.7 %collective-permute-start.10 = (f32[352,128]{1,0:T(8,128)S(1)}, f32[352,128]{1,0:T(8,128)S(1)}, u32[]{:S(2)}, u32[]{:S(2)}) collective-permute-start(f32[352,128]{1,0:T(8,128)S(1)} %all_gather.10), channel_id=1, source_target_pairs={{0,2},{1,3},{2,0},{3,1},{4,6},{5,7},{6,4},{7,5},{8,10},{9,11},{10,... | collective-permute-start | bytes 540680 | tf_op jit(solution)/shard_map/ppermute | solution.py:121
  232.5 8.3 %collective-permute-start.9 = (f32[352,128]{1,0:T(8,128)S(1)}, f32[352,128]{1,0:T(8,128)S(1)}, u32[]{:S(2)}, u32[]{:S(2)}) collective-permute-start(f32[352,128]{1,0:T(8,128)S(1)} %all_gather.10), channel_id=1, source_target_pairs={{0,1},{1,2},{2,3},{3,0},{4,5},{5,6},{6,7},{7,4},{8,9},{9,10},{10,1... | collective-permute-start | bytes 540680 | tf_op jit(solution)/shard_map/ppermute | solution.py:121
  240.8 9.8 %collective-permute-start.12 = (f32[4,352,128]{2,1,0:T(8,128)S(1)}, f32[4,352,128]{2,1,0:T(8,128)S(1)}, u32[]{:S(2)}, u32[]{:S(2)}) collective-permute-start(f32[4,352,128]{2,1,0:T(8,128)S(1)} %pad_maximum_fusion.5), channel_id=1, source_target_pairs={{0,4},{4,0},{1,5},{5,1},{2,6},{6,2},{3,7},{7,3},{8,12},{12,8},{9,1... | collective-permute-start | bytes 2162696 | tf_op jit(solution)/shard_map/ppermute | solution.py:166
  250.9 1.9 copy-start.4
  259.1 3.6 %collective-permute-start.13 = (f32[352,256]{1,0:T(8,128)S(1)}, f32[352,256]{1,0:T(8,128)S(1)}, u32[]{:S(2)}, u32[]{:S(2)}) collective-permute-start(f32[352,256]{1,0:T(8,128)S(1)} %pad_maximum_fusion.7), channel_id=1, source_target_pairs={{0,4},{4,0},{1,5},{5,1},{2,6},{6,2},{3,7},{7,3},{8,12},{12,8},{9,1... | collective-permute-start | bytes 1081352 | tf_op jit(solution)/shard_map/ppermute | solution.py:157
  281.7 7.1 %collective-permute-start.14 = (f32[352,128]{1,0:T(8,128)S(1)}, f32[352,128]{1,0:T(8,128)S(1)}, u32[]{:S(2)}, u32[]{:S(2)}) collective-permute-start(f32[352,128]{1,0:T(8,128)S(1)} %all_gather.11), channel_id=1, source_target_pairs={{0,4},{4,0},{1,5},{5,1},{2,6},{6,2},{3,7},{7,3},{8,12},{12,8},{9,1... | collective-permute-start | bytes 540680 | tf_op jit(solution)/shard_map/ppermute | solution.py:163
Sparse Core Ops, SparseCore 0:
  105.2 56.6 all-gather.1

commit v2 on v1

v2 whole, which is shorter than its diff:
```python
import numpy as np
import jax
import jax.numpy as jnp
from jax import lax
from jax.experimental import pallas as pl
from jax.experimental.pallas import tpu as pltpu
from jax.sharding import Mesh
from jax.sharding import PartitionSpec as P

ITERS = 2
FINE = 256
SHARE = 128
GROUP = 32


def sylvester(count):
    matrix = np.ones((1, 1), np.float32)
    while matrix.shape[0] < count:
        matrix = np.block([[matrix, matrix], [matrix, -matrix]])
    return matrix


def shift(axis, by):
    count = lax.axis_size(axis)
    return [(i, (i + by) % count) for i in range(count)]


def signs_of(position, count):
    return lax.dynamic_slice_in_dim(jnp.asarray(sylvester(count)), position, 1, axis=0)[0]


def spread_kernel(bits_ref, rows_ref, fine_ref, out_ref):
    frames = rows_ref.shape[0]
    coarse = frames // FINE
    for part in range(coarse):
        here = pl.ds(part * FINE, FINE)
        signs = (1 - 2 * bits_ref[:, here]).astype(jnp.float32)
        matrix = (fine_ref[...] * signs).astype(jnp.bfloat16)
        value = rows_ref[here, :]
        high = value.astype(jnp.bfloat16)
        low = (value - high.astype(jnp.float32)).astype(jnp.bfloat16)
        out_ref[here, :] = jnp.dot(
            jnp.concatenate([matrix, matrix], axis=1),
            jnp.concatenate([high, low], axis=0),
            preferred_element_type=jnp.float32,
        )
    step = 16

    def stage(i, carry):
        at = [pl.ds(pl.multiple_of(part * FINE + i * step, step), step) for part in range(coarse)]
        values = [out_ref[a, :] for a in at]
        apart = 1
        while apart < coarse:
            new = list(values)
            for j in range(coarse):
                if not j & apart:
                    new[j] = values[j] + values[j | apart]
                    new[j | apart] = values[j] - values[j | apart]
            values = new
            apart *= 2
        for a, v in zip(at, values):
            out_ref[a, :] = v
        return carry

    lax.fori_loop(0, FINE // step, stage, 0)


def spread(bits, rows):
    vmem = pl.BlockSpec(memory_space=pltpu.VMEM)
    return pl.pallas_call(
        spread_kernel,
        out_shape=jax.ShapeDtypeStruct(rows.shape, jnp.float32),
        in_specs=[vmem, vmem, vmem],
        out_specs=vmem,
        compiler_params=pltpu.CompilerParams(vmem_limit_bytes=24 << 20),
    )(bits.reshape(1, -1), rows, jnp.asarray(sylvester(FINE)))


def pick_kernel(sign_ref, to_ref, rows_ref, own_ref, other_ref, out_ref, work_ref):
    sign = sign_ref[0]
    count = out_ref.shape[0]
    per_chip = count // to_ref.shape[0]
    work_ref[...] = other_ref[...] + sign * own_ref[...]

    def pick(i, carry):
        first = pl.multiple_of(i * GROUP, GROUP)
        found = [work_ref[pl.ds(rows_ref[first + j], 1), :] for j in range(GROUP)]
        out_ref[pl.ds(first, GROUP), :] = jnp.concatenate(found, axis=0) * to_ref[first // per_chip]
        return carry

    lax.fori_loop(0, count // GROUP, pick, 0)


def pick(sign, to, rows, own, other):
    vmem = pl.BlockSpec(memory_space=pltpu.VMEM)
    smem = pl.BlockSpec(memory_space=pltpu.SMEM)
    return pl.pallas_call(
        pick_kernel,
        out_shape=jax.ShapeDtypeStruct((rows.shape[0], own.shape[1]), jnp.float32),
        in_specs=[smem, smem, smem, vmem, vmem],
        out_specs=vmem,
        scratch_shapes=[pltpu.VMEM(own.shape, jnp.float32)],
        compiler_params=pltpu.CompilerParams(vmem_limit_bytes=24 << 20),
    )(sign, to, rows, own, other)


def times(a, b, dims):
    return lax.dot_general(a, b, (dims, ((), ())), precision=lax.Precision.HIGH, preferred_element_type=jnp.float32)


def ratio(signed, total):
    damping = 1.0
    return jnp.sqrt((jnp.maximum(signed, 0.0) + damping) / (jnp.maximum(-signed, 0.0) + total + damping))


def by_core(core, own, other):
    return jnp.where(core == 0, jnp.concatenate([own, other], axis=-1), jnp.concatenate([other, own], axis=-1))


def body(spectrum, sign_bits, kept_rows, mask, w_init, h_init):
    n_z, n_y, n_x = (lax.axis_size(axis) for axis in ("z", "y", "x"))
    at_z, at_y, core, at_x = (lax.axis_index(axis) for axis in ("z", "y", "core", "x"))
    swap = [(0, 1), (1, 0)]
    frames = spectrum.shape[0]
    per_block = kept_rows.shape[0] // (n_z * n_y * 2)
    k = h_init.shape[0]
    mine, theirs = core * SHARE, (1 - core) * SHARE

    def across(value):
        return [value] + [lax.ppermute(value, "x", shift("x", by)) for by in range(1, n_x)]

    own = spread(sign_bits, spectrum)
    other = lax.ppermute(own, "core", swap)
    rows = lax.dynamic_index_in_dim(kept_rows.reshape(n_z, n_y, 2, per_block), core, 2, keepdims=False)
    rows = rows.transpose(1, 0, 2).reshape(-1)
    to = (signs_of(at_y, n_y)[:, None] * signs_of(at_z, n_z)[None, :]).reshape(-1)
    partial_rows = pick((1 - 2 * core).astype(jnp.float32).reshape(1), to, rows, own, other)
    bins = spectrum.shape[1]

    partial_rows, w_init = lax.optimization_barrier((partial_rows, w_init))
    got = lax.all_to_all(partial_rows.reshape(n_y, -1, bins), "y", 0, 0)
    activations = lax.all_gather(w_init, "z", tiled=True)
    got, activations, h_init = lax.optimization_barrier((got, activations, h_init))
    partial_rows = jnp.sum(got, axis=0)
    got = lax.all_to_all(partial_rows.reshape(n_z, -1, bins), "z", 0, 0)
    templates = jnp.concatenate(across(h_init * mask.astype(jnp.float32)), axis=1)
    gram = times(templates, templates, ((1,), (1,)))
    total = times(activations, gram, ((1,), (0,)))
    got, templates, total = lax.optimization_barrier((got, templates, total))
    sketch = jnp.sum(got, axis=0) / jnp.sqrt(jnp.float32(frames * n_z * n_y * 2))
    sketch_own = lax.all_gather(sketch, "z", tiled=True)
    sketch = jnp.concatenate(across(sketch_own), axis=1)
    for round_index in range(ITERS):
        if round_index:
            gram = times(templates, templates, ((1,), (1,)))
            total = times(activations, gram, ((1,), (0,)))
        proj = times(sketch, templates, ((1,), (1,)))
        activations = activations * ratio(proj, total)
        cross = times(activations, sketch_own, ((0,), (0,)))
        model = times(activations, templates[:, :bins], ((1,), (0,)))
        total = times(activations, model, ((0,), (0,)))

        def half(at):
            return jnp.concatenate([lax.dynamic_slice_in_dim(v, at, SHARE, axis=1) for v in (cross, total)], axis=1)

        both = half(mine) + lax.ppermute(half(theirs), "core", swap)
        both = jnp.sum(lax.all_to_all(both.reshape(n_y, k // n_y, 2 * SHARE), "y", 0, 0), axis=0)
        piece = lax.dynamic_slice(templates, (at_y * (k // n_y), mine), (k // n_y, SHARE))
        piece = piece * ratio(both[:, :SHARE], both[:, SHARE:])
        if round_index == ITERS - 1:
            piece = lax.all_gather(piece, "y", tiled=True)
            templates = by_core(core, piece, lax.ppermute(piece, "core", swap))
        else:
            pieces = lax.all_gather(piece, ("y", "x")).reshape(n_y, n_x, k // n_y, SHARE)
            other = lax.ppermute(pieces, "core", swap)
            order = [jnp.remainder(at_x - by, n_x) for by in range(n_x)]
            quarters = [[lax.dynamic_slice_in_dim(v, at, 1, axis=1).reshape(k, SHARE) for v in (pieces, other)] for at in order]
            templates = jnp.concatenate([by_core(core, *quarter) for quarter in quarters], axis=1)
    activations = lax.dynamic_slice_in_dim(activations, at_z * per_block, per_block)
    return (activations, templates)


def solution(mesh):
    torus = Mesh(mesh.devices.reshape(16, 4, 2, 4), ("z", "y", "core", "x"))
    frames = ("z", "y", "core")
    in_specs = (P(frames, "x"), P(frames), P(), P(None, "x"), P(frames, None), P(None, "x"))
    out_specs = (P(frames, None), P(None, "x"))
    return jax.shard_map(body, mesh=torus, in_specs=in_specs, out_specs=out_specs, check_vma=False)
```

time: 298 us -> 240 us (0.81)
  waiting for transfers between devices: 122 us -> 36.4 us
  blocking collectives: 28.2 us -> 83.2 us
  between operations: 14.6 us -> 1.22 us
  starting transfers between devices: 90 us -> 79.4 us
  matrix products: 18.4 us -> 11.5 us
  local copies, waits for them, and re-layouts: 5.82 us -> 11.5 us
    all_gather x0 -> x3, blocking collectives: none -> 74 us  [the longest x1 29.8 us: body(): activations = lax.all_gather(w_init, 'z', tiled=True)]
    all_gather x1 -> x0, waiting for transfers between devices: 47.3 us -> none  [body(): lax.all_gather(jnp.concatenate([sketch, w_init], axis=1), 'z', tiled=True)]
    all_to_all x2, waiting for transfers between devices: 46.5 us -> 0.01 us  [the longest x1 0.01 us: body(): got = lax.all_to_all(partial_rows.reshape(n_y, -1, bins), 'y', 0, 0)]
    all_gather x2 -> x1, blocking collectives: 18.8 us -> 9.24 us  [body(): piece = lax.all_gather(piece, 'y', tiled=True)]
    all_to_all x1 -> x0, blocking collectives: 9.4 us -> none  [body(): lax.all_to_all(both.reshape(n_y, k // n_y, 2 * SHARE), 'y', 0, 0)]
    ppermute x3 -> x2, starting transfers between devices: 23.6 us -> 14.8 us  [the longest x1 8.79 us: body(): other = lax.ppermute(own, 'core', swap)]
    ppermute x9 -> x6, starting transfers between devices: 25.4 us -> 18.4 us  [across(): lax.ppermute(value, 'x', shift('x', by))]
    dot_general x12, matrix products: 18.4 us -> 11.5 us  [times(): lax.dot_general(a, b, (dims, ((), ())), precision=lax.Precision.HIGH, pre...]
  transfers between devices with their start and end apart: 19 -> 15, of which waited for: 14 -> 12; matrix products, arithmetic and copies ran while one was open for 3% -> 5% of each run, Pallas kernels for 0% -> 0%
where the time goes in v2:
time: 240 us; the launch traced here: 238 us
  blocking collectives  83.2 us (35%)
  starting transfers between devices  79.4 us (33%)
  waiting for transfers between devices  36.4 us (15%)
  local copies, waits for them, and re-layouts  11.5 us (5%)
  matrix products  11.5 us (5%)
  other arithmetic  7.53 us (3%)
  Pallas kernels  7.44 us (3%)
    all_gather x1, blocking collectives, body(): activations = lax.all_gather(w_init, 'z', tiled=True)  29.8 us
    all_gather x1, blocking collectives, body(): sketch_own = lax.all_gather(sketch, 'z', tiled=True)  25.2 us
    ppermute x2, starting transfers between devices, body(): both = half(mine) + lax.ppermute(half(theirs), 'core', swap)  20.2 us
    all_gather x1, blocking collectives, body(): lax.all_gather(piece, ('y', 'x')).reshape(n_y, n_x, k // n_y, SHARE)  18.9 us
    ppermute x6, starting transfers between devices, across(): lax.ppermute(value, 'x', shift('x', by))  18.4 us
    ppermute x6, waiting for transfers between devices, across(): lax.ppermute(value, 'x', shift('x', by))  16.7 us
    all_to_all x2, waiting for transfers between devices, body(): lax.all_to_all(both.reshape(n_y, k // n_y, 2 * SHARE), 'y', 0, 0)  13.4 us
    dot_general x12, matrix products, times(): lax.dot_general(a, b, (dims, ((), ())), precision=lax.Precision.HIGH, pre...  11.5 us
  transfers between devices with their start and end apart: 15, of which 12 were waited for; matrix products, arithmetic and copies ran while one was open for 5% of the time, Pallas kernels for 0%

profile of v2, /device:TPU:1, one launch (start us, length us, event | category | flops | bytes accessed | tf_op | source)
XLA Modules:
  0.0 238.3 jit_solution(558638464107229455)
XLA Ops:
  0.6 1.6 copy-done.1
  2.2 0.9 copy-done.2
  3.2 0.7 copy-done.3
  3.9 1.1 shard_map.104.own_ref
  5.0 8.8 %collective-permute-start = (f32[2048,256]{1,0:T(8,128)S(1)}, f32[2048,256]{1,0:T(8,128)}, u32[]{:S(2)}, u32[]{:S(2)}) collective-permute-start(f32[2048,256]{1,0:T(8,128)S(1)} %shard_map.104.own_ref), channel_id=1, source_target_pairs={{0,4},{4,0},{1,5},{5,1},{2,6},{6,2},{3,7},{7,3},{8,12},{12,8},{9,1... | collective-permute-start | bytes 6291464 | tf_op jit(solution)/shard_map/ppermute | solution.py:133
  13.8 0.7 fusion.11
  14.5 0.7 fusion.10
  15.6 2.1 collective-permute-done.other_ref
  17.7 6.3 %shard_map.105 = f32[2048,256]{1,0:T(8,128)S(1)} custom-call(f32[1]{0:T(128)} %bitcast.sign_ref, f32[64]{0:T(128)S(1)} %mul.58.to_ref, s32[2048]{0:T(1024)S(1)} %reshape.62.rows_ref, f32[2048,256]{1,0:T(8,128)S(1)} %shard_map.104.own_ref, f32[2048,256]{1,0:T(8,128)} %collective-permute-done.other_ref), custom_call_target="tpu_custom_call" | custom-call | tf_op jit(solution)/shard_map/pallas_call | solution.py:97
  24.0 1.3 copy-done
  25.4 3.7 %all-to-all-start = ((f32[4,512,256]{2,1,0:T(8,128)}), f32[4,512,256]{2,1,0:T(8,128)S(1)}, u32[]{:S(2)}, u32[]{:S(2)}) async-start(f32[4,512,256]{2,1,0:T(8,128)} %bitcast.42), calls=%async_computation | async-start | bytes 4194304 | tf_op jit(solution)/shard_map/all_to_all | solution.py:141
  29.1 29.8 %all_gather.15 = f32[512,352]{1,0:T(8,128)S(1)} all-gather(f32[32,352]{1,0:T(8,128)S(1)} %copy-done.8), channel_id=1, replica_groups=mesh['z'=16,'y'=4,'core'=2,'x'=4] {'z'}, dimensions={0}, use_global_device_ids=true | all-gather | bytes 765952 | tf_op jit(solution)/shard_map/all_gather | solution.py:142
  58.9 1.0 reduce_sum.36
  59.9 7.0 %all-to-all-start.1 = ((f32[16,32,256]{2,1,0:T(8,128)}), f32[16,32,256]{2,1,0:T(8,128)S(1)}, u32[]{:S(2)}, u32[]{:S(2)}) async-start(f32[16,32,256]{2,1,0:T(8,128)} %bitcast.7), calls=%async_computation.1 | async-start | bytes 1048576 | tf_op jit(solution)/shard_map/all_to_all | solution.py:145
  66.9 1.1 convert_multiply_fusion
  68.1 4.4 %collective-permute-start.3 = (f32[352,256]{1,0:T(8,128)S(1)}, f32[352,256]{1,0:T(8,128)S(1)}, u32[]{:S(2)}, u32[]{:S(2)}) collective-permute-start(f32[352,256]{1,0:T(8,128)S(1)} %convert_multiply_fusion), channel_id=1, source_target_pairs={{0,3},{1,0},{2,1},{3,2},{4,7},{5,4},{6,5},{7,6},{8,11},{9,8},{10,9... | collective-permute-start | bytes 1081352 | tf_op jit(solution)/shard_map/ppermute | solution.py:130
  72.4 2.4 %collective-permute-start.2 = (f32[352,256]{1,0:T(8,128)S(1)}, f32[352,256]{1,0:T(8,128)S(1)}, u32[]{:S(2)}, u32[]{:S(2)}) collective-permute-start(f32[352,256]{1,0:T(8,128)S(1)} %convert_multiply_fusion), channel_id=1, source_target_pairs={{0,2},{1,3},{2,0},{3,1},{4,6},{5,7},{6,4},{7,5},{8,10},{9,11},{10,... | collective-permute-start | bytes 1081352 | tf_op jit(solution)/shard_map/ppermute | solution.py:130
  74.9 2.5 %collective-permute-start.1 = (f32[352,256]{1,0:T(8,128)S(1)}, f32[352,256]{1,0:T(8,128)S(1)}, u32[]{:S(2)}, u32[]{:S(2)}) collective-permute-start(f32[352,256]{1,0:T(8,128)S(1)} %convert_multiply_fusion), channel_id=1, source_target_pairs={{0,1},{1,2},{2,3},{3,0},{4,5},{5,6},{6,7},{7,4},{8,9},{9,10},{10,1... | collective-permute-start | bytes 1081352 | tf_op jit(solution)/shard_map/ppermute | solution.py:130
  77.4 3.0 %collective-permute-done.3 = f32[352,256]{1,0:T(8,128)S(1)} collective-permute-done((f32[352,256]{1,0:T(8,128)S(1)}, f32[352,256]{1,0:T(8,128)S(1)}, u32[]{:S(2)}, u32[]{:S(2)}) %collective-permute-start.3) | collective-permute-done | bytes 360480 | tf_op jit(solution)/shard_map/ppermute | solution.py:130
  80.4 2.1 collective-permute-done.2
  82.4 4.9 %collective-permute-done.1 = f32[352,256]{1,0:T(8,128)S(1)} collective-permute-done((f32[352,256]{1,0:T(8,128)S(1)}, f32[352,256]{1,0:T(8,128)S(1)}, u32[]{:S(2)}, u32[]{:S(2)}) %collective-permute-start.1) | collective-permute-done | bytes 360480 | tf_op jit(solution)/shard_map/ppermute | solution.py:130
  87.3 1.3 fusion.12
  88.9 1.7 fusion.15
  90.6 25.2 %all_gather.16 = f32[512,256]{1,0:T(8,128)S(1)} all-gather(f32[32,256]{1,0:T(8,128)S(1)} %broadcast_multiply_fusion), channel_id=1, replica_groups=mesh['z'=16,'y'=4,'core'=2,'x'=4] {'z'}, dimensions={0}, use_global_device_ids=true | all-gather | bytes 557056 | tf_op jit(solution)/shard_map/all_gather | solution.py:151
  115.9 1.9 collective-permute-start.4
  117.8 4.2 %collective-permute-start.5 = (f32[512,256]{1,0:T(8,128)S(1)}, f32[512,256]{1,0:T(8,128)}, u32[]{:S(2)}, u32[]{:S(2)}) collective-permute-start(f32[512,256]{1,0:T(8,128)S(1)} %all_gather.16), channel_id=1, source_target_pairs={{0,2},{1,3},{2,0},{3,1},{4,6},{5,7},{6,4},{7,5},{8,10},{9,11},{10,... | collective-permute-start | bytes 1572872 | tf_op jit(solution)/shard_map/ppermute | solution.py:130
  122.0 3.0 %collective-permute-start.6 = (f32[512,256]{1,0:T(8,128)S(1)}, f32[512,256]{1,0:T(8,128)S(1)}, u32[]{:S(2)}, u32[]{:S(2)}) collective-permute-start(f32[512,256]{1,0:T(8,128)S(1)} %all_gather.16), channel_id=1, source_target_pairs={{0,3},{1,0},{2,1},{3,2},{4,7},{5,4},{6,5},{7,6},{8,11},{9,8},{10,9... | collective-permute-start | bytes 1572872 | tf_op jit(solution)/shard_map/ppermute | solution.py:130
  124.9 1.1 copy.21
  126.1 6.6 %collective-permute-done.4 = f32[512,256]{1,0:T(8,128)} collective-permute-done((f32[512,256]{1,0:T(8,128)S(1)}, f32[512,256]{1,0:T(8,128)}, u32[]{:S(2)}, u32[]{:S(2)}) %collective-permute-start.4) | collective-permute-done | bytes 524320 | tf_op jit(solution)/shard_map/ppermute | solution.py:130
  132.7 1.1 constant_dynamic-update-slice_fusion.2
  133.8 1.1 constant_dynamic-update-slice_fusion.1
  134.9 0.2 collective-permute-done.6
  135.2 1.3 fusion.16
  136.6 0.2 copy-done.6
  136.8 0.5 copy-done.7
  137.3 0.4 sqrt_multiply_fusion.1
  137.7 0.8 fusion
  138.5 0.5 fusion.17
  139.0 0.5 fusion.18
  139.6 17.9 %collective-permute-start.7 = (f32[352,256]{1,0:T(8,128)S(1)}, f32[352,256]{1,0:T(8,128)S(1)}, u32[]{:S(2)}, u32[]{:S(2)}) collective-permute-start(f32[352,256]{1,0:T(8,128)S(1)} %pad_maximum_fusion.2), channel_id=1, source_target_pairs={{0,4},{4,0},{1,5},{5,1},{2,6},{6,2},{3,7},{7,3},{8,12},{12,8},{9,1... | collective-permute-start | bytes 1081352 | tf_op jit(solution)/shard_map/ppermute | solution.py:166
  157.5 1.3 collective-permute-done.7
  158.8 0.8 maximum_add_fusion
  159.6 3.5 %all-to-all-start.2 = ((f32[4,88,256]{2,1,0:T(8,128)}), f32[4,88,256]{2,1,0:T(8,128)S(1)}, u32[]{:S(2)}, u32[]{:S(2)}) async-start(f32[4,88,256]{2,1,0:T(8,128)} %bitcast.8), calls=%async_computation.2 | async-start | bytes 720896 | tf_op jit(solution)/shard_map/all_to_all | solution.py:167
  163.0 7.3 %all-to-all-done.2 = f32[4,88,256]{2,1,0:T(8,128)S(1)} async-done(((f32[4,88,256]{2,1,0:T(8,128)}), f32[4,88,256]{2,1,0:T(8,128)S(1)}, u32[]{:S(2)}, u32[]{:S(2)}) %all-to-all-start.2) | async-done | bytes 360480 | tf_op jit(solution)/shard_map/all_to_all | solution.py:167
  170.4 18.9 %all-gather = f32[1408,128]{1,0:T(8,128)S(1)} all-gather(f32[88,128]{1,0:T(8,128)S(1)} %fusion.9), channel_id=2, replica_groups=mesh['z'=16,'y'=4,'core'=2,'x'=4] {'y','x'}, dimensions={0}, use_global_device_ids=true | all-gather | bytes 765952 | tf_op jit(solution)/shard_map/all_gather | solution.py:174
  189.3 8.4 %collective-permute-start.8 = (f32[4,4,88,128]{3,2,1,0:T(8,128)S(1)}, f32[4,4,88,128]{3,2,1,0:T(8,128)S(1)}, u32[]{:S(2)}, u32[]{:S(2)}) collective-permute-start(f32[4,4,88,128]{3,2,1,0:T(8,128)S(1)} %bitcast.44), channel_id=1, source_target_pairs={{0,4},{4,0},{1,5},{5,1},{2,6},{6,2},{3,7},{7,3},{8,12},{12,8},{9,1... | collective-permute-start | bytes 2162696 | tf_op jit(solution)/shard_map/ppermute | solution.py:175
  197.9 1.4 collective-permute-done.8
  199.6 1.3 fusion.13
  200.9 0.8 fusion.19
  201.7 1.6 sqrt_multiply_fusion
  203.3 0.8 fusion.21
  204.1 0.5 fusion.20
  204.6 0.5 fusion.22
  205.2 2.3 collective-permute-start.9
  207.5 1.3 collective-permute-done.9
  208.8 0.8 maximum_add_fusion.1
  209.5 3.5 %all-to-all-start.3 = ((f32[4,88,256]{2,1,0:T(8,128)}), f32[4,88,256]{2,1,0:T(8,128)S(1)}, u32[]{:S(2)}, u32[]{:S(2)}) async-start(f32[4,88,256]{2,1,0:T(8,128)} %bitcast.18), calls=%async_computation.3 | async-start | bytes 720896 | tf_op jit(solution)/shard_map/all_to_all | solution.py:167
  213.0 1.3 pad_maximum_fusion.1
  214.3 6.1 %all-to-all-done.3 = f32[4,88,256]{2,1,0:T(8,128)S(1)} async-done(((f32[4,88,256]{2,1,0:T(8,128)}), f32[4,88,256]{2,1,0:T(8,128)S(1)}, u32[]{:S(2)}, u32[]{:S(2)}) %all-to-all-start.3) | async-done | bytes 360480 | tf_op jit(solution)/shard_map/all_to_all | solution.py:167
  220.5 0.8 fusion.5
  221.3 9.2 %all_gather.19 = f32[352,128]{1,0:T(8,128)S(1)} all-gather(f32[88,128]{1,0:T(8,128)S(1)} %fusion.5), channel_id=1, replica_groups=mesh['z'=16,'y'=4,'core'=2,'x'=4] {'y'}, dimensions={0}, use_global_device_ids=true | all-gather | bytes 225280 | tf_op jit(solution)/shard_map/all_gather | solution.py:171
  230.5 6.0 %collective-permute-start.10 = (f32[352,128]{1,0:T(8,128)S(1)}, f32[352,128]{1,0:T(8,128)S(1)}, u32[]{:S(2)}, u32[]{:S(2)}) collective-permute-start(f32[352,128]{1,0:T(8,128)S(1)} %all_gather.19), channel_id=1, source_target_pairs={{0,4},{4,0},{1,5},{5,1},{2,6},{6,2},{3,7},{7,3},{8,12},{12,8},{9,1... | collective-permute-start | bytes 540680 | tf_op jit(solution)/shard_map/ppermute | solution.py:172
  236.6 0.7 copy.22
  237.5 0.8 maximum_select_fusion.4
  (44 shorter events, 1.6 us)
Async XLA Ops:
  0.6 1.6 copy-start.1
  2.2 0.9 copy-start.2
  3.2 0.7 copy-start.3
  3.9 11.5 %copy-start.9 = (s32[4096]{0:T(1024)S(1)}, s32[4096]{0:T(1024)}, u32[]{:S(2)}) copy-start(s32[4096]{0:T(1024)} %param.11) | copy-start | bytes 49156
  5.0 12.7 %collective-permute-start = (f32[2048,256]{1,0:T(8,128)S(1)}, f32[2048,256]{1,0:T(8,128)}, u32[]{:S(2)}, u32[]{:S(2)}) collective-permute-start(f32[2048,256]{1,0:T(8,128)S(1)} %shard_map.104.own_ref), channel_id=1, source_target_pairs={{0,4},{4,0},{1,5},{5,1},{2,6},{6,2},{3,7},{7,3},{8,12},{12,8},{9,1... | collective-permute-start | bytes 6291464 | tf_op jit(solution)/shard_map/ppermute | solution.py:133
  24.0 1.3 copy-start
  25.4 3.8 %copy-start.8 = (f32[32,352]{1,0:T(8,128)S(1)}, f32[32,352]{1,0:T(8,128)}, u32[]{:S(2)}) copy-start(f32[32,352]{1,0:T(8,128)} %param.13) | copy-start | bytes 135172
  25.4 33.6 %all-to-all-start = ((f32[4,512,256]{2,1,0:T(8,128)}), f32[4,512,256]{2,1,0:T(8,128)S(1)}, u32[]{:S(2)}, u32[]{:S(2)}) async-start(f32[4,512,256]{2,1,0:T(8,128)} %bitcast.42), calls=%async_computation | async-start | bytes 4194304 | tf_op jit(solution)/shard_map/all_to_all | solution.py:141
  59.9 30.6 %all-to-all-start.1 = ((f32[16,32,256]{2,1,0:T(8,128)}), f32[16,32,256]{2,1,0:T(8,128)S(1)}, u32[]{:S(2)}, u32[]{:S(2)}) async-start(f32[16,32,256]{2,1,0:T(8,128)} %bitcast.7), calls=%async_computation.1 | async-start | bytes 1048576 | tf_op jit(solution)/shard_map/all_to_all | solution.py:145
  68.1 12.3 %collective-permute-start.3 = (f32[352,256]{1,0:T(8,128)S(1)}, f32[352,256]{1,0:T(8,128)S(1)}, u32[]{:S(2)}, u32[]{:S(2)}) collective-permute-start(f32[352,256]{1,0:T(8,128)S(1)} %convert_multiply_fusion), channel_id=1, source_target_pairs={{0,3},{1,0},{2,1},{3,2},{4,7},{5,4},{6,5},{7,6},{8,11},{9,8},{10,9... | collective-permute-start | bytes 1081352 | tf_op jit(solution)/shard_map/ppermute | solution.py:130
  72.4 10.0 %collective-permute-start.2 = (f32[352,256]{1,0:T(8,128)S(1)}, f32[352,256]{1,0:T(8,128)S(1)}, u32[]{:S(2)}, u32[]{:S(2)}) collective-permute-start(f32[352,256]{1,0:T(8,128)S(1)} %convert_multiply_fusion), channel_id=1, source_target_pairs={{0,2},{1,3},{2,0},{3,1},{4,6},{5,7},{6,4},{7,5},{8,10},{9,11},{10,... | collective-permute-start | bytes 1081352 | tf_op jit(solution)/shard_map/ppermute | solution.py:130
  74.9 12.5 %collective-permute-start.1 = (f32[352,256]{1,0:T(8,128)S(1)}, f32[352,256]{1,0:T(8,128)S(1)}, u32[]{:S(2)}, u32[]{:S(2)}) collective-permute-start(f32[352,256]{1,0:T(8,128)S(1)} %convert_multiply_fusion), channel_id=1, source_target_pairs={{0,1},{1,2},{2,3},{3,0},{4,5},{5,6},{6,7},{7,4},{8,9},{9,10},{10,1... | collective-permute-start | bytes 1081352 | tf_op jit(solution)/shard_map/ppermute | solution.py:130
  115.9 16.8 %collective-permute-start.4 = (f32[512,256]{1,0:T(8,128)S(1)}, f32[512,256]{1,0:T(8,128)}, u32[]{:S(2)}, u32[]{:S(2)}) collective-permute-start(f32[512,256]{1,0:T(8,128)S(1)} %all_gather.16), channel_id=1, source_target_pairs={{0,1},{1,2},{2,3},{3,0},{4,5},{5,6},{6,7},{7,4},{8,9},{9,10},{10,1... | collective-permute-start | bytes 1572872 | tf_op jit(solution)/shard_map/ppermute | solution.py:130
  117.8 16.0 %collective-permute-start.5 = (f32[512,256]{1,0:T(8,128)S(1)}, f32[512,256]{1,0:T(8,128)}, u32[]{:S(2)}, u32[]{:S(2)}) collective-permute-start(f32[512,256]{1,0:T(8,128)S(1)} %all_gather.16), channel_id=1, source_target_pairs={{0,2},{1,3},{2,0},{3,1},{4,6},{5,7},{6,4},{7,5},{8,10},{9,11},{10,... | collective-permute-start | bytes 1572872 | tf_op jit(solution)/shard_map/ppermute | solution.py:130
  122.0 13.2 %collective-permute-start.6 = (f32[512,256]{1,0:T(8,128)S(1)}, f32[512,256]{1,0:T(8,128)S(1)}, u32[]{:S(2)}, u32[]{:S(2)}) collective-permute-start(f32[512,256]{1,0:T(8,128)S(1)} %all_gather.16), channel_id=1, source_target_pairs={{0,3},{1,0},{2,1},{3,2},{4,7},{5,4},{6,5},{7,6},{8,11},{9,8},{10,9... | collective-permute-start | bytes 1572872 | tf_op jit(solution)/shard_map/ppermute | solution.py:130
  135.2 1.4 copy-start.4
  135.2 1.6 copy-start.6
  135.2 2.1 copy-start.7
  139.6 19.2 %collective-permute-start.7 = (f32[352,256]{1,0:T(8,128)S(1)}, f32[352,256]{1,0:T(8,128)S(1)}, u32[]{:S(2)}, u32[]{:S(2)}) collective-permute-start(f32[352,256]{1,0:T(8,128)S(1)} %pad_maximum_fusion.2), channel_id=1, source_target_pairs={{0,4},{4,0},{1,5},{5,1},{2,6},{6,2},{3,7},{7,3},{8,12},{12,8},{9,1... | collective-permute-start | bytes 1081352 | tf_op jit(solution)/shard_map/ppermute | solution.py:166
  159.6 10.8 %all-to-all-start.2 = ((f32[4,88,256]{2,1,0:T(8,128)}), f32[4,88,256]{2,1,0:T(8,128)S(1)}, u32[]{:S(2)}, u32[]{:S(2)}) async-start(f32[4,88,256]{2,1,0:T(8,128)} %bitcast.8), calls=%async_computation.2 | async-start | bytes 720896 | tf_op jit(solution)/shard_map/all_to_all | solution.py:167
  189.3 10.0 %collective-permute-start.8 = (f32[4,4,88,128]{3,2,1,0:T(8,128)S(1)}, f32[4,4,88,128]{3,2,1,0:T(8,128)S(1)}, u32[]{:S(2)}, u32[]{:S(2)}) collective-permute-start(f32[4,4,88,128]{3,2,1,0:T(8,128)S(1)} %bitcast.44), channel_id=1, source_target_pairs={{0,4},{4,0},{1,5},{5,1},{2,6},{6,2},{3,7},{7,3},{8,12},{12,8},{9,1... | collective-permute-start | bytes 2162696 | tf_op jit(solution)/shard_map/ppermute | solution.py:175
  199.6 2.1 copy-start.5
  205.2 3.6 %collective-permute-start.9 = (f32[352,256]{1,0:T(8,128)S(1)}, f32[352,256]{1,0:T(8,128)S(1)}, u32[]{:S(2)}, u32[]{:S(2)}) collective-permute-start(f32[352,256]{1,0:T(8,128)S(1)} %pad_maximum_fusion.3), channel_id=1, source_target_pairs={{0,4},{4,0},{1,5},{5,1},{2,6},{6,2},{3,7},{7,3},{8,12},{12,8},{9,1... | collective-permute-start | bytes 1081352 | tf_op jit(solution)/shard_map/ppermute | solution.py:166
  209.5 10.9 %all-to-all-start.3 = ((f32[4,88,256]{2,1,0:T(8,128)}), f32[4,88,256]{2,1,0:T(8,128)S(1)}, u32[]{:S(2)}, u32[]{:S(2)}) async-start(f32[4,88,256]{2,1,0:T(8,128)} %bitcast.18), calls=%async_computation.3 | async-start | bytes 720896 | tf_op jit(solution)/shard_map/all_to_all | solution.py:167
  230.5 7.0 %collective-permute-start.10 = (f32[352,128]{1,0:T(8,128)S(1)}, f32[352,128]{1,0:T(8,128)S(1)}, u32[]{:S(2)}, u32[]{:S(2)}) collective-permute-start(f32[352,128]{1,0:T(8,128)S(1)} %all_gather.19), channel_id=1, source_target_pairs={{0,4},{4,0},{1,5},{5,1},{2,6},{6,2},{3,7},{7,3},{8,12},{12,8},{9,1... | collective-permute-start | bytes 540680 | tf_op jit(solution)/shard_map/ppermute | solution.py:172

commit v3 on v2

--- a/solution.py
+++ b/solution.py
@@ -10,7 +10,7 @@
 ITERS = 2
 FINE = 256
 SHARE = 128
-GROUP = 32
+GROUP = 64
 
 
 def sylvester(count):
@@ -29,14 +29,24 @@
     return lax.dynamic_slice_in_dim(jnp.asarray(sylvester(count)), position, 1, axis=0)[0]
 
 
-def spread_kernel(bits_ref, rows_ref, fine_ref, out_ref):
+def spread_kernel(bits_ref, rows_ref, fine_ref, out_ref, bits_vmem, rows_vmem, fine_vmem, sems):
     frames = rows_ref.shape[0]
     coarse = frames // FINE
-    for part in range(coarse):
-        here = pl.ds(part * FINE, FINE)
-        signs = (1 - 2 * bits_ref[:, here]).astype(jnp.float32)
-        matrix = (fine_ref[...] * signs).astype(jnp.bfloat16)
-        value = rows_ref[here, :]
+    chunk = [pl.ds(part * FINE, FINE) for part in range(coarse)]
+    small = [
+        pltpu.make_async_copy(bits_ref, bits_vmem, sems.at[coarse]),
+        pltpu.make_async_copy(fine_ref, fine_vmem, sems.at[coarse + 1]),
+    ]
+    large = [pltpu.make_async_copy(rows_ref.at[c, :], rows_vmem.at[c, :], sems.at[part]) for part, c in enumerate(chunk)]
+    for copy in small + large:
+        copy.start()
+    for copy in small:
+        copy.wait()
+    for part, here in enumerate(chunk):
+        signs = (1 - 2 * bits_vmem[:, here]).astype(jnp.float32)
+        matrix = fine_vmem[...] * signs.astype(jnp.bfloat16)
+        large[part].wait()
+        value = rows_vmem[here, :]
         high = value.astype(jnp.bfloat16)
         low = (value - high.astype(jnp.float32)).astype(jnp.bfloat16)
         out_ref[here, :] = jnp.dot(
@@ -66,40 +76,62 @@
 
 
 def spread(bits, rows):
-    vmem = pl.BlockSpec(memory_space=pltpu.VMEM)
+    hbm = pl.BlockSpec(memory_space=pltpu.HBM)
+    frames = rows.shape[0]
     return pl.pallas_call(
         spread_kernel,
         out_shape=jax.ShapeDtypeStruct(rows.shape, jnp.float32),
-        in_specs=[vmem, vmem, vmem],
-        out_specs=vmem,
+        in_specs=[hbm, hbm, hbm],
+        out_specs=pl.BlockSpec(memory_space=pltpu.VMEM),
+        scratch_shapes=[
+            pltpu.VMEM((1, frames), jnp.int32),
+            pltpu.VMEM(rows.shape, jnp.float32),
+            pltpu.VMEM((FINE, FINE), jnp.bfloat16),
+            pltpu.SemaphoreType.DMA((frames // FINE + 2,)),
+        ],
         compiler_params=pltpu.CompilerParams(vmem_limit_bytes=24 << 20),
-    )(bits.reshape(1, -1), rows, jnp.asarray(sylvester(FINE)))
-
-
-def pick_kernel(sign_ref, to_ref, rows_ref, own_ref, other_ref, out_ref, work_ref):
+    )(bits.reshape(1, -1), pltpu.with_memory_space_constraint(rows, pltpu.HBM), jnp.asarray(sylvester(FINE), jnp.bfloat16))
+
+
+def pick_kernel(sign_ref, to_ref, rows_ref, own_ref, other_ref, out_ref, work_ref, kept_ref, sems):
     sign = sign_ref[0]
-    count = out_ref.shape[0]
+    count = kept_ref.shape[0]
     per_chip = count // to_ref.shape[0]
+    parts = sems.shape[0]
     work_ref[...] = other_ref[...] + sign * own_ref[...]
 
     def pick(i, carry):
         first = pl.multiple_of(i * GROUP, GROUP)
         found = [work_ref[pl.ds(rows_ref[first + j], 1), :] for j in range(GROUP)]
-        out_ref[pl.ds(first, GROUP), :] = jnp.concatenate(found, axis=0) * to_ref[first // per_chip]
+        found = [jnp.concatenate(found[j : j + per_chip], axis=0) * to_ref[(first + j) // per_chip] for j in range(0, GROUP, per_chip)]
+        kept_ref[pl.ds(first, GROUP), :] = jnp.concatenate(found, axis=0)
         return carry
 
-    lax.fori_loop(0, count // GROUP, pick, 0)
+    steps = count // parts // GROUP
+    copies = []
+    for part in range(parts):
+        lax.fori_loop(part * steps, (part + 1) * steps, pick, 0)
+        here = pl.ds(part * steps * GROUP, steps * GROUP)
+        copies.append(pltpu.make_async_copy(kept_ref.at[here, :], out_ref.at[here, :], sems.at[part]))
+        copies[-1].start()
+    for copy in copies:
+        copy.wait()
 
 
 def pick(sign, to, rows, own, other):
     vmem = pl.BlockSpec(memory_space=pltpu.VMEM)
     smem = pl.BlockSpec(memory_space=pltpu.SMEM)
+    shape = (rows.shape[0], own.shape[1])
     return pl.pallas_call(
         pick_kernel,
-        out_shape=jax.ShapeDtypeStruct((rows.shape[0], own.shape[1]), jnp.float32),
+        out_shape=pltpu.HBM(shape, jnp.float32),
         in_specs=[smem, smem, smem, vmem, vmem],
-        out_specs=vmem,
-        scratch_shapes=[pltpu.VMEM(own.shape, jnp.float32)],
+        out_specs=pl.BlockSpec(memory_space=pltpu.HBM),
+        scratch_shapes=[
+            pltpu.VMEM(own.shape, jnp.float32),
+            pltpu.VMEM(shape, jnp.float32),
+            pltpu.SemaphoreType.DMA((4,)),
+        ],
         compiler_params=pltpu.CompilerParams(vmem_limit_bytes=24 << 20),
     )(sign, to, rows, own, other)
 
@@ -111,6 +143,10 @@
 def ratio(signed, total):
     damping = 1.0
     return jnp.sqrt((jnp.maximum(signed, 0.0) + damping) / (jnp.maximum(-signed, 0.0) + total + damping))
+
+
+def everywhere(value, axes, count):
+    return lax.all_to_all(jnp.broadcast_to(value[None], (count, *value.shape)), axes, 0, 0)
 
 
 def by_core(core, own, other):
@@ -144,16 +180,14 @@
     partial_rows = jnp.sum(got, axis=0)
     got = lax.all_to_all(partial_rows.reshape(n_z, -1, bins), "z", 0, 0)
     templates = jnp.concatenate(across(h_init * mask.astype(jnp.float32)), axis=1)
-    gram = times(templates, templates, ((1,), (1,)))
-    total = times(activations, gram, ((1,), (0,)))
-    got, templates, total = lax.optimization_barrier((got, templates, total))
+    order = [jnp.remainder(at_x - by, n_x) for by in range(n_x)]
+    got, templates = lax.optimization_barrier((got, templates))
     sketch = jnp.sum(got, axis=0) / jnp.sqrt(jnp.float32(frames * n_z * n_y * 2))
     sketch_own = lax.all_gather(sketch, "z", tiled=True)
     sketch = jnp.concatenate(across(sketch_own), axis=1)
     for round_index in range(ITERS):
-        if round_index:
-            gram = times(templates, templates, ((1,), (1,)))
-            total = times(activations, gram, ((1,), (0,)))
+        gram = times(templates, templates, ((1,), (1,)))
+        total = times(activations, gram, ((1,), (0,)))
         proj = times(sketch, templates, ((1,), (1,)))
         activations = activations * ratio(proj, total)
         cross = times(activations, sketch_own, ((0,), (0,)))
@@ -168,12 +202,11 @@
         piece = lax.dynamic_slice(templates, (at_y * (k // n_y), mine), (k // n_y, SHARE))
         piece = piece * ratio(both[:, :SHARE], both[:, SHARE:])
         if round_index == ITERS - 1:
-            piece = lax.all_gather(piece, "y", tiled=True)
-            templates = by_core(core, piece, lax.ppermute(piece, "core", swap))
+            pieces = everywhere(piece, ("y", "core"), n_y * 2).reshape(n_y, 2, k // n_y, SHARE)
+            templates = pieces.transpose(0, 2, 1, 3).reshape(k, 2 * SHARE)
         else:
-            pieces = lax.all_gather(piece, ("y", "x")).reshape(n_y, n_x, k // n_y, SHARE)
+            pieces = everywhere(piece, ("y", "x"), n_y * n_x).reshape(n_y, n_x, k // n_y, SHARE)
             other = lax.ppermute(pieces, "core", swap)
-            order = [jnp.remainder(at_x - by, n_x) for by in range(n_x)]
             quarters = [[lax.dynamic_slice_in_dim(v, at, 1, axis=1).reshape(k, SHARE) for v in (pieces, other)] for at in order]
             templates = jnp.concatenate([by_core(core, *quarter) for quarter in quarters], axis=1)
     activations = lax.dynamic_slice_in_dim(activations, at_z * per_block, per_block)

time: 240 us -> 228 us (0.950)
  blocking collectives: 83.2 us -> 74.8 us
  local copies, waits for them, and re-layouts: 11.5 us -> 7.55 us
  Pallas kernels: 7.44 us -> 10.8 us
  starting transfers between devices: 79.4 us -> 76.5 us
    all_gather x2 -> x0, blocking collectives: 28.2 us -> none  [the longest x1 18.9 us: body(): lax.all_gather(piece, ('y', 'x')).reshape(n_y, n_x, k // n_y, SHARE)]
    all_to_all x0 -> x1, blocking collectives: none -> 16.4 us  [everywhere(): lax.all_to_all(jnp.broadcast_to(value[None], (count, *value.shape)), axes...]
    all_to_all x0 -> x1, waiting for transfers between devices: none -> 6.9 us  [everywhere(): lax.all_to_all(jnp.broadcast_to(value[None], (count, *value.shape)), axes...]
    ppermute x1 -> x0, starting transfers between devices: 5.96 us -> none  [body(): templates = by_core(core, piece, lax.ppermute(piece, 'core', swap))]
    unnamed x24 -> x21, local copies, waits for them, and re-layouts: 8.25 us -> 3.27 us
    ppermute x6, waiting for transfers between devices: 16.7 us -> 11.8 us  [across(): lax.ppermute(value, 'x', shift('x', by))]
    all_to_all x0 -> x1, starting transfers between devices: none -> 4.55 us  [everywhere(): lax.all_to_all(jnp.broadcast_to(value[None], (count, *value.shape)), axes...]
    ppermute x1, starting transfers between devices: 8.39 us -> 5.06 us  [body(): other = lax.ppermute(pieces, 'core', swap)]
  transfers between devices with their start and end apart: 15 -> 15, of which waited for: 12 -> 11; matrix products, arithmetic and copies ran while one was open for 5% -> 4% of each run, Pallas kernels for 0% -> 0%
where the time goes in v3:
time: 228 us; the launch traced here: 227 us
  starting transfers between devices  76.5 us (34%)
  blocking collectives  74.8 us (33%)
  waiting for transfers between devices  37.8 us (17%)
  matrix products  10.9 us (5%)
  Pallas kernels  10.8 us (5%)
  local copies, waits for them, and re-layouts  7.55 us (3%)
  other arithmetic  7.33 us (3%)
    all_gather x1, blocking collectives, body(): activations = lax.all_gather(w_init, 'z', tiled=True)  29.8 us
    all_gather x1, blocking collectives, body(): sketch_own = lax.all_gather(sketch, 'z', tiled=True)  28.6 us
    ppermute x6, starting transfers between devices, across(): lax.ppermute(value, 'x', shift('x', by))  21.1 us
    ppermute x2, starting transfers between devices, body(): both = half(mine) + lax.ppermute(half(theirs), 'core', swap)  18.9 us
    all_to_all x1, blocking collectives, everywhere(): lax.all_to_all(jnp.broadcast_to(value[None], (count, *value.shape)), axes...  16.4 us
    all_to_all x2, waiting for transfers between devices, body(): lax.all_to_all(both.reshape(n_y, k // n_y, 2 * SHARE), 'y', 0, 0)  13 us
    ppermute x6, waiting for transfers between devices, across(): lax.ppermute(value, 'x', shift('x', by))  11.8 us
    dot_general x12, matrix products, times(): lax.dot_general(a, b, (dims, ((), ())), precision=lax.Precision.HIGH, pre...  10.9 us
  transfers between devices with their start and end apart: 15, of which 11 were waited for; matrix products, arithmetic and copies ran while one was open for 4% of the time, Pallas kernels for 0%

profile of v3, /device:TPU:1, one launch (start us, length us, event | category | flops | bytes accessed | tf_op | source)
XLA Modules:
  0.0 226.9 jit_solution(17931082346854711142)
XLA Ops:
  0.6 0.9 copy-done
  1.5 0.7 copy-done.1
  2.2 3.9 %shard_map.104.own_ref = f32[2048,256]{1,0:T(8,128)S(1)} custom-call(s32[1,2048]{1,0:T(1,128)S(1)} %bitcast.52, f32[2048,256]{1,0:T(8,128)} %rows_ref.1, bf16[256,256]{1,0:T(8,128)(2,1)S(1)} %copy-done), custom_call_target="tpu_custom_call" | custom-call | tf_op jit(solution)/shard_map/pallas_call | solution.py:81
  6.2 8.8 %collective-permute-start = (f32[2048,256]{1,0:T(8,128)S(1)}, f32[2048,256]{1,0:T(8,128)}, u32[]{:S(2)}, u32[]{:S(2)}) collective-permute-start(f32[2048,256]{1,0:T(8,128)S(1)} %shard_map.104.own_ref), channel_id=1, source_target_pairs={{0,4},{4,0},{1,5},{5,1},{2,6},{6,2},{3,7},{7,3},{8,12},{12,8},{9,1... | collective-permute-start | bytes 6291464 | tf_op jit(solution)/shard_map/ppermute | solution.py:169
  15.0 0.7 fusion.10
  15.7 0.7 fusion.11
  16.4 0.1 mul.58.to_ref
  16.5 0.1 reshape.69
  16.8 2.1 collective-permute-done.other_ref
  18.8 6.9 %shard_map.105 = f32[2048,256]{1,0:T(8,128)} custom-call(f32[1]{0:T(128)} %bitcast.sign_ref, f32[64]{0:T(128)S(1)} %mul.58.to_ref, s32[2048]{0:T(1024)S(1)} %reshape.70.rows_ref, f32[2048,256]{1,0:T(8,128)S(1)} %shard_map.104.own_ref, f32[2048,256]{1,0:T(8,128)} %collective-permute-done.other_ref), custom_call_target="tpu_custom_call" | custom-call | tf_op jit(solution)/shard_map/pallas_call | solution.py:125
  25.8 3.8 %all-to-all-start = ((f32[4,512,256]{2,1,0:T(8,128)}), f32[4,512,256]{2,1,0:T(8,128)S(1)}, u32[]{:S(2)}, u32[]{:S(2)}) async-start(f32[4,512,256]{2,1,0:T(8,128)} %bitcast.53), calls=%async_computation | async-start | bytes 4194304 | tf_op jit(solution)/shard_map/all_to_all | solution.py:177
  29.6 29.8 %all_gather.6 = f32[512,352]{1,0:T(8,128)S(1)} all-gather(f32[32,352]{1,0:T(8,128)S(1)} %copy-done.6), channel_id=1, replica_groups=mesh['z'=16,'y'=4,'core'=2,'x'=4] {'z'}, dimensions={0}, use_global_device_ids=true | all-gather | bytes 765952 | tf_op jit(solution)/shard_map/all_gather | solution.py:178
  59.4 1.0 reduce_sum.36
  60.4 7.0 %all-to-all-start.1 = ((f32[16,32,256]{2,1,0:T(8,128)}), f32[16,32,256]{2,1,0:T(8,128)S(1)}, u32[]{:S(2)}, u32[]{:S(2)}) async-start(f32[16,32,256]{2,1,0:T(8,128)} %bitcast.7), calls=%async_computation.1 | async-start | bytes 1048576 | tf_op jit(solution)/shard_map/all_to_all | solution.py:181
  67.4 1.0 convert_multiply_fusion
  68.4 3.1 %collective-permute-start.1 = (f32[352,256]{1,0:T(8,128)S(1)}, f32[352,256]{1,0:T(8,128)S(1)}, u32[]{:S(2)}, u32[]{:S(2)}) collective-permute-start(f32[352,256]{1,0:T(8,128)S(1)} %convert_multiply_fusion), channel_id=1, source_target_pairs={{0,1},{1,2},{2,3},{3,0},{4,5},{5,6},{6,7},{7,4},{8,9},{9,10},{10,1... | collective-permute-start | bytes 1081352 | tf_op jit(solution)/shard_map/ppermute | solution.py:166
  71.5 4.4 %collective-permute-start.2 = (f32[352,256]{1,0:T(8,128)S(1)}, f32[352,256]{1,0:T(8,128)}, u32[]{:S(2)}, u32[]{:S(2)}) collective-permute-start(f32[352,256]{1,0:T(8,128)S(1)} %convert_multiply_fusion), channel_id=1, source_target_pairs={{0,2},{1,3},{2,0},{3,1},{4,6},{5,7},{6,4},{7,5},{8,10},{9,11},{10,... | collective-permute-start | bytes 1081352 | tf_op jit(solution)/shard_map/ppermute | solution.py:166
  75.9 3.1 %collective-permute-start.3 = (f32[352,256]{1,0:T(8,128)S(1)}, f32[352,256]{1,0:T(8,128)}, u32[]{:S(2)}, u32[]{:S(2)}) collective-permute-start(f32[352,256]{1,0:T(8,128)S(1)} %convert_multiply_fusion), channel_id=1, source_target_pairs={{0,3},{1,0},{2,1},{3,2},{4,7},{5,4},{6,5},{7,6},{8,11},{9,8},{10,9... | collective-permute-start | bytes 1081352 | tf_op jit(solution)/shard_map/ppermute | solution.py:166
  79.0 1.1 copy.23
  80.1 4.2 %collective-permute-done.2 = f32[352,256]{1,0:T(8,128)} collective-permute-done((f32[352,256]{1,0:T(8,128)S(1)}, f32[352,256]{1,0:T(8,128)}, u32[]{:S(2)}, u32[]{:S(2)}) %collective-permute-start.2) | collective-permute-done | bytes 360480 | tf_op jit(solution)/shard_map/ppermute | solution.py:166
  84.3 1.2 collective-permute-done.3
  85.5 1.3 pad_maximum_fusion
  86.8 28.6 %all_gather.7 = f32[512,256]{1,0:T(8,128)S(1)} all-gather(f32[32,256]{1,0:T(8,128)S(1)} %broadcast_multiply_fusion), channel_id=1, replica_groups=mesh['z'=16,'y'=4,'core'=2,'x'=4] {'z'}, dimensions={0}, use_global_device_ids=true | all-gather | bytes 557056 | tf_op jit(solution)/shard_map/all_gather | solution.py:186
  115.4 2.7 %collective-permute-start.4 = (f32[512,256]{1,0:T(8,128)S(1)}, f32[512,256]{1,0:T(8,128)S(1)}, u32[]{:S(2)}, u32[]{:S(2)}) collective-permute-start(f32[512,256]{1,0:T(8,128)S(1)} %all_gather.7), channel_id=1, source_target_pairs={{0,1},{1,2},{2,3},{3,0},{4,5},{5,6},{6,7},{7,4},{8,9},{9,10},{10,1... | collective-permute-start | bytes 1572872 | tf_op jit(solution)/shard_map/ppermute | solution.py:166
  118.2 4.8 %collective-permute-start.5 = (f32[512,256]{1,0:T(8,128)S(1)}, f32[512,256]{1,0:T(8,128)S(1)}, u32[]{:S(2)}, u32[]{:S(2)}) collective-permute-start(f32[512,256]{1,0:T(8,128)S(1)} %all_gather.7), channel_id=1, source_target_pairs={{0,2},{1,3},{2,0},{3,1},{4,6},{5,7},{6,4},{7,5},{8,10},{9,11},{10,... | collective-permute-start | bytes 1572872 | tf_op jit(solution)/shard_map/ppermute | solution.py:166
  123.0 3.0 %collective-permute-start.6 = (f32[512,256]{1,0:T(8,128)S(1)}, f32[512,256]{1,0:T(8,128)S(1)}, u32[]{:S(2)}, u32[]{:S(2)}) collective-permute-start(f32[512,256]{1,0:T(8,128)S(1)} %all_gather.7), channel_id=1, source_target_pairs={{0,3},{1,0},{2,1},{3,2},{4,7},{5,4},{6,5},{7,6},{8,11},{9,8},{10,9... | collective-permute-start | bytes 1572872 | tf_op jit(solution)/shard_map/ppermute | solution.py:166
  126.0 1.3 fusion.14
  127.3 0.8 fusion.15
  128.2 5.1 %collective-permute-done.5 = f32[512,256]{1,0:T(8,128)S(1)} collective-permute-done((f32[512,256]{1,0:T(8,128)S(1)}, f32[512,256]{1,0:T(8,128)S(1)}, u32[]{:S(2)}, u32[]{:S(2)}) %collective-permute-start.5) | collective-permute-done | bytes 524320 | tf_op jit(solution)/shard_map/ppermute | solution.py:166
  133.3 1.4 collective-permute-done.6
  134.8 1.7 sqrt_multiply_fusion.1
  136.4 0.5 fusion.16
  136.9 0.8 fusion
  137.7 0.5 fusion.17
  138.3 16.6 %collective-permute-start.7 = (f32[352,256]{1,0:T(8,128)S(1)}, f32[352,256]{1,0:T(8,128)S(1)}, u32[]{:S(2)}, u32[]{:S(2)}) collective-permute-start(f32[352,256]{1,0:T(8,128)S(1)} %pad_maximum_fusion.2), channel_id=1, source_target_pairs={{0,4},{4,0},{1,5},{5,1},{2,6},{6,2},{3,7},{7,3},{8,12},{12,8},{9,1... | collective-permute-start | bytes 1081352 | tf_op jit(solution)/shard_map/ppermute | solution.py:200
  155.0 1.3 collective-permute-done.7
  156.3 0.8 maximum_add_fusion
  157.0 3.9 %all-to-all-start.2 = ((f32[4,88,256]{2,1,0:T(8,128)}), f32[4,88,256]{2,1,0:T(8,128)S(1)}, u32[]{:S(2)}, u32[]{:S(2)}) async-start(f32[4,88,256]{2,1,0:T(8,128)} %bitcast.8), calls=%async_computation.2 | async-start | bytes 720896 | tf_op jit(solution)/shard_map/all_to_all | solution.py:201
  160.9 6.9 %all-to-all-done.2 = f32[4,88,256]{2,1,0:T(8,128)S(1)} async-done(((f32[4,88,256]{2,1,0:T(8,128)}), f32[4,88,256]{2,1,0:T(8,128)S(1)}, u32[]{:S(2)}, u32[]{:S(2)}) %all-to-all-start.2) | async-done | bytes 360480 | tf_op jit(solution)/shard_map/all_to_all | solution.py:201
  167.9 16.4 %all_to_all.30 = f32[16,88,128]{2,1,0:T(8,128)S(1)} all-to-all(f32[16,88,128]{2,1,0:T(8,128)S(1)} %broadcast_in_dim.4), channel_id=1, replica_groups=mesh['z'=16,'y'=4,'core'=2,'x'=4] {'y','x'}, dimensions={0} | all-to-all | bytes 1441792 | tf_op jit(solution)/shard_map/all_to_all | solution.py:149
  184.3 5.1 %collective-permute-start.8 = (f32[4,4,88,128]{3,2,1,0:T(8,128)S(1)}, f32[4,4,88,128]{3,2,1,0:T(8,128)S(1)}, u32[]{:S(2)}, u32[]{:S(2)}) collective-permute-start(f32[4,4,88,128]{3,2,1,0:T(8,128)S(1)} %bitcast.54), channel_id=1, source_target_pairs={{0,4},{4,0},{1,5},{5,1},{2,6},{6,2},{3,7},{7,3},{8,12},{12,8},{9,1... | collective-permute-start | bytes 2162696 | tf_op jit(solution)/shard_map/ppermute | solution.py:209
  189.4 0.1 constant_dynamic-slice_fusion.12
  189.5 1.4 collective-permute-done.8
  190.9 0.1 constant_dynamic-slice_fusion.11
  191.2 1.3 fusion.12
  192.5 0.8 fusion.18
  193.3 1.6 sqrt_multiply_fusion
  194.9 0.5 fusion.19
  195.4 0.8 fusion.20
  196.2 0.5 fusion.21
  196.8 2.3 %collective-permute-start.9 = (f32[352,256]{1,0:T(8,128)S(1)}, f32[352,256]{1,0:T(8,128)S(1)}, u32[]{:S(2)}, u32[]{:S(2)}) collective-permute-start(f32[352,256]{1,0:T(8,128)S(1)} %pad_maximum_fusion.3), channel_id=1, source_target_pairs={{0,4},{4,0},{1,5},{5,1},{2,6},{6,2},{3,7},{7,3},{8,12},{12,8},{9,1... | collective-permute-start | bytes 1081352 | tf_op jit(solution)/shard_map/ppermute | solution.py:200
  199.1 1.3 collective-permute-done.9
  200.4 0.8 maximum_add_fusion.1
  201.1 3.5 %all-to-all-start.4 = ((f32[4,88,256]{2,1,0:T(8,128)}), f32[4,88,256]{2,1,0:T(8,128)S(1)}, u32[]{:S(2)}, u32[]{:S(2)}) async-start(f32[4,88,256]{2,1,0:T(8,128)} %bitcast.18), calls=%async_computation.4 | async-start | bytes 720896 | tf_op jit(solution)/shard_map/all_to_all | solution.py:201
  204.6 1.3 pad_maximum_fusion.1
  205.9 6.1 %all-to-all-done.4 = f32[4,88,256]{2,1,0:T(8,128)S(1)} async-done(((f32[4,88,256]{2,1,0:T(8,128)}), f32[4,88,256]{2,1,0:T(8,128)S(1)}, u32[]{:S(2)}, u32[]{:S(2)}) %all-to-all-start.4) | async-done | bytes 360480 | tf_op jit(solution)/shard_map/all_to_all | solution.py:201
  212.1 0.8 fusion.5
  212.9 0.8 broadcast_in_dim.5
  213.7 4.5 %all-to-all-start.5 = ((f32[8,88,128]{2,1,0:T(8,128)}), f32[8,88,128]{2,1,0:T(8,128)S(1)}, u32[]{:S(2)}, u32[]{:S(2)}) async-start(f32[8,88,128]{2,1,0:T(8,128)} %broadcast_in_dim.5), calls=%async_computation.5 | async-start | bytes 720896 | tf_op jit(solution)/shard_map/all_to_all | solution.py:149
  218.2 0.1 constant_dynamic-slice_fusion.4
  218.3 0.7 copy.25
  219.1 6.9 %all-to-all-done.5 = f32[8,88,128]{2,1,0:T(8,128)S(1)} async-done(((f32[8,88,128]{2,1,0:T(8,128)}), f32[8,88,128]{2,1,0:T(8,128)S(1)}, u32[]{:S(2)}, u32[]{:S(2)}) %all-to-all-start.5) | async-done | bytes 360480 | tf_op jit(solution)/shard_map/all_to_all | solution.py:149
  226.0 0.2 copy.24
  226.1 0.8 copy.29
  (41 shorter events, 0.9 us)
Async XLA Ops:
  0.6 0.9 copy-start
  1.5 0.7 copy-start.1
  2.2 14.3 %copy-start.7 = (s32[4096]{0:T(1024)S(1)}, s32[4096]{0:T(1024)}, u32[]{:S(2)}) copy-start(s32[4096]{0:T(1024)} %param.11) | copy-start | bytes 49156
  6.2 12.7 %collective-permute-start = (f32[2048,256]{1,0:T(8,128)S(1)}, f32[2048,256]{1,0:T(8,128)}, u32[]{:S(2)}, u32[]{:S(2)}) collective-permute-start(f32[2048,256]{1,0:T(8,128)S(1)} %shard_map.104.own_ref), channel_id=1, source_target_pairs={{0,4},{4,0},{1,5},{5,1},{2,6},{6,2},{3,7},{7,3},{8,12},{12,8},{9,1... | collective-permute-start | bytes 6291464 | tf_op jit(solution)/shard_map/ppermute | solution.py:169
  25.8 3.8 %copy-start.6 = (f32[32,352]{1,0:T(8,128)S(1)}, f32[32,352]{1,0:T(8,128)}, u32[]{:S(2)}) copy-start(f32[32,352]{1,0:T(8,128)} %param.13) | copy-start | bytes 135172
  25.8 33.6 %all-to-all-start = ((f32[4,512,256]{2,1,0:T(8,128)}), f32[4,512,256]{2,1,0:T(8,128)S(1)}, u32[]{:S(2)}, u32[]{:S(2)}) async-start(f32[4,512,256]{2,1,0:T(8,128)} %bitcast.53), calls=%async_computation | async-start | bytes 4194304 | tf_op jit(solution)/shard_map/all_to_all | solution.py:177
  59.4 8.0 %copy-start.5 = (f32[352,256]{1,0:T(8,128)S(1)}, f32[352,256]{1,0:T(8,128)}, u32[]{:S(2)}) copy-start(f32[352,256]{1,0:T(8,128)} %param.14) | copy-start | bytes 1081348
  60.4 26.4 %all-to-all-start.1 = ((f32[16,32,256]{2,1,0:T(8,128)}), f32[16,32,256]{2,1,0:T(8,128)S(1)}, u32[]{:S(2)}, u32[]{:S(2)}) async-start(f32[16,32,256]{2,1,0:T(8,128)} %bitcast.7), calls=%async_computation.1 | async-start | bytes 1048576 | tf_op jit(solution)/shard_map/all_to_all | solution.py:181
  68.4 11.7 %collective-permute-start.1 = (f32[352,256]{1,0:T(8,128)S(1)}, f32[352,256]{1,0:T(8,128)S(1)}, u32[]{:S(2)}, u32[]{:S(2)}) collective-permute-start(f32[352,256]{1,0:T(8,128)S(1)} %convert_multiply_fusion), channel_id=1, source_target_pairs={{0,1},{1,2},{2,3},{3,0},{4,5},{5,6},{6,7},{7,4},{8,9},{9,10},{10,1... | collective-permute-start | bytes 1081352 | tf_op jit(solution)/shard_map/ppermute | solution.py:166
  71.5 12.7 %collective-permute-start.2 = (f32[352,256]{1,0:T(8,128)S(1)}, f32[352,256]{1,0:T(8,128)}, u32[]{:S(2)}, u32[]{:S(2)}) collective-permute-start(f32[352,256]{1,0:T(8,128)S(1)} %convert_multiply_fusion), channel_id=1, source_target_pairs={{0,2},{1,3},{2,0},{3,1},{4,6},{5,7},{6,4},{7,5},{8,10},{9,11},{10,... | collective-permute-start | bytes 1081352 | tf_op jit(solution)/shard_map/ppermute | solution.py:166
  75.9 9.6 %collective-permute-start.3 = (f32[352,256]{1,0:T(8,128)S(1)}, f32[352,256]{1,0:T(8,128)}, u32[]{:S(2)}, u32[]{:S(2)}) collective-permute-start(f32[352,256]{1,0:T(8,128)S(1)} %convert_multiply_fusion), channel_id=1, source_target_pairs={{0,3},{1,0},{2,1},{3,2},{4,7},{5,4},{6,5},{7,6},{8,11},{9,8},{10,9... | collective-permute-start | bytes 1081352 | tf_op jit(solution)/shard_map/ppermute | solution.py:166
  115.4 12.7 %collective-permute-start.4 = (f32[512,256]{1,0:T(8,128)S(1)}, f32[512,256]{1,0:T(8,128)S(1)}, u32[]{:S(2)}, u32[]{:S(2)}) collective-permute-start(f32[512,256]{1,0:T(8,128)S(1)} %all_gather.7), channel_id=1, source_target_pairs={{0,1},{1,2},{2,3},{3,0},{4,5},{5,6},{6,7},{7,4},{8,9},{9,10},{10,1... | collective-permute-start | bytes 1572872 | tf_op jit(solution)/shard_map/ppermute | solution.py:166
  118.2 15.1 %collective-permute-start.5 = (f32[512,256]{1,0:T(8,128)S(1)}, f32[512,256]{1,0:T(8,128)S(1)}, u32[]{:S(2)}, u32[]{:S(2)}) collective-permute-start(f32[512,256]{1,0:T(8,128)S(1)} %all_gather.7), channel_id=1, source_target_pairs={{0,2},{1,3},{2,0},{3,1},{4,6},{5,7},{6,4},{7,5},{8,10},{9,11},{10,... | collective-permute-start | bytes 1572872 | tf_op jit(solution)/shard_map/ppermute | solution.py:166
  123.0 11.7 %collective-permute-start.6 = (f32[512,256]{1,0:T(8,128)S(1)}, f32[512,256]{1,0:T(8,128)S(1)}, u32[]{:S(2)}, u32[]{:S(2)}) collective-permute-start(f32[512,256]{1,0:T(8,128)S(1)} %all_gather.7), channel_id=1, source_target_pairs={{0,3},{1,0},{2,1},{3,2},{4,7},{5,4},{6,5},{7,6},{8,11},{9,8},{10,9... | collective-permute-start | bytes 1572872 | tf_op jit(solution)/shard_map/ppermute | solution.py:166
  128.1 6.7 %copy-start.4 = (f32[512,352]{0,1:T(8,128)S(1)}, f32[512,352]{0,1:T(8,128)}, u32[]{:S(2)}) copy-start(f32[512,352]{0,1:T(8,128)} %copy.23) | copy-start | bytes 2162692
  134.7 1.7 copy-start.2
  138.3 17.9 %collective-permute-start.7 = (f32[352,256]{1,0:T(8,128)S(1)}, f32[352,256]{1,0:T(8,128)S(1)}, u32[]{:S(2)}, u32[]{:S(2)}) collective-permute-start(f32[352,256]{1,0:T(8,128)S(1)} %pad_maximum_fusion.2), channel_id=1, source_target_pairs={{0,4},{4,0},{1,5},{5,1},{2,6},{6,2},{3,7},{7,3},{8,12},{12,8},{9,1... | collective-permute-start | bytes 1081352 | tf_op jit(solution)/shard_map/ppermute | solution.py:200
  157.0 10.7 %all-to-all-start.2 = ((f32[4,88,256]{2,1,0:T(8,128)}), f32[4,88,256]{2,1,0:T(8,128)S(1)}, u32[]{:S(2)}, u32[]{:S(2)}) async-start(f32[4,88,256]{2,1,0:T(8,128)} %bitcast.8), calls=%async_computation.2 | async-start | bytes 720896 | tf_op jit(solution)/shard_map/all_to_all | solution.py:201
  184.3 6.7 %collective-permute-start.8 = (f32[4,4,88,128]{3,2,1,0:T(8,128)S(1)}, f32[4,4,88,128]{3,2,1,0:T(8,128)S(1)}, u32[]{:S(2)}, u32[]{:S(2)}) collective-permute-start(f32[4,4,88,128]{3,2,1,0:T(8,128)S(1)} %bitcast.54), channel_id=1, source_target_pairs={{0,4},{4,0},{1,5},{5,1},{2,6},{6,2},{3,7},{7,3},{8,12},{12,8},{9,1... | collective-permute-start | bytes 2162696 | tf_op jit(solution)/shard_map/ppermute | solution.py:209
  191.2 2.1 copy-start.3
  196.8 3.6 %collective-permute-start.9 = (f32[352,256]{1,0:T(8,128)S(1)}, f32[352,256]{1,0:T(8,128)S(1)}, u32[]{:S(2)}, u32[]{:S(2)}) collective-permute-start(f32[352,256]{1,0:T(8,128)S(1)} %pad_maximum_fusion.3), channel_id=1, source_target_pairs={{0,4},{4,0},{1,5},{5,1},{2,6},{6,2},{3,7},{7,3},{8,12},{12,8},{9,1... | collective-permute-start | bytes 1081352 | tf_op jit(solution)/shard_map/ppermute | solution.py:200
  201.1 10.9 %all-to-all-start.4 = ((f32[4,88,256]{2,1,0:T(8,128)}), f32[4,88,256]{2,1,0:T(8,128)S(1)}, u32[]{:S(2)}, u32[]{:S(2)}) async-start(f32[4,88,256]{2,1,0:T(8,128)} %bitcast.18), calls=%async_computation.4 | async-start | bytes 720896 | tf_op jit(solution)/shard_map/all_to_all | solution.py:201
  213.7 12.3 %all-to-all-start.5 = ((f32[8,88,128]{2,1,0:T(8,128)}), f32[8,88,128]{2,1,0:T(8,128)S(1)}, u32[]{:S(2)}, u32[]{:S(2)}) async-start(f32[8,88,128]{2,1,0:T(8,128)} %broadcast_in_dim.5), calls=%async_computation.5 | async-start | bytes 720896 | tf_op jit(solution)/shard_map/all_to_all | solution.py:149

commit v4 on v3

--- a/solution.py
+++ b/solution.py
@@ -90,28 +90,32 @@
             pltpu.SemaphoreType.DMA((frames // FINE + 2,)),
         ],
         compiler_params=pltpu.CompilerParams(vmem_limit_bytes=24 << 20),
-    )(bits.reshape(1, -1), pltpu.with_memory_space_constraint(rows, pltpu.HBM), jnp.asarray(sylvester(FINE), jnp.bfloat16))
+    )(*(pltpu.with_memory_space_constraint(v, pltpu.HBM) for v in (bits.reshape(1, -1), rows, jnp.asarray(sylvester(FINE), jnp.bfloat16))))
 
 
 def pick_kernel(sign_ref, to_ref, rows_ref, own_ref, other_ref, out_ref, work_ref, kept_ref, sems):
     sign = sign_ref[0]
-    count = kept_ref.shape[0]
+    frames, bins = own_ref.shape
+    fold = bins // SHARE
+    count = rows_ref.shape[0]
     per_chip = count // to_ref.shape[0]
     parts = sems.shape[0]
-    work_ref[...] = other_ref[...] + sign * own_ref[...]
+    for half in range(fold):
+        lanes = slice(half * SHARE, (half + 1) * SHARE)
+        work_ref[pl.ds(half, frames, stride=fold), :] = other_ref[:, lanes] + sign * own_ref[:, lanes]
 
     def pick(i, carry):
         first = pl.multiple_of(i * GROUP, GROUP)
-        found = [work_ref[pl.ds(rows_ref[first + j], 1), :] for j in range(GROUP)]
+        found = [work_ref[pl.ds(pl.multiple_of(rows_ref[first + j] * fold, fold), fold), :] for j in range(GROUP)]
         found = [jnp.concatenate(found[j : j + per_chip], axis=0) * to_ref[(first + j) // per_chip] for j in range(0, GROUP, per_chip)]
-        kept_ref[pl.ds(first, GROUP), :] = jnp.concatenate(found, axis=0)
+        kept_ref[pl.ds(first * fold, GROUP * fold), :] = jnp.concatenate(found, axis=0)
         return carry
 
     steps = count // parts // GROUP
     copies = []
     for part in range(parts):
         lax.fori_loop(part * steps, (part + 1) * steps, pick, 0)
-        here = pl.ds(part * steps * GROUP, steps * GROUP)
+        here = pl.ds(part * steps * GROUP * fold, steps * GROUP * fold)
         copies.append(pltpu.make_async_copy(kept_ref.at[here, :], out_ref.at[here, :], sems.at[part]))
         copies[-1].start()
     for copy in copies:
@@ -121,14 +125,15 @@
 def pick(sign, to, rows, own, other):
     vmem = pl.BlockSpec(memory_space=pltpu.VMEM)
     smem = pl.BlockSpec(memory_space=pltpu.SMEM)
-    shape = (rows.shape[0], own.shape[1])
+    frames, bins = own.shape
+    shape = (rows.shape[0] * bins // SHARE, SHARE)
     return pl.pallas_call(
         pick_kernel,
         out_shape=pltpu.HBM(shape, jnp.float32),
         in_specs=[smem, smem, smem, vmem, vmem],
         out_specs=pl.BlockSpec(memory_space=pltpu.HBM),
         scratch_shapes=[
-            pltpu.VMEM(own.shape, jnp.float32),
+            pltpu.VMEM((frames * bins // SHARE + 8, SHARE), jnp.float32),
             pltpu.VMEM(shape, jnp.float32),
             pltpu.SemaphoreType.DMA((4,)),
         ],
@@ -154,16 +159,17 @@
 
 
 def body(spectrum, sign_bits, kept_rows, mask, w_init, h_init):
-    n_z, n_y, n_x = (lax.axis_size(axis) for axis in ("z", "y", "x"))
-    at_z, at_y, core, at_x = (lax.axis_index(axis) for axis in ("z", "y", "core", "x"))
+    ring = ("far", "near")
+    n_z, n_near, n_y, n_x = (lax.axis_size(axis) for axis in (ring, "near", "y", "x"))
+    at_z, at_far, at_y, core, at_x = (lax.axis_index(axis) for axis in (ring, "far", "y", "core", "x"))
     swap = [(0, 1), (1, 0)]
     frames = spectrum.shape[0]
     per_block = kept_rows.shape[0] // (n_z * n_y * 2)
     k = h_init.shape[0]
     mine, theirs = core * SHARE, (1 - core) * SHARE
 
-    def across(value):
-        return [value] + [lax.ppermute(value, "x", shift("x", by)) for by in range(1, n_x)]
+    def along_x(value, by):
+        return lax.ppermute(value, "x", shift("x", by))
 
     own = spread(sign_bits, spectrum)
     other = lax.ppermute(own, "core", swap)
@@ -173,25 +179,29 @@
     partial_rows = pick((1 - 2 * core).astype(jnp.float32).reshape(1), to, rows, own, other)
     bins = spectrum.shape[1]
 
-    partial_rows, w_init = lax.optimization_barrier((partial_rows, w_init))
-    got = lax.all_to_all(partial_rows.reshape(n_y, -1, bins), "y", 0, 0)
-    activations = lax.all_gather(w_init, "z", tiled=True)
-    got, activations, h_init = lax.optimization_barrier((got, activations, h_init))
+    partial_rows, h_init, w_init = lax.optimization_barrier((partial_rows, h_init, w_init))
+    got = lax.all_to_all(partial_rows.reshape(n_y, -1, SHARE), "y", 0, 0)
+    masked = h_init * mask.astype(jnp.float32)
+    opposite = along_x(masked, 2)
+    activations = lax.all_gather(w_init, "far", tiled=True)
+    got, masked, opposite, activations = lax.optimization_barrier((got, masked, opposite, activations))
     partial_rows = jnp.sum(got, axis=0)
-    got = lax.all_to_all(partial_rows.reshape(n_z, -1, bins), "z", 0, 0)
-    templates = jnp.concatenate(across(h_init * mask.astype(jnp.float32)), axis=1)
-    order = [jnp.remainder(at_x - by, n_x) for by in range(n_x)]
+    got = lax.all_to_all(partial_rows.reshape(n_z, -1, SHARE), ring, 0, 0)
+    quarters = jnp.stack([masked, along_x(masked, 1), opposite, along_x(masked, 3)])
+    templates = [lax.dynamic_index_in_dim(quarters, jnp.remainder(at_x - i, n_x), keepdims=False) for i in range(n_x)]
+    templates = jnp.concatenate(templates, axis=1)
     got, templates = lax.optimization_barrier((got, templates))
     sketch = jnp.sum(got, axis=0) / jnp.sqrt(jnp.float32(frames * n_z * n_y * 2))
-    sketch_own = lax.all_gather(sketch, "z", tiled=True)
-    sketch = jnp.concatenate(across(sketch_own), axis=1)
+    sketch = sketch.reshape(per_block, bins)
+    sketch_own = lax.all_gather(sketch, "far", tiled=True)
+    sketch = lax.all_gather(sketch_own, "x", axis=1, tiled=True)
     for round_index in range(ITERS):
         gram = times(templates, templates, ((1,), (1,)))
         total = times(activations, gram, ((1,), (0,)))
         proj = times(sketch, templates, ((1,), (1,)))
         activations = activations * ratio(proj, total)
         cross = times(activations, sketch_own, ((0,), (0,)))
-        model = times(activations, templates[:, :bins], ((1,), (0,)))
+        model = times(activations, lax.dynamic_slice_in_dim(templates, at_x * bins, bins, axis=1), ((1,), (0,)))
         total = times(activations, model, ((0,), (0,)))
 
         def half(at):
@@ -199,7 +209,8 @@
 
         both = half(mine) + lax.ppermute(half(theirs), "core", swap)
         both = jnp.sum(lax.all_to_all(both.reshape(n_y, k // n_y, 2 * SHARE), "y", 0, 0), axis=0)
-        piece = lax.dynamic_slice(templates, (at_y * (k // n_y), mine), (k // n_y, SHARE))
+        both = both + sum(lax.ppermute(both, "near", shift("near", by)) for by in range(1, n_near))
+        piece = lax.dynamic_slice(templates, (at_y * (k // n_y), at_x * bins + mine), (k // n_y, SHARE))
         piece = piece * ratio(both[:, :SHARE], both[:, SHARE:])
         if round_index == ITERS - 1:
             pieces = everywhere(piece, ("y", "core"), n_y * 2).reshape(n_y, 2, k // n_y, SHARE)
@@ -207,15 +218,15 @@
         else:
             pieces = everywhere(piece, ("y", "x"), n_y * n_x).reshape(n_y, n_x, k // n_y, SHARE)
             other = lax.ppermute(pieces, "core", swap)
-            quarters = [[lax.dynamic_slice_in_dim(v, at, 1, axis=1).reshape(k, SHARE) for v in (pieces, other)] for at in order]
+            quarters = [[v[:, at].reshape(k, SHARE) for v in (pieces, other)] for at in range(n_x)]
             templates = jnp.concatenate([by_core(core, *quarter) for quarter in quarters], axis=1)
-    activations = lax.dynamic_slice_in_dim(activations, at_z * per_block, per_block)
+    activations = lax.dynamic_slice_in_dim(activations, at_far * per_block, per_block)
     return (activations, templates)
 
 
 def solution(mesh):
-    torus = Mesh(mesh.devices.reshape(16, 4, 2, 4), ("z", "y", "core", "x"))
-    frames = ("z", "y", "core")
+    torus = Mesh(mesh.devices.reshape(4, 4, 4, 2, 4), ("far", "near", "y", "core", "x"))
+    frames = ("far", "near", "y", "core")
     in_specs = (P(frames, "x"), P(frames), P(), P(None, "x"), P(frames, None), P(None, "x"))
     out_specs = (P(frames, None), P(None, "x"))
     return jax.shard_map(body, mesh=torus, in_specs=in_specs, out_specs=out_specs, check_vma=False)

time: 228 us -> 223 us (0.978)
  blocking collectives: 74.8 us -> 87.3 us
  other arithmetic: 7.33 us -> 2.1 us
  starting transfers between devices: 76.5 us -> 71.9 us
  matrix products: 10.9 us -> 7.36 us
  local copies, waits for them, and re-layouts: 7.55 us -> 4.8 us
    all_to_all x0 -> x2, blocking collectives: none -> 19.7 us  [body(): lax.all_to_all(both.reshape(n_y, k // n_y, 2 * SHARE), 'y', 0, 0)]
    ppermute x2, starting transfers between devices: 18.9 us -> 10.6 us  [body(): both = half(mine) + lax.ppermute(half(theirs), 'core', swap)]
    ppermute x6 -> x9, starting transfers between devices: 21.1 us -> 28.6 us  [the longest x6 20.4 us: body(): lax.ppermute(both, 'near', shift('near', by))]
    all_gather x2 -> x3, blocking collectives: 58.4 us -> 52.5 us  [the longest x1 21.2 us: body(): activations = lax.all_gather(w_init, 'far', tiled=True)]
    all_to_all x4 -> x2, starting transfers between devices: 18.1 us -> 13.6 us  [the longest x1 9.82 us: body(): got = lax.all_to_all(partial_rows.reshape(n_z, -1, SHARE), ring, 0, 0)]
    dot_general x12, matrix products: 10.9 us -> 7.36 us  [times(): lax.dot_general(a, b, (dims, ((), ())), precision=lax.Precision.HIGH, pre...]
    ppermute x6 -> x9, waiting for transfers between devices: 11.8 us -> 15.3 us  [the longest x3 8.8 us: along_x(): return lax.ppermute(value, 'x', shift('x', by))]
    all_to_all x4 -> x2, waiting for transfers between devices: 13 us -> 9.57 us  [the longest x1 6.76 us: body(): got = lax.all_to_all(partial_rows.reshape(n_z, -1, SHARE), ring, 0, 0)]
  transfers between devices with their start and end apart: 15 -> 16, of which waited for: 11 -> 13; matrix products, arithmetic and copies ran while one was open for 4% -> 1% of each run, Pallas kernels for 0% -> 0%
where the time goes in v4:
time: 223 us; the launch traced here: 222 us
  blocking collectives  87.3 us (39%)
  starting transfers between devices  71.9 us (32%)
  waiting for transfers between devices  38 us (17%)
  Pallas kernels  9.15 us (4%)
  matrix products  7.36 us (3%)
  local copies, waits for them, and re-layouts  4.8 us (2%)
    all_gather x1, blocking collectives, body(): activations = lax.all_gather(w_init, 'far', tiled=True)  21.2 us
    all_gather x1, blocking collectives, body(): sketch_own = lax.all_gather(sketch, 'far', tiled=True)  21.1 us
    ppermute x6, starting transfers between devices, body(): lax.ppermute(both, 'near', shift('near', by))  20.4 us
    all_to_all x2, blocking collectives, body(): lax.all_to_all(both.reshape(n_y, k // n_y, 2 * SHARE), 'y', 0, 0)  19.7 us
    all_to_all x1, blocking collectives, everywhere(): lax.all_to_all(jnp.broadcast_to(value[None], (count, *value.shape)), axes...  15 us
    ppermute x2, starting transfers between devices, body(): both = half(mine) + lax.ppermute(half(theirs), 'core', swap)  10.6 us
    all_gather x1, blocking collectives, body(): sketch = lax.all_gather(sketch_own, 'x', axis=1, tiled=True)  10.2 us
    all_to_all x1, starting transfers between devices, body(): got = lax.all_to_all(partial_rows.reshape(n_z, -1, SHARE), ring, 0, 0)  9.82 us
  transfers between devices with their start and end apart: 16, of which 13 were waited for; matrix products, arithmetic and copies ran while one was open for 1% of the time, Pallas kernels for 0%

profile of v4, /device:TPU:1, one launch (start us, length us, event | category | flops | bytes accessed | tf_op | source)
XLA Modules:
  0.0 221.8 jit_solution(12309716366349719341)
XLA Ops:
  0.6 3.8 %shard_map.104.own_ref = f32[2048,256]{1,0:T(8,128)S(1)} custom-call(s32[1,2048]{1,0:T(1,128)} %bitcast.84, f32[2048,256]{1,0:T(8,128)} %rows_ref.1, bf16[256,256]{1,0:T(8,128)(2,1)} %constant.101.clone.fine_ref), custom_call_target="tpu_custom_call" | custom-call | tf_op jit(solution)/shard_map/pallas_call | solution.py:81
  4.5 8.8 %collective-permute-start = (f32[2048,256]{1,0:T(8,128)S(1)}, f32[2048,256]{1,0:T(8,128)}, u32[]{:S(2)}, u32[]{:S(2)}) collective-permute-start(f32[2048,256]{1,0:T(8,128)S(1)} %shard_map.104.own_ref), channel_id=1, source_target_pairs={{0,4},{4,0},{1,5},{5,1},{2,6},{6,2},{3,7},{7,3},{8,12},{12,8},{9,1... | collective-permute-start | bytes 6291464 | tf_op jit(solution)/shard_map/ppermute | solution.py:175
  13.3 0.7 fusion.22
  14.0 0.7 fusion.21
  14.8 0.1 mul.68.to_ref
  14.8 0.1 reshape.49
  15.1 2.1 collective-permute-done.other_ref
  17.2 5.3 %shard_map.105 = f32[4096,128]{1,0:T(8,128)} custom-call(f32[1]{0:T(128)} %bitcast.sign_ref, f32[64]{0:T(128)S(1)} %mul.68.to_ref, s32[2048]{0:T(1024)S(1)} %reshape.50.rows_ref, f32[2048,256]{1,0:T(8,128)S(1)} %shard_map.104.own_ref, f32[2048,256]{1,0:T(8,128)} %collective-permute-done.other_ref), custom_call_target="tpu_custom_call" | custom-call | tf_op jit(solution)/shard_map/pallas_call | solution.py:130
  22.5 3.8 %all-to-all-start = ((f32[4,1024,128]{2,1,0:T(8,128)}), f32[4,1024,128]{2,1,0:T(8,128)S(1)}, u32[]{:S(2)}, u32[]{:S(2)}) async-start(f32[4,1024,128]{2,1,0:T(8,128)} %bitcast.63), calls=%async_computation | async-start | bytes 4194304 | tf_op jit(solution)/shard_map/all_to_all | solution.py:183
  26.4 1.9 collective-permute-start.1
  28.3 21.2 %all_gather.9 = f32[128,352]{1,0:T(8,128)S(1)} all-gather(f32[32,352]{1,0:T(8,128)S(1)} %copy-done.2), channel_id=1, replica_groups=mesh['far'=4,'near'=4,'y'=4,'core'=2,'x'=4] {'far'}, dimensions={0}, use_global_device_ids=true | all-gather | bytes 225280 | tf_op jit(solution)/shard_map/all_gather | solution.py:186
  49.5 2.8 %all-to-all-done = f32[4,1024,128]{2,1,0:T(8,128)S(1)} async-done(((f32[4,1024,128]{2,1,0:T(8,128)}), f32[4,1024,128]{2,1,0:T(8,128)S(1)}, u32[]{:S(2)}, u32[]{:S(2)}) %all-to-all-start) | async-done | bytes 2097184 | tf_op jit(solution)/shard_map/all_to_all | solution.py:183
  52.3 0.9 reduce_sum.36
  53.3 9.8 %all-to-all-start.1 = ((f32[16,64,128]{2,1,0:T(8,128)}), f32[16,64,128]{2,1,0:T(8,128)S(1)}, u32[]{:S(2)}, u32[]{:S(2)}) async-start(f32[16,64,128]{2,1,0:T(8,128)} %bitcast.7), calls=%async_computation.1 | async-start | bytes 1048576 | tf_op jit(solution)/shard_map/all_to_all | solution.py:189
  63.1 4.4 %collective-permute-start.3 = (f32[352,256]{1,0:T(8,128)S(1)}, f32[352,256]{1,0:T(8,128)S(1)}, u32[]{:S(2)}, u32[]{:S(2)}) collective-permute-start(f32[352,256]{1,0:T(8,128)S(1)} %convert_multiply_fusion), channel_id=1, source_target_pairs={{0,3},{1,0},{2,1},{3,2},{4,7},{5,4},{6,5},{7,6},{8,11},{9,8},{10,9... | collective-permute-start | bytes 1081352 | tf_op jit(solution)/shard_map/ppermute | solution.py:172
  67.5 1.9 collective-permute-start.2
  69.5 0.1 copy.23
  69.6 3.7 %collective-permute-done.3 = f32[352,256]{1,0:T(8,128)S(1)} collective-permute-done((f32[352,256]{1,0:T(8,128)S(1)}, f32[352,256]{1,0:T(8,128)S(1)}, u32[]{:S(2)}, u32[]{:S(2)}) %collective-permute-start.3) | collective-permute-done | bytes 360480 | tf_op jit(solution)/shard_map/ppermute | solution.py:172
  73.4 5.0 %collective-permute-done.2 = f32[352,256]{1,0:T(8,128)S(1)} collective-permute-done((f32[352,256]{1,0:T(8,128)S(1)}, f32[352,256]{1,0:T(8,128)S(1)}, u32[]{:S(2)}, u32[]{:S(2)}) %collective-permute-start.2) | collective-permute-done | bytes 360480 | tf_op jit(solution)/shard_map/ppermute | solution.py:172
  78.4 0.1 pad_maximum_fusion
  78.6 0.1 dynamic-slice_bitcast_fusion.3
  78.7 0.2 pad_maximum_fusion.1
  78.9 6.8 %all-to-all-done.1 = f32[16,64,128]{2,1,0:T(8,128)S(1)} async-done(((f32[16,64,128]{2,1,0:T(8,128)}), f32[16,64,128]{2,1,0:T(8,128)S(1)}, u32[]{:S(2)}, u32[]{:S(2)}) %all-to-all-start.1) | async-done | bytes 524320 | tf_op jit(solution)/shard_map/all_to_all | solution.py:189
  85.7 21.1 %all_gather.10 = f32[128,256]{1,0:T(8,128)S(1)} all-gather(f32[32,256]{1,0:T(8,128)S(1)} %div.22), channel_id=1, replica_groups=mesh['far'=4,'near'=4,'y'=4,'core'=2,'x'=4] {'far'}, dimensions={0}, use_global_device_ids=true | all-gather | bytes 163840 | tf_op jit(solution)/shard_map/all_gather | solution.py:196
  106.8 10.2 %all_gather.11 = f32[128,1024]{1,0:T(8,128)S(1)} all-gather(f32[128,256]{1,0:T(8,128)S(1)} %all_gather.10), channel_id=1, replica_groups=mesh['far'=4,'near'=4,'y'=4,'core'=2,'x'=4] {'x'}, dimensions={1}, use_global_device_ids=true | all-gather | bytes 655360 | tf_op jit(solution)/shard_map/all_gather | solution.py:197
  117.1 1.3 fusion.28
  118.3 0.7 fusion.27
  119.1 0.7 fusion.3
  119.8 0.3 fusion.29
  120.1 0.4 fusion.9
  120.4 0.3 fusion.30
  120.9 8.3 %collective-permute-start.4 = (f32[352,256]{1,0:T(8,128)S(1)}, f32[352,256]{1,0:T(8,128)S(1)}, u32[]{:S(2)}, u32[]{:S(2)}) collective-permute-start(f32[352,256]{1,0:T(8,128)S(1)} %pad_maximum_fusion.3), channel_id=1, source_target_pairs={{0,4},{4,0},{1,5},{5,1},{2,6},{6,2},{3,7},{7,3},{8,12},{12,8},{9,1... | collective-permute-start | bytes 1081352 | tf_op jit(solution)/shard_map/ppermute | solution.py:210
  129.2 1.3 collective-permute-done.4
  130.5 9.9 %all_to_all.30 = f32[4,88,256]{2,1,0:T(8,128)S(1)} all-to-all(f32[4,88,256]{2,1,0:T(8,128)S(1)} %bitcast.67), channel_id=1, replica_groups=mesh['far'=4,'near'=4,'y'=4,'core'=2,'x'=4] {'y'}, dimensions={0} | all-to-all | bytes 720896 | tf_op jit(solution)/shard_map/all_to_all | solution.py:211
  140.4 4.1 %collective-permute-start.5 = (f32[88,256]{1,0:T(8,128)S(1)}, f32[88,256]{1,0:T(8,128)S(1)}, u32[]{:S(2)}, u32[]{:S(2)}) collective-permute-start(f32[88,256]{1,0:T(8,128)S(1)} %reduce_sum.38), channel_id=1, source_target_pairs={{0,32},{32,64},{64,96},{96,0},{1,33},{33,65},{65,97},{97,1},{2,34}... | collective-permute-start | bytes 270344 | tf_op jit(solution)/shard_map/ppermute | solution.py:212
  144.6 3.6 %collective-permute-start.6 = (f32[88,256]{1,0:T(8,128)S(1)}, f32[88,256]{1,0:T(8,128)S(1)}, u32[]{:S(2)}, u32[]{:S(2)}) collective-permute-start(f32[88,256]{1,0:T(8,128)S(1)} %reduce_sum.38), channel_id=1, source_target_pairs={{0,64},{32,96},{64,0},{96,32},{1,65},{33,97},{65,1},{97,33},{2,66}... | collective-permute-start | bytes 270344 | tf_op jit(solution)/shard_map/ppermute | solution.py:212
  148.2 3.1 %collective-permute-start.7 = (f32[88,256]{1,0:T(8,128)S(1)}, f32[88,256]{1,0:T(8,128)S(1)}, u32[]{:S(2)}, u32[]{:S(2)}) collective-permute-start(f32[88,256]{1,0:T(8,128)S(1)} %reduce_sum.38), channel_id=1, source_target_pairs={{0,96},{32,0},{64,32},{96,64},{1,97},{33,1},{65,33},{97,65},{2,98}... | collective-permute-start | bytes 270344 | tf_op jit(solution)/shard_map/ppermute | solution.py:212
  151.3 0.4 collective-permute-done.6
  151.7 2.2 collective-permute-done.7
  154.0 15.0 %all_to_all.31 = f32[16,88,128]{2,1,0:T(8,128)S(1)} all-to-all(f32[16,88,128]{2,1,0:T(8,128)S(1)} %broadcast_in_dim.4), channel_id=1, replica_groups=mesh['far'=4,'near'=4,'y'=4,'core'=2,'x'=4] {'y','x'}, dimensions={0} | all-to-all | bytes 1441792 | tf_op jit(solution)/shard_map/all_to_all | solution.py:154
  169.0 5.6 %collective-permute-start.8 = (f32[4,4,88,128]{3,2,1,0:T(8,128)S(1)}, f32[4,4,88,128]{3,2,1,0:T(8,128)S(1)}, u32[]{:S(2)}, u32[]{:S(2)}) collective-permute-start(f32[4,4,88,128]{3,2,1,0:T(8,128)S(1)} %bitcast.64), channel_id=1, source_target_pairs={{0,4},{4,0},{1,5},{5,1},{2,6},{6,2},{3,7},{7,3},{8,12},{12,8},{9,1... | collective-permute-start | bytes 2162696 | tf_op jit(solution)/shard_map/ppermute | solution.py:220
  174.7 1.6 collective-permute-done.8
  176.4 0.8 fusion.24
  177.2 1.3 fusion.23
  178.5 0.2 pad_maximum_fusion.2
  178.7 0.7 fusion.6
  179.4 0.3 fusion.31
  179.7 0.4 fusion.7
  180.1 0.3 fusion.32
  180.5 2.3 %collective-permute-start.9 = (f32[352,256]{1,0:T(8,128)S(1)}, f32[352,256]{1,0:T(8,128)S(1)}, u32[]{:S(2)}, u32[]{:S(2)}) collective-permute-start(f32[352,256]{1,0:T(8,128)S(1)} %pad_maximum_fusion.4), channel_id=1, source_target_pairs={{0,4},{4,0},{1,5},{5,1},{2,6},{6,2},{3,7},{7,3},{8,12},{12,8},{9,1... | collective-permute-start | bytes 1081352 | tf_op jit(solution)/shard_map/ppermute | solution.py:210
  182.8 1.3 collective-permute-done.9
  184.1 9.9 %all_to_all.32 = f32[4,88,256]{2,1,0:T(8,128)S(1)} all-to-all(f32[4,88,256]{2,1,0:T(8,128)S(1)} %bitcast.68), channel_id=1, replica_groups=mesh['far'=4,'near'=4,'y'=4,'core'=2,'x'=4] {'y'}, dimensions={0} | all-to-all | bytes 720896 | tf_op jit(solution)/shard_map/all_to_all | solution.py:211
  194.0 3.6 %collective-permute-start.10 = (f32[88,256]{1,0:T(8,128)S(1)}, f32[88,256]{1,0:T(8,128)S(1)}, u32[]{:S(2)}, u32[]{:S(2)}) collective-permute-start(f32[88,256]{1,0:T(8,128)S(1)} %reduce_sum.39), channel_id=1, source_target_pairs={{0,32},{32,64},{64,96},{96,0},{1,33},{33,65},{65,97},{97,1},{2,34}... | collective-permute-start | bytes 270344 | tf_op jit(solution)/shard_map/ppermute | solution.py:212
  197.7 3.0 %collective-permute-start.11 = (f32[88,256]{1,0:T(8,128)S(1)}, f32[88,256]{1,0:T(8,128)S(1)}, u32[]{:S(2)}, u32[]{:S(2)}) collective-permute-start(f32[88,256]{1,0:T(8,128)S(1)} %reduce_sum.39), channel_id=1, source_target_pairs={{0,64},{32,96},{64,0},{96,32},{1,65},{33,97},{65,1},{97,33},{2,66}... | collective-permute-start | bytes 270344 | tf_op jit(solution)/shard_map/ppermute | solution.py:212
  200.7 2.9 %collective-permute-start.12 = (f32[88,256]{1,0:T(8,128)S(1)}, f32[88,256]{1,0:T(8,128)S(1)}, u32[]{:S(2)}, u32[]{:S(2)}) collective-permute-start(f32[88,256]{1,0:T(8,128)S(1)} %reduce_sum.39), channel_id=1, source_target_pairs={{0,96},{32,0},{64,32},{96,64},{1,97},{33,1},{65,33},{97,65},{2,98}... | collective-permute-start | bytes 270344 | tf_op jit(solution)/shard_map/ppermute | solution.py:212
  203.6 2.6 %collective-permute-done.11 = f32[88,256]{1,0:T(8,128)S(1)} collective-permute-done((f32[88,256]{1,0:T(8,128)S(1)}, f32[88,256]{1,0:T(8,128)S(1)}, u32[]{:S(2)}, u32[]{:S(2)}) %collective-permute-start.11) | collective-permute-done | bytes 90144 | tf_op jit(solution)/shard_map/ppermute | solution.py:212
  206.2 1.3 collective-permute-done.12
  207.6 0.8 broadcast_in_dim.5
  208.3 4.8 %all-to-all-start.5 = ((f32[8,88,128]{2,1,0:T(8,128)}), f32[8,88,128]{2,1,0:T(8,128)S(1)}, u32[]{:S(2)}, u32[]{:S(2)}) async-start(f32[8,88,128]{2,1,0:T(8,128)} %broadcast_in_dim.5), calls=%async_computation.5 | async-start | bytes 720896 | tf_op jit(solution)/shard_map/all_to_all | solution.py:154
  213.1 0.1 constant_dynamic-slice_fusion.4
  213.2 0.7 copy.25
  213.9 6.9 %all-to-all-done.5 = f32[8,88,128]{2,1,0:T(8,128)S(1)} async-done(((f32[8,88,128]{2,1,0:T(8,128)}), f32[8,88,128]{2,1,0:T(8,128)S(1)}, u32[]{:S(2)}, u32[]{:S(2)}) %all-to-all-start.5) | async-done | bytes 360480 | tf_op jit(solution)/shard_map/all_to_all | solution.py:154
  220.8 0.2 copy.24
  221.0 0.8 copy.29
  (40 shorter events, 1.1 us)
Async XLA Ops:
  0.6 14.2 %copy-start.3 = (s32[4096]{0:T(1024)S(1)}, s32[4096]{0:T(1024)}, u32[]{:S(2)}) copy-start(s32[4096]{0:T(1024)} %param.11) | copy-start | bytes 49156
  4.5 12.7 %collective-permute-start = (f32[2048,256]{1,0:T(8,128)S(1)}, f32[2048,256]{1,0:T(8,128)}, u32[]{:S(2)}, u32[]{:S(2)}) collective-permute-start(f32[2048,256]{1,0:T(8,128)S(1)} %shard_map.104.own_ref), channel_id=1, source_target_pairs={{0,4},{4,0},{1,5},{5,1},{2,6},{6,2},{3,7},{7,3},{8,12},{12,8},{9,1... | collective-permute-start | bytes 6291464 | tf_op jit(solution)/shard_map/ppermute | solution.py:175
  22.5 3.8 %copy-start = (f32[352,256]{1,0:T(8,128)S(1)}, f32[352,256]{1,0:T(8,128)}, u32[]{:S(2)}) copy-start(f32[352,256]{1,0:T(8,128)} %param.14) | copy-start | bytes 1081348
  22.5 3.8 %copy-start.1 = (s32[352,256]{1,0:T(8,128)S(1)}, s32[352,256]{1,0:T(8,128)}, u32[]{:S(2)}) copy-start(s32[352,256]{1,0:T(8,128)} %param.12) | copy-start | bytes 1081348
  22.5 5.8 %copy-start.2 = (f32[32,352]{1,0:T(8,128)S(1)}, f32[32,352]{1,0:T(8,128)}, u32[]{:S(2)}) copy-start(f32[32,352]{1,0:T(8,128)} %param.13) | copy-start | bytes 135172
  22.5 29.8 %all-to-all-start = ((f32[4,1024,128]{2,1,0:T(8,128)}), f32[4,1024,128]{2,1,0:T(8,128)S(1)}, u32[]{:S(2)}, u32[]{:S(2)}) async-start(f32[4,1024,128]{2,1,0:T(8,128)} %bitcast.63), calls=%async_computation | async-start | bytes 4194304 | tf_op jit(solution)/shard_map/all_to_all | solution.py:183
  26.4 23.2 %collective-permute-start.1 = (f32[352,256]{1,0:T(8,128)S(1)}, f32[352,256]{1,0:T(8,128)S(1)}, u32[]{:S(2)}, u32[]{:S(2)}) collective-permute-start(f32[352,256]{1,0:T(8,128)S(1)} %convert_multiply_fusion), channel_id=1, source_target_pairs={{0,2},{1,3},{2,0},{3,1},{4,6},{5,7},{6,4},{7,5},{8,10},{9,11},{10,... | collective-permute-start | bytes 1081352 | tf_op jit(solution)/shard_map/ppermute | solution.py:172
  53.3 32.4 %all-to-all-start.1 = ((f32[16,64,128]{2,1,0:T(8,128)}), f32[16,64,128]{2,1,0:T(8,128)S(1)}, u32[]{:S(2)}, u32[]{:S(2)}) async-start(f32[16,64,128]{2,1,0:T(8,128)} %bitcast.7), calls=%async_computation.1 | async-start | bytes 1048576 | tf_op jit(solution)/shard_map/all_to_all | solution.py:189
  63.1 10.3 %collective-permute-start.3 = (f32[352,256]{1,0:T(8,128)S(1)}, f32[352,256]{1,0:T(8,128)S(1)}, u32[]{:S(2)}, u32[]{:S(2)}) collective-permute-start(f32[352,256]{1,0:T(8,128)S(1)} %convert_multiply_fusion), channel_id=1, source_target_pairs={{0,3},{1,0},{2,1},{3,2},{4,7},{5,4},{6,5},{7,6},{8,11},{9,8},{10,9... | collective-permute-start | bytes 1081352 | tf_op jit(solution)/shard_map/ppermute | solution.py:172
  67.5 10.9 %collective-permute-start.2 = (f32[352,256]{1,0:T(8,128)S(1)}, f32[352,256]{1,0:T(8,128)S(1)}, u32[]{:S(2)}, u32[]{:S(2)}) collective-permute-start(f32[352,256]{1,0:T(8,128)S(1)} %convert_multiply_fusion), channel_id=1, source_target_pairs={{0,1},{1,2},{2,3},{3,0},{4,5},{5,6},{6,7},{7,4},{8,9},{9,10},{10,1... | collective-permute-start | bytes 1081352 | tf_op jit(solution)/shard_map/ppermute | solution.py:172
  120.9 9.6 %collective-permute-start.4 = (f32[352,256]{1,0:T(8,128)S(1)}, f32[352,256]{1,0:T(8,128)S(1)}, u32[]{:S(2)}, u32[]{:S(2)}) collective-permute-start(f32[352,256]{1,0:T(8,128)S(1)} %pad_maximum_fusion.3), channel_id=1, source_target_pairs={{0,4},{4,0},{1,5},{5,1},{2,6},{6,2},{3,7},{7,3},{8,12},{12,8},{9,1... | collective-permute-start | bytes 1081352 | tf_op jit(solution)/shard_map/ppermute | solution.py:210
  140.4 10.9 %collective-permute-start.5 = (f32[88,256]{1,0:T(8,128)S(1)}, f32[88,256]{1,0:T(8,128)S(1)}, u32[]{:S(2)}, u32[]{:S(2)}) collective-permute-start(f32[88,256]{1,0:T(8,128)S(1)} %reduce_sum.38), channel_id=1, source_target_pairs={{0,32},{32,64},{64,96},{96,0},{1,33},{33,65},{65,97},{97,1},{2,34}... | collective-permute-start | bytes 270344 | tf_op jit(solution)/shard_map/ppermute | solution.py:212
  144.6 7.1 %collective-permute-start.6 = (f32[88,256]{1,0:T(8,128)S(1)}, f32[88,256]{1,0:T(8,128)S(1)}, u32[]{:S(2)}, u32[]{:S(2)}) collective-permute-start(f32[88,256]{1,0:T(8,128)S(1)} %reduce_sum.38), channel_id=1, source_target_pairs={{0,64},{32,96},{64,0},{96,32},{1,65},{33,97},{65,1},{97,33},{2,66}... | collective-permute-start | bytes 270344 | tf_op jit(solution)/shard_map/ppermute | solution.py:212
  148.2 5.7 %collective-permute-start.7 = (f32[88,256]{1,0:T(8,128)S(1)}, f32[88,256]{1,0:T(8,128)S(1)}, u32[]{:S(2)}, u32[]{:S(2)}) collective-permute-start(f32[88,256]{1,0:T(8,128)S(1)} %reduce_sum.38), channel_id=1, source_target_pairs={{0,96},{32,0},{64,32},{96,64},{1,97},{33,1},{65,33},{97,65},{2,98}... | collective-permute-start | bytes 270344 | tf_op jit(solution)/shard_map/ppermute | solution.py:212
  169.0 7.2 %collective-permute-start.8 = (f32[4,4,88,128]{3,2,1,0:T(8,128)S(1)}, f32[4,4,88,128]{3,2,1,0:T(8,128)S(1)}, u32[]{:S(2)}, u32[]{:S(2)}) collective-permute-start(f32[4,4,88,128]{3,2,1,0:T(8,128)S(1)} %bitcast.64), channel_id=1, source_target_pairs={{0,4},{4,0},{1,5},{5,1},{2,6},{6,2},{3,7},{7,3},{8,12},{12,8},{9,1... | collective-permute-start | bytes 2162696 | tf_op jit(solution)/shard_map/ppermute | solution.py:220
  180.5 3.6 %collective-permute-start.9 = (f32[352,256]{1,0:T(8,128)S(1)}, f32[352,256]{1,0:T(8,128)S(1)}, u32[]{:S(2)}, u32[]{:S(2)}) collective-permute-start(f32[352,256]{1,0:T(8,128)S(1)} %pad_maximum_fusion.4), channel_id=1, source_target_pairs={{0,4},{4,0},{1,5},{5,1},{2,6},{6,2},{3,7},{7,3},{8,12},{12,8},{9,1... | collective-permute-start | bytes 1081352 | tf_op jit(solution)/shard_map/ppermute | solution.py:210
  194.0 9.6 %collective-permute-start.10 = (f32[88,256]{1,0:T(8,128)S(1)}, f32[88,256]{1,0:T(8,128)S(1)}, u32[]{:S(2)}, u32[]{:S(2)}) collective-permute-start(f32[88,256]{1,0:T(8,128)S(1)} %reduce_sum.39), channel_id=1, source_target_pairs={{0,32},{32,64},{64,96},{96,0},{1,33},{33,65},{65,97},{97,1},{2,34}... | collective-permute-start | bytes 270344 | tf_op jit(solution)/shard_map/ppermute | solution.py:212
  197.7 8.5 %collective-permute-start.11 = (f32[88,256]{1,0:T(8,128)S(1)}, f32[88,256]{1,0:T(8,128)S(1)}, u32[]{:S(2)}, u32[]{:S(2)}) collective-permute-start(f32[88,256]{1,0:T(8,128)S(1)} %reduce_sum.39), channel_id=1, source_target_pairs={{0,64},{32,96},{64,0},{96,32},{1,65},{33,97},{65,1},{97,33},{2,66}... | collective-permute-start | bytes 270344 | tf_op jit(solution)/shard_map/ppermute | solution.py:212
  200.7 6.8 %collective-permute-start.12 = (f32[88,256]{1,0:T(8,128)S(1)}, f32[88,256]{1,0:T(8,128)S(1)}, u32[]{:S(2)}, u32[]{:S(2)}) collective-permute-start(f32[88,256]{1,0:T(8,128)S(1)} %reduce_sum.39), channel_id=1, source_target_pairs={{0,96},{32,0},{64,32},{96,64},{1,97},{33,1},{65,33},{97,65},{2,98}... | collective-permute-start | bytes 270344 | tf_op jit(solution)/shard_map/ppermute | solution.py:212
  208.3 12.5 %all-to-all-start.5 = ((f32[8,88,128]{2,1,0:T(8,128)}), f32[8,88,128]{2,1,0:T(8,128)S(1)}, u32[]{:S(2)}, u32[]{:S(2)}) async-start(f32[8,88,128]{2,1,0:T(8,128)} %broadcast_in_dim.5), calls=%async_computation.5 | async-start | bytes 720896 | tf_op jit(solution)/shard_map/all_to_all | solution.py:154

commit v5 on v4

--- a/solution.py
+++ b/solution.py
@@ -190,14 +190,17 @@
     quarters = jnp.stack([masked, along_x(masked, 1), opposite, along_x(masked, 3)])
     templates = [lax.dynamic_index_in_dim(quarters, jnp.remainder(at_x - i, n_x), keepdims=False) for i in range(n_x)]
     templates = jnp.concatenate(templates, axis=1)
-    got, templates = lax.optimization_barrier((got, templates))
+    gram = times(templates, templates, ((1,), (1,)))
+    total = times(activations, gram, ((1,), (0,)))
+    got, templates, total = lax.optimization_barrier((got, templates, total))
     sketch = jnp.sum(got, axis=0) / jnp.sqrt(jnp.float32(frames * n_z * n_y * 2))
     sketch = sketch.reshape(per_block, bins)
     sketch_own = lax.all_gather(sketch, "far", tiled=True)
     sketch = lax.all_gather(sketch_own, "x", axis=1, tiled=True)
     for round_index in range(ITERS):
-        gram = times(templates, templates, ((1,), (1,)))
-        total = times(activations, gram, ((1,), (0,)))
+        if round_index:
+            gram = times(templates, templates, ((1,), (1,)))
+            total = times(activations, gram, ((1,), (0,)))
         proj = times(sketch, templates, ((1,), (1,)))
         activations = activations * ratio(proj, total)
         cross = times(activations, sketch_own, ((0,), (0,)))

time: 223 us -> 221 us (level)
  transfers between devices with their start and end apart: 16 -> 16, of which waited for: 13 -> 13; matrix products, arithmetic and copies ran while one was open for 1% -> 2% of each run, Pallas kernels for 0% -> 0%
where the time goes in v5:
time: 221 us; the launch traced here: 220 us
  blocking collectives  87.3 us (40%)
  starting transfers between devices  72 us (33%)
  waiting for transfers between devices  35.9 us (16%)
  Pallas kernels  9.15 us (4%)
  matrix products  7.4 us (3%)
  local copies, waits for them, and re-layouts  4.8 us (2%)
    all_gather x1, blocking collectives, body(): activations = lax.all_gather(w_init, 'far', tiled=True)  21.2 us
    all_gather x1, blocking collectives, body(): sketch_own = lax.all_gather(sketch, 'far', tiled=True)  21.1 us
    ppermute x6, starting transfers between devices, body(): lax.ppermute(both, 'near', shift('near', by))  20.4 us
    all_to_all x2, blocking collectives, body(): lax.all_to_all(both.reshape(n_y, k // n_y, 2 * SHARE), 'y', 0, 0)  19.7 us
    all_to_all x1, blocking collectives, everywhere(): lax.all_to_all(jnp.broadcast_to(value[None], (count, *value.shape)), axes...  15 us
    ppermute x2, starting transfers between devices, body(): both = half(mine) + lax.ppermute(half(theirs), 'core', swap)  10.6 us
    all_gather x1, blocking collectives, body(): sketch = lax.all_gather(sketch_own, 'x', axis=1, tiled=True)  10.2 us
    all_to_all x1, starting transfers between devices, body(): got = lax.all_to_all(partial_rows.reshape(n_z, -1, SHARE), ring, 0, 0)  9.82 us
  transfers between devices with their start and end apart: 16, of which 13 were waited for; matrix products, arithmetic and copies ran while one was open for 2% of the time, Pallas kernels for 0%

profile of v5, /device:TPU:1, one launch (start us, length us, event | category | flops | bytes accessed | tf_op | source)
XLA Modules:
  0.0 219.9 jit_solution(4271270824373526028)
XLA Ops:
  0.6 3.8 %shard_map.104.own_ref = f32[2048,256]{1,0:T(8,128)S(1)} custom-call(s32[1,2048]{1,0:T(1,128)} %bitcast.82, f32[2048,256]{1,0:T(8,128)} %rows_ref.1, bf16[256,256]{1,0:T(8,128)(2,1)} %constant.101.clone.fine_ref), custom_call_target="tpu_custom_call" | custom-call | tf_op jit(solution)/shard_map/pallas_call | solution.py:81
  4.5 8.8 %collective-permute-start = (f32[2048,256]{1,0:T(8,128)S(1)}, f32[2048,256]{1,0:T(8,128)}, u32[]{:S(2)}, u32[]{:S(2)}) collective-permute-start(f32[2048,256]{1,0:T(8,128)S(1)} %shard_map.104.own_ref), channel_id=1, source_target_pairs={{0,4},{4,0},{1,5},{5,1},{2,6},{6,2},{3,7},{7,3},{8,12},{12,8},{9,1... | collective-permute-start | bytes 6291464 | tf_op jit(solution)/shard_map/ppermute | solution.py:175
  13.3 0.7 fusion.19
  14.0 0.7 fusion.18
  14.8 0.1 reshape.49
  15.1 2.1 collective-permute-done.other_ref
  17.2 5.3 %shard_map.105 = f32[4096,128]{1,0:T(8,128)} custom-call(f32[1]{0:T(128)} %bitcast.sign_ref, f32[64]{0:T(128)S(1)} %mul.68.to_ref, s32[2048]{0:T(1024)S(1)} %reshape.50.rows_ref, f32[2048,256]{1,0:T(8,128)S(1)} %shard_map.104.own_ref, f32[2048,256]{1,0:T(8,128)} %collective-permute-done.other_ref), custom_call_target="tpu_custom_call" | custom-call | tf_op jit(solution)/shard_map/pallas_call | solution.py:130
  22.5 3.8 %all-to-all-start = ((f32[4,1024,128]{2,1,0:T(8,128)}), f32[4,1024,128]{2,1,0:T(8,128)S(1)}, u32[]{:S(2)}, u32[]{:S(2)}) async-start(f32[4,1024,128]{2,1,0:T(8,128)} %bitcast.61), calls=%async_computation | async-start | bytes 4194304 | tf_op jit(solution)/shard_map/all_to_all | solution.py:183
  26.4 1.9 collective-permute-start.1
  28.3 21.2 %all_gather.9 = f32[128,352]{1,0:T(8,128)S(1)} all-gather(f32[32,352]{1,0:T(8,128)S(1)} %copy-done.2), channel_id=1, replica_groups=mesh['far'=4,'near'=4,'y'=4,'core'=2,'x'=4] {'far'}, dimensions={0}, use_global_device_ids=true | all-gather | bytes 225280 | tf_op jit(solution)/shard_map/all_gather | solution.py:186
  49.5 2.8 %all-to-all-done = f32[4,1024,128]{2,1,0:T(8,128)S(1)} async-done(((f32[4,1024,128]{2,1,0:T(8,128)}), f32[4,1024,128]{2,1,0:T(8,128)S(1)}, u32[]{:S(2)}, u32[]{:S(2)}) %all-to-all-start) | async-done | bytes 2097184 | tf_op jit(solution)/shard_map/all_to_all | solution.py:183
  52.3 0.9 reduce_sum.36
  53.3 9.8 %all-to-all-start.1 = ((f32[16,64,128]{2,1,0:T(8,128)}), f32[16,64,128]{2,1,0:T(8,128)S(1)}, u32[]{:S(2)}, u32[]{:S(2)}) async-start(f32[16,64,128]{2,1,0:T(8,128)} %bitcast.7), calls=%async_computation.1 | async-start | bytes 1048576 | tf_op jit(solution)/shard_map/all_to_all | solution.py:189
  63.1 4.4 %collective-permute-start.3 = (f32[352,256]{1,0:T(8,128)S(1)}, f32[352,256]{1,0:T(8,128)S(1)}, u32[]{:S(2)}, u32[]{:S(2)}) collective-permute-start(f32[352,256]{1,0:T(8,128)S(1)} %convert_multiply_fusion), channel_id=1, source_target_pairs={{0,3},{1,0},{2,1},{3,2},{4,7},{5,4},{6,5},{7,6},{8,11},{9,8},{10,9... | collective-permute-start | bytes 1081352 | tf_op jit(solution)/shard_map/ppermute | solution.py:172
  67.5 1.9 collective-permute-start.2
  69.5 0.1 copy.23
  69.6 3.7 %collective-permute-done.3 = f32[352,256]{1,0:T(8,128)S(1)} collective-permute-done((f32[352,256]{1,0:T(8,128)S(1)}, f32[352,256]{1,0:T(8,128)S(1)}, u32[]{:S(2)}, u32[]{:S(2)}) %collective-permute-start.3) | collective-permute-done | bytes 360480 | tf_op jit(solution)/shard_map/ppermute | solution.py:172
  73.4 5.0 %collective-permute-done.2 = f32[352,256]{1,0:T(8,128)S(1)} collective-permute-done((f32[352,256]{1,0:T(8,128)S(1)}, f32[352,256]{1,0:T(8,128)S(1)}, u32[]{:S(2)}, u32[]{:S(2)}) %collective-permute-start.2) | collective-permute-done | bytes 360480 | tf_op jit(solution)/shard_map/ppermute | solution.py:172
  78.4 0.1 pad_maximum_fusion
  78.6 0.1 dynamic-slice_bitcast_fusion.3
  78.7 1.3 fusion.20
  80.0 0.2 pad_maximum_fusion.1
  80.2 0.7 fusion.25
  80.9 4.8 %all-to-all-done.1 = f32[16,64,128]{2,1,0:T(8,128)S(1)} async-done(((f32[16,64,128]{2,1,0:T(8,128)}), f32[16,64,128]{2,1,0:T(8,128)S(1)}, u32[]{:S(2)}, u32[]{:S(2)}) %all-to-all-start.1) | async-done | bytes 524320 | tf_op jit(solution)/shard_map/all_to_all | solution.py:189
  85.7 21.1 %all_gather.10 = f32[128,256]{1,0:T(8,128)S(1)} all-gather(f32[32,256]{1,0:T(8,128)S(1)} %div.22), channel_id=1, replica_groups=mesh['far'=4,'near'=4,'y'=4,'core'=2,'x'=4] {'far'}, dimensions={0}, use_global_device_ids=true | all-gather | bytes 163840 | tf_op jit(solution)/shard_map/all_gather | solution.py:198
  106.8 10.2 %all_gather.11 = f32[128,1024]{1,0:T(8,128)S(1)} all-gather(f32[128,256]{1,0:T(8,128)S(1)} %all_gather.10), channel_id=1, replica_groups=mesh['far'=4,'near'=4,'y'=4,'core'=2,'x'=4] {'x'}, dimensions={1}, use_global_device_ids=true | all-gather | bytes 655360 | tf_op jit(solution)/shard_map/all_gather | solution.py:199
  117.1 0.7 fusion.26
  117.8 0.1 sqrt_multiply_fusion
  117.9 0.3 fusion.27
  118.2 0.4 fusion.6
  118.6 0.3 fusion.28
  119.0 8.3 %collective-permute-start.4 = (f32[352,256]{1,0:T(8,128)S(1)}, f32[352,256]{1,0:T(8,128)S(1)}, u32[]{:S(2)}, u32[]{:S(2)}) collective-permute-start(f32[352,256]{1,0:T(8,128)S(1)} %pad_maximum_fusion.3), channel_id=1, source_target_pairs={{0,4},{4,0},{1,5},{5,1},{2,6},{6,2},{3,7},{7,3},{8,12},{12,8},{9,1... | collective-permute-start | bytes 1081352 | tf_op jit(solution)/shard_map/ppermute | solution.py:213
  127.3 1.3 collective-permute-done.4
  128.7 9.9 %all_to_all.30 = f32[4,88,256]{2,1,0:T(8,128)S(1)} all-to-all(f32[4,88,256]{2,1,0:T(8,128)S(1)} %bitcast.65), channel_id=1, replica_groups=mesh['far'=4,'near'=4,'y'=4,'core'=2,'x'=4] {'y'}, dimensions={0} | all-to-all | bytes 720896 | tf_op jit(solution)/shard_map/all_to_all | solution.py:214
  138.5 4.1 %collective-permute-start.5 = (f32[88,256]{1,0:T(8,128)S(1)}, f32[88,256]{1,0:T(8,128)S(1)}, u32[]{:S(2)}, u32[]{:S(2)}) collective-permute-start(f32[88,256]{1,0:T(8,128)S(1)} %reduce_sum.38), channel_id=1, source_target_pairs={{0,32},{32,64},{64,96},{96,0},{1,33},{33,65},{65,97},{97,1},{2,34}... | collective-permute-start | bytes 270344 | tf_op jit(solution)/shard_map/ppermute | solution.py:215
  142.7 3.6 %collective-permute-start.6 = (f32[88,256]{1,0:T(8,128)S(1)}, f32[88,256]{1,0:T(8,128)S(1)}, u32[]{:S(2)}, u32[]{:S(2)}) collective-permute-start(f32[88,256]{1,0:T(8,128)S(1)} %reduce_sum.38), channel_id=1, source_target_pairs={{0,64},{32,96},{64,0},{96,32},{1,65},{33,97},{65,1},{97,33},{2,66}... | collective-permute-start | bytes 270344 | tf_op jit(solution)/shard_map/ppermute | solution.py:215
  146.3 3.1 %collective-permute-start.7 = (f32[88,256]{1,0:T(8,128)S(1)}, f32[88,256]{1,0:T(8,128)S(1)}, u32[]{:S(2)}, u32[]{:S(2)}) collective-permute-start(f32[88,256]{1,0:T(8,128)S(1)} %reduce_sum.38), channel_id=1, source_target_pairs={{0,96},{32,0},{64,32},{96,64},{1,97},{33,1},{65,33},{97,65},{2,98}... | collective-permute-start | bytes 270344 | tf_op jit(solution)/shard_map/ppermute | solution.py:215
  149.4 0.4 collective-permute-done.6
  149.8 2.2 collective-permute-done.7
  152.1 15.0 %all_to_all.31 = f32[16,88,128]{2,1,0:T(8,128)S(1)} all-to-all(f32[16,88,128]{2,1,0:T(8,128)S(1)} %broadcast_in_dim.4), channel_id=1, replica_groups=mesh['far'=4,'near'=4,'y'=4,'core'=2,'x'=4] {'y','x'}, dimensions={0} | all-to-all | bytes 1441792 | tf_op jit(solution)/shard_map/all_to_all | solution.py:154
  167.1 5.6 %collective-permute-start.8 = (f32[4,4,88,128]{3,2,1,0:T(8,128)S(1)}, f32[4,4,88,128]{3,2,1,0:T(8,128)S(1)}, u32[]{:S(2)}, u32[]{:S(2)}) collective-permute-start(f32[4,4,88,128]{3,2,1,0:T(8,128)S(1)} %bitcast.62), channel_id=1, source_target_pairs={{0,4},{4,0},{1,5},{5,1},{2,6},{6,2},{3,7},{7,3},{8,12},{12,8},{9,1... | collective-permute-start | bytes 2162696 | tf_op jit(solution)/shard_map/ppermute | solution.py:223
  172.8 1.6 collective-permute-done.8
  174.6 0.8 fusion.22
  175.3 1.3 fusion.21
  176.7 0.2 pad_maximum_fusion.2
  176.9 0.7 fusion.3
  177.6 0.3 fusion.29
  177.9 0.4 fusion.4
  178.2 0.3 fusion.30
  178.6 2.3 %collective-permute-start.9 = (f32[352,256]{1,0:T(8,128)S(1)}, f32[352,256]{1,0:T(8,128)S(1)}, u32[]{:S(2)}, u32[]{:S(2)}) collective-permute-start(f32[352,256]{1,0:T(8,128)S(1)} %pad_maximum_fusion.4), channel_id=1, source_target_pairs={{0,4},{4,0},{1,5},{5,1},{2,6},{6,2},{3,7},{7,3},{8,12},{12,8},{9,1... | collective-permute-start | bytes 1081352 | tf_op jit(solution)/shard_map/ppermute | solution.py:213
  180.9 1.3 collective-permute-done.9
  182.2 9.9 %all_to_all.32 = f32[4,88,256]{2,1,0:T(8,128)S(1)} all-to-all(f32[4,88,256]{2,1,0:T(8,128)S(1)} %bitcast.66), channel_id=1, replica_groups=mesh['far'=4,'near'=4,'y'=4,'core'=2,'x'=4] {'y'}, dimensions={0} | all-to-all | bytes 720896 | tf_op jit(solution)/shard_map/all_to_all | solution.py:214
  192.1 3.6 %collective-permute-start.10 = (f32[88,256]{1,0:T(8,128)S(1)}, f32[88,256]{1,0:T(8,128)S(1)}, u32[]{:S(2)}, u32[]{:S(2)}) collective-permute-start(f32[88,256]{1,0:T(8,128)S(1)} %reduce_sum.39), channel_id=1, source_target_pairs={{0,32},{32,64},{64,96},{96,0},{1,33},{33,65},{65,97},{97,1},{2,34}... | collective-permute-start | bytes 270344 | tf_op jit(solution)/shard_map/ppermute | solution.py:215
  195.8 3.0 %collective-permute-start.11 = (f32[88,256]{1,0:T(8,128)S(1)}, f32[88,256]{1,0:T(8,128)S(1)}, u32[]{:S(2)}, u32[]{:S(2)}) collective-permute-start(f32[88,256]{1,0:T(8,128)S(1)} %reduce_sum.39), channel_id=1, source_target_pairs={{0,64},{32,96},{64,0},{96,32},{1,65},{33,97},{65,1},{97,33},{2,66}... | collective-permute-start | bytes 270344 | tf_op jit(solution)/shard_map/ppermute | solution.py:215
  198.8 2.9 %collective-permute-start.12 = (f32[88,256]{1,0:T(8,128)S(1)}, f32[88,256]{1,0:T(8,128)S(1)}, u32[]{:S(2)}, u32[]{:S(2)}) collective-permute-start(f32[88,256]{1,0:T(8,128)S(1)} %reduce_sum.39), channel_id=1, source_target_pairs={{0,96},{32,0},{64,32},{96,64},{1,97},{33,1},{65,33},{97,65},{2,98}... | collective-permute-start | bytes 270344 | tf_op jit(solution)/shard_map/ppermute | solution.py:215
  201.7 2.6 %collective-permute-done.11 = f32[88,256]{1,0:T(8,128)S(1)} collective-permute-done((f32[88,256]{1,0:T(8,128)S(1)}, f32[88,256]{1,0:T(8,128)S(1)}, u32[]{:S(2)}, u32[]{:S(2)}) %collective-permute-start.11) | collective-permute-done | bytes 90144 | tf_op jit(solution)/shard_map/ppermute | solution.py:215
  204.3 1.3 collective-permute-done.12
  205.7 0.8 broadcast_in_dim.5
  206.4 4.8 %all-to-all-start.5 = ((f32[8,88,128]{2,1,0:T(8,128)}), f32[8,88,128]{2,1,0:T(8,128)S(1)}, u32[]{:S(2)}, u32[]{:S(2)}) async-start(f32[8,88,128]{2,1,0:T(8,128)} %broadcast_in_dim.5), calls=%async_computation.5 | async-start | bytes 720896 | tf_op jit(solution)/shard_map/all_to_all | solution.py:154
  211.2 0.1 constant_dynamic-slice_fusion.4
  211.3 0.7 copy.25
  212.1 6.9 %all-to-all-done.5 = f32[8,88,128]{2,1,0:T(8,128)S(1)} async-done(((f32[8,88,128]{2,1,0:T(8,128)}), f32[8,88,128]{2,1,0:T(8,128)S(1)}, u32[]{:S(2)}, u32[]{:S(2)}) %all-to-all-start.5) | async-done | bytes 360480 | tf_op jit(solution)/shard_map/all_to_all | solution.py:154
  219.0 0.2 copy.24
  219.2 0.8 copy.29
  (40 shorter events, 1.2 us)
Async XLA Ops:
  0.6 14.2 %copy-start.3 = (s32[4096]{0:T(1024)S(1)}, s32[4096]{0:T(1024)}, u32[]{:S(2)}) copy-start(s32[4096]{0:T(1024)} %param.11) | copy-start | bytes 49156
  4.5 12.7 %collective-permute-start = (f32[2048,256]{1,0:T(8,128)S(1)}, f32[2048,256]{1,0:T(8,128)}, u32[]{:S(2)}, u32[]{:S(2)}) collective-permute-start(f32[2048,256]{1,0:T(8,128)S(1)} %shard_map.104.own_ref), channel_id=1, source_target_pairs={{0,4},{4,0},{1,5},{5,1},{2,6},{6,2},{3,7},{7,3},{8,12},{12,8},{9,1... | collective-permute-start | bytes 6291464 | tf_op jit(solution)/shard_map/ppermute | solution.py:175
  22.5 3.8 %copy-start = (f32[352,256]{1,0:T(8,128)S(1)}, f32[352,256]{1,0:T(8,128)}, u32[]{:S(2)}) copy-start(f32[352,256]{1,0:T(8,128)} %param.14) | copy-start | bytes 1081348
  22.5 3.8 %copy-start.1 = (s32[352,256]{1,0:T(8,128)S(1)}, s32[352,256]{1,0:T(8,128)}, u32[]{:S(2)}) copy-start(s32[352,256]{1,0:T(8,128)} %param.12) | copy-start | bytes 1081348
  22.5 5.8 %copy-start.2 = (f32[32,352]{1,0:T(8,128)S(1)}, f32[32,352]{1,0:T(8,128)}, u32[]{:S(2)}) copy-start(f32[32,352]{1,0:T(8,128)} %param.13) | copy-start | bytes 135172
  22.5 29.8 %all-to-all-start = ((f32[4,1024,128]{2,1,0:T(8,128)}), f32[4,1024,128]{2,1,0:T(8,128)S(1)}, u32[]{:S(2)}, u32[]{:S(2)}) async-start(f32[4,1024,128]{2,1,0:T(8,128)} %bitcast.61), calls=%async_computation | async-start | bytes 4194304 | tf_op jit(solution)/shard_map/all_to_all | solution.py:183
  26.4 23.2 %collective-permute-start.1 = (f32[352,256]{1,0:T(8,128)S(1)}, f32[352,256]{1,0:T(8,128)S(1)}, u32[]{:S(2)}, u32[]{:S(2)}) collective-permute-start(f32[352,256]{1,0:T(8,128)S(1)} %convert_multiply_fusion), channel_id=1, source_target_pairs={{0,2},{1,3},{2,0},{3,1},{4,6},{5,7},{6,4},{7,5},{8,10},{9,11},{10,... | collective-permute-start | bytes 1081352 | tf_op jit(solution)/shard_map/ppermute | solution.py:172
  53.3 32.4 %all-to-all-start.1 = ((f32[16,64,128]{2,1,0:T(8,128)}), f32[16,64,128]{2,1,0:T(8,128)S(1)}, u32[]{:S(2)}, u32[]{:S(2)}) async-start(f32[16,64,128]{2,1,0:T(8,128)} %bitcast.7), calls=%async_computation.1 | async-start | bytes 1048576 | tf_op jit(solution)/shard_map/all_to_all | solution.py:189
  63.1 10.3 %collective-permute-start.3 = (f32[352,256]{1,0:T(8,128)S(1)}, f32[352,256]{1,0:T(8,128)S(1)}, u32[]{:S(2)}, u32[]{:S(2)}) collective-permute-start(f32[352,256]{1,0:T(8,128)S(1)} %convert_multiply_fusion), channel_id=1, source_target_pairs={{0,3},{1,0},{2,1},{3,2},{4,7},{5,4},{6,5},{7,6},{8,11},{9,8},{10,9... | collective-permute-start | bytes 1081352 | tf_op jit(solution)/shard_map/ppermute | solution.py:172
  67.5 10.9 %collective-permute-start.2 = (f32[352,256]{1,0:T(8,128)S(1)}, f32[352,256]{1,0:T(8,128)S(1)}, u32[]{:S(2)}, u32[]{:S(2)}) collective-permute-start(f32[352,256]{1,0:T(8,128)S(1)} %convert_multiply_fusion), channel_id=1, source_target_pairs={{0,1},{1,2},{2,3},{3,0},{4,5},{5,6},{6,7},{7,4},{8,9},{9,10},{10,1... | collective-permute-start | bytes 1081352 | tf_op jit(solution)/shard_map/ppermute | solution.py:172
  119.0 9.6 %collective-permute-start.4 = (f32[352,256]{1,0:T(8,128)S(1)}, f32[352,256]{1,0:T(8,128)S(1)}, u32[]{:S(2)}, u32[]{:S(2)}) collective-permute-start(f32[352,256]{1,0:T(8,128)S(1)} %pad_maximum_fusion.3), channel_id=1, source_target_pairs={{0,4},{4,0},{1,5},{5,1},{2,6},{6,2},{3,7},{7,3},{8,12},{12,8},{9,1... | collective-permute-start | bytes 1081352 | tf_op jit(solution)/shard_map/ppermute | solution.py:213
  138.5 10.9 %collective-permute-start.5 = (f32[88,256]{1,0:T(8,128)S(1)}, f32[88,256]{1,0:T(8,128)S(1)}, u32[]{:S(2)}, u32[]{:S(2)}) collective-permute-start(f32[88,256]{1,0:T(8,128)S(1)} %reduce_sum.38), channel_id=1, source_target_pairs={{0,32},{32,64},{64,96},{96,0},{1,33},{33,65},{65,97},{97,1},{2,34}... | collective-permute-start | bytes 270344 | tf_op jit(solution)/shard_map/ppermute | solution.py:215
  142.7 7.1 %collective-permute-start.6 = (f32[88,256]{1,0:T(8,128)S(1)}, f32[88,256]{1,0:T(8,128)S(1)}, u32[]{:S(2)}, u32[]{:S(2)}) collective-permute-start(f32[88,256]{1,0:T(8,128)S(1)} %reduce_sum.38), channel_id=1, source_target_pairs={{0,64},{32,96},{64,0},{96,32},{1,65},{33,97},{65,1},{97,33},{2,66}... | collective-permute-start | bytes 270344 | tf_op jit(solution)/shard_map/ppermute | solution.py:215
  146.3 5.7 %collective-permute-start.7 = (f32[88,256]{1,0:T(8,128)S(1)}, f32[88,256]{1,0:T(8,128)S(1)}, u32[]{:S(2)}, u32[]{:S(2)}) collective-permute-start(f32[88,256]{1,0:T(8,128)S(1)} %reduce_sum.38), channel_id=1, source_target_pairs={{0,96},{32,0},{64,32},{96,64},{1,97},{33,1},{65,33},{97,65},{2,98}... | collective-permute-start | bytes 270344 | tf_op jit(solution)/shard_map/ppermute | solution.py:215
  167.1 7.2 %collective-permute-start.8 = (f32[4,4,88,128]{3,2,1,0:T(8,128)S(1)}, f32[4,4,88,128]{3,2,1,0:T(8,128)S(1)}, u32[]{:S(2)}, u32[]{:S(2)}) collective-permute-start(f32[4,4,88,128]{3,2,1,0:T(8,128)S(1)} %bitcast.62), channel_id=1, source_target_pairs={{0,4},{4,0},{1,5},{5,1},{2,6},{6,2},{3,7},{7,3},{8,12},{12,8},{9,1... | collective-permute-start | bytes 2162696 | tf_op jit(solution)/shard_map/ppermute | solution.py:223
  178.6 3.6 %collective-permute-start.9 = (f32[352,256]{1,0:T(8,128)S(1)}, f32[352,256]{1,0:T(8,128)S(1)}, u32[]{:S(2)}, u32[]{:S(2)}) collective-permute-start(f32[352,256]{1,0:T(8,128)S(1)} %pad_maximum_fusion.4), channel_id=1, source_target_pairs={{0,4},{4,0},{1,5},{5,1},{2,6},{6,2},{3,7},{7,3},{8,12},{12,8},{9,1... | collective-permute-start | bytes 1081352 | tf_op jit(solution)/shard_map/ppermute | solution.py:213
  192.1 9.6 %collective-permute-start.10 = (f32[88,256]{1,0:T(8,128)S(1)}, f32[88,256]{1,0:T(8,128)S(1)}, u32[]{:S(2)}, u32[]{:S(2)}) collective-permute-start(f32[88,256]{1,0:T(8,128)S(1)} %reduce_sum.39), channel_id=1, source_target_pairs={{0,32},{32,64},{64,96},{96,0},{1,33},{33,65},{65,97},{97,1},{2,34}... | collective-permute-start | bytes 270344 | tf_op jit(solution)/shard_map/ppermute | solution.py:215
  195.8 8.5 %collective-permute-start.11 = (f32[88,256]{1,0:T(8,128)S(1)}, f32[88,256]{1,0:T(8,128)S(1)}, u32[]{:S(2)}, u32[]{:S(2)}) collective-permute-start(f32[88,256]{1,0:T(8,128)S(1)} %reduce_sum.39), channel_id=1, source_target_pairs={{0,64},{32,96},{64,0},{96,32},{1,65},{33,97},{65,1},{97,33},{2,66}... | collective-permute-start | bytes 270344 | tf_op jit(solution)/shard_map/ppermute | solution.py:215
  198.8 6.8 %collective-permute-start.12 = (f32[88,256]{1,0:T(8,128)S(1)}, f32[88,256]{1,0:T(8,128)S(1)}, u32[]{:S(2)}, u32[]{:S(2)}) collective-permute-start(f32[88,256]{1,0:T(8,128)S(1)} %reduce_sum.39), channel_id=1, source_target_pairs={{0,96},{32,0},{64,32},{96,64},{1,97},{33,1},{65,33},{97,65},{2,98}... | collective-permute-start | bytes 270344 | tf_op jit(solution)/shard_map/ppermute | solution.py:215
  206.4 12.5 %all-to-all-start.5 = ((f32[8,88,128]{2,1,0:T(8,128)}), f32[8,88,128]{2,1,0:T(8,128)S(1)}, u32[]{:S(2)}, u32[]{:S(2)}) async-start(f32[8,88,128]{2,1,0:T(8,128)} %broadcast_in_dim.5), calls=%async_computation.5 | async-start | bytes 720896 | tf_op jit(solution)/shard_map/all_to_all | solution.py:154

commit v6 on v5

--- a/solution.py
+++ b/solution.py
@@ -10,7 +10,7 @@
 ITERS = 2
 FINE = 256
 SHARE = 128
-GROUP = 64
+GROUP = 128
 
 
 def sylvester(count):

time: 221 us -> 221 us (level)
  no operation moved by 1% of the time
where the time goes in v6:
time: 221 us; the launch traced here: 220 us
  blocking collectives  87.3 us (40%)
  starting transfers between devices  72 us (33%)
  waiting for transfers between devices  35.9 us (16%)
  Pallas kernels  9.04 us (4%)
  matrix products  7.4 us (3%)
  local copies, waits for them, and re-layouts  4.8 us (2%)
    all_gather x1, blocking collectives, body(): activations = lax.all_gather(w_init, 'far', tiled=True)  21.2 us
    all_gather x1, blocking collectives, body(): sketch_own = lax.all_gather(sketch, 'far', tiled=True)  21.1 us
    ppermute x6, starting transfers between devices, body(): lax.ppermute(both, 'near', shift('near', by))  20.4 us
    all_to_all x2, blocking collectives, body(): lax.all_to_all(both.reshape(n_y, k // n_y, 2 * SHARE), 'y', 0, 0)  19.7 us
    all_to_all x1, blocking collectives, everywhere(): lax.all_to_all(jnp.broadcast_to(value[None], (count, *value.shape)), axes...  15 us
    ppermute x2, starting transfers between devices, body(): both = half(mine) + lax.ppermute(half(theirs), 'core', swap)  10.6 us
    all_gather x1, blocking collectives, body(): sketch = lax.all_gather(sketch_own, 'x', axis=1, tiled=True)  10.2 us
    all_to_all x1, starting transfers between devices, body(): got = lax.all_to_all(partial_rows.reshape(n_z, -1, SHARE), ring, 0, 0)  9.82 us
  transfers between devices with their start and end apart: 16, of which 13 were waited for; matrix products, arithmetic and copies ran while one was open for 2% of the time, Pallas kernels for 0%

profile of v6, /device:TPU:1, one launch (start us, length us, event | category | flops | bytes accessed | tf_op | source)
XLA Modules:
  0.0 219.8 jit_solution(14047683845282679994)
XLA Ops:
  0.6 3.8 %shard_map.104.own_ref = f32[2048,256]{1,0:T(8,128)S(1)} custom-call(s32[1,2048]{1,0:T(1,128)} %bitcast.82, f32[2048,256]{1,0:T(8,128)} %rows_ref.1, bf16[256,256]{1,0:T(8,128)(2,1)} %constant.101.clone.fine_ref), custom_call_target="tpu_custom_call" | custom-call | tf_op jit(solution)/shard_map/pallas_call | solution.py:81
  4.5 8.8 %collective-permute-start = (f32[2048,256]{1,0:T(8,128)S(1)}, f32[2048,256]{1,0:T(8,128)}, u32[]{:S(2)}, u32[]{:S(2)}) collective-permute-start(f32[2048,256]{1,0:T(8,128)S(1)} %shard_map.104.own_ref), channel_id=1, source_target_pairs={{0,4},{4,0},{1,5},{5,1},{2,6},{6,2},{3,7},{7,3},{8,12},{12,8},{9,1... | collective-permute-start | bytes 6291464 | tf_op jit(solution)/shard_map/ppermute | solution.py:175
  13.3 0.7 fusion.19
  14.0 0.7 fusion.18
  14.8 0.1 reshape.49
  15.1 2.1 collective-permute-done.other_ref
  17.2 5.2 %shard_map.105 = f32[4096,128]{1,0:T(8,128)} custom-call(f32[1]{0:T(128)} %bitcast.sign_ref, f32[64]{0:T(128)S(1)} %mul.68.to_ref, s32[2048]{0:T(1024)S(1)} %reshape.50.rows_ref, f32[2048,256]{1,0:T(8,128)S(1)} %shard_map.104.own_ref, f32[2048,256]{1,0:T(8,128)} %collective-permute-done.other_ref), custom_call_target="tpu_custom_call" | custom-call | tf_op jit(solution)/shard_map/pallas_call | solution.py:130
  22.4 3.8 %all-to-all-start = ((f32[4,1024,128]{2,1,0:T(8,128)}), f32[4,1024,128]{2,1,0:T(8,128)S(1)}, u32[]{:S(2)}, u32[]{:S(2)}) async-start(f32[4,1024,128]{2,1,0:T(8,128)} %bitcast.61), calls=%async_computation | async-start | bytes 4194304 | tf_op jit(solution)/shard_map/all_to_all | solution.py:183
  26.3 1.9 collective-permute-start.1
  28.2 21.2 %all_gather.9 = f32[128,352]{1,0:T(8,128)S(1)} all-gather(f32[32,352]{1,0:T(8,128)S(1)} %copy-done.2), channel_id=1, replica_groups=mesh['far'=4,'near'=4,'y'=4,'core'=2,'x'=4] {'far'}, dimensions={0}, use_global_device_ids=true | all-gather | bytes 225280 | tf_op jit(solution)/shard_map/all_gather | solution.py:186
  49.4 2.8 %all-to-all-done = f32[4,1024,128]{2,1,0:T(8,128)S(1)} async-done(((f32[4,1024,128]{2,1,0:T(8,128)}), f32[4,1024,128]{2,1,0:T(8,128)S(1)}, u32[]{:S(2)}, u32[]{:S(2)}) %all-to-all-start) | async-done | bytes 2097184 | tf_op jit(solution)/shard_map/all_to_all | solution.py:183
  52.2 0.9 reduce_sum.36
  53.2 9.8 %all-to-all-start.1 = ((f32[16,64,128]{2,1,0:T(8,128)}), f32[16,64,128]{2,1,0:T(8,128)S(1)}, u32[]{:S(2)}, u32[]{:S(2)}) async-start(f32[16,64,128]{2,1,0:T(8,128)} %bitcast.7), calls=%async_computation.1 | async-start | bytes 1048576 | tf_op jit(solution)/shard_map/all_to_all | solution.py:189
  63.0 4.4 %collective-permute-start.3 = (f32[352,256]{1,0:T(8,128)S(1)}, f32[352,256]{1,0:T(8,128)S(1)}, u32[]{:S(2)}, u32[]{:S(2)}) collective-permute-start(f32[352,256]{1,0:T(8,128)S(1)} %convert_multiply_fusion), channel_id=1, source_target_pairs={{0,3},{1,0},{2,1},{3,2},{4,7},{5,4},{6,5},{7,6},{8,11},{9,8},{10,9... | collective-permute-start | bytes 1081352 | tf_op jit(solution)/shard_map/ppermute | solution.py:172
  67.4 1.9 collective-permute-start.2
  69.4 0.1 copy.23
  69.5 3.7 %collective-permute-done.3 = f32[352,256]{1,0:T(8,128)S(1)} collective-permute-done((f32[352,256]{1,0:T(8,128)S(1)}, f32[352,256]{1,0:T(8,128)S(1)}, u32[]{:S(2)}, u32[]{:S(2)}) %collective-permute-start.3) | collective-permute-done | bytes 360480 | tf_op jit(solution)/shard_map/ppermute | solution.py:172
  73.3 5.0 %collective-permute-done.2 = f32[352,256]{1,0:T(8,128)S(1)} collective-permute-done((f32[352,256]{1,0:T(8,128)S(1)}, f32[352,256]{1,0:T(8,128)S(1)}, u32[]{:S(2)}, u32[]{:S(2)}) %collective-permute-start.2) | collective-permute-done | bytes 360480 | tf_op jit(solution)/shard_map/ppermute | solution.py:172
  78.3 0.1 pad_maximum_fusion
  78.4 0.1 dynamic-slice_bitcast_fusion.3
  78.6 1.3 fusion.20
  79.9 0.2 pad_maximum_fusion.1
  80.1 0.7 fusion.25
  80.8 4.8 %all-to-all-done.1 = f32[16,64,128]{2,1,0:T(8,128)S(1)} async-done(((f32[16,64,128]{2,1,0:T(8,128)}), f32[16,64,128]{2,1,0:T(8,128)S(1)}, u32[]{:S(2)}, u32[]{:S(2)}) %all-to-all-start.1) | async-done | bytes 524320 | tf_op jit(solution)/shard_map/all_to_all | solution.py:189
  85.6 21.1 %all_gather.10 = f32[128,256]{1,0:T(8,128)S(1)} all-gather(f32[32,256]{1,0:T(8,128)S(1)} %div.22), channel_id=1, replica_groups=mesh['far'=4,'near'=4,'y'=4,'core'=2,'x'=4] {'far'}, dimensions={0}, use_global_device_ids=true | all-gather | bytes 163840 | tf_op jit(solution)/shard_map/all_gather | solution.py:198
  106.7 10.2 %all_gather.11 = f32[128,1024]{1,0:T(8,128)S(1)} all-gather(f32[128,256]{1,0:T(8,128)S(1)} %all_gather.10), channel_id=1, replica_groups=mesh['far'=4,'near'=4,'y'=4,'core'=2,'x'=4] {'x'}, dimensions={1}, use_global_device_ids=true | all-gather | bytes 655360 | tf_op jit(solution)/shard_map/all_gather | solution.py:199
  116.9 0.7 fusion.26
  117.7 0.1 sqrt_multiply_fusion
  117.8 0.3 fusion.27
  118.1 0.4 fusion.6
  118.5 0.3 fusion.28
  118.9 8.3 %collective-permute-start.4 = (f32[352,256]{1,0:T(8,128)S(1)}, f32[352,256]{1,0:T(8,128)S(1)}, u32[]{:S(2)}, u32[]{:S(2)}) collective-permute-start(f32[352,256]{1,0:T(8,128)S(1)} %pad_maximum_fusion.3), channel_id=1, source_target_pairs={{0,4},{4,0},{1,5},{5,1},{2,6},{6,2},{3,7},{7,3},{8,12},{12,8},{9,1... | collective-permute-start | bytes 1081352 | tf_op jit(solution)/shard_map/ppermute | solution.py:213
  127.2 1.3 collective-permute-done.4
  128.6 9.9 %all_to_all.30 = f32[4,88,256]{2,1,0:T(8,128)S(1)} all-to-all(f32[4,88,256]{2,1,0:T(8,128)S(1)} %bitcast.65), channel_id=1, replica_groups=mesh['far'=4,'near'=4,'y'=4,'core'=2,'x'=4] {'y'}, dimensions={0} | all-to-all | bytes 720896 | tf_op jit(solution)/shard_map/all_to_all | solution.py:214
  138.4 4.1 %collective-permute-start.5 = (f32[88,256]{1,0:T(8,128)S(1)}, f32[88,256]{1,0:T(8,128)S(1)}, u32[]{:S(2)}, u32[]{:S(2)}) collective-permute-start(f32[88,256]{1,0:T(8,128)S(1)} %reduce_sum.38), channel_id=1, source_target_pairs={{0,32},{32,64},{64,96},{96,0},{1,33},{33,65},{65,97},{97,1},{2,34}... | collective-permute-start | bytes 270344 | tf_op jit(solution)/shard_map/ppermute | solution.py:215
  142.6 3.6 %collective-permute-start.6 = (f32[88,256]{1,0:T(8,128)S(1)}, f32[88,256]{1,0:T(8,128)S(1)}, u32[]{:S(2)}, u32[]{:S(2)}) collective-permute-start(f32[88,256]{1,0:T(8,128)S(1)} %reduce_sum.38), channel_id=1, source_target_pairs={{0,64},{32,96},{64,0},{96,32},{1,65},{33,97},{65,1},{97,33},{2,66}... | collective-permute-start | bytes 270344 | tf_op jit(solution)/shard_map/ppermute | solution.py:215
  146.2 3.1 %collective-permute-start.7 = (f32[88,256]{1,0:T(8,128)S(1)}, f32[88,256]{1,0:T(8,128)S(1)}, u32[]{:S(2)}, u32[]{:S(2)}) collective-permute-start(f32[88,256]{1,0:T(8,128)S(1)} %reduce_sum.38), channel_id=1, source_target_pairs={{0,96},{32,0},{64,32},{96,64},{1,97},{33,1},{65,33},{97,65},{2,98}... | collective-permute-start | bytes 270344 | tf_op jit(solution)/shard_map/ppermute | solution.py:215
  149.3 0.4 collective-permute-done.6
  149.7 2.2 collective-permute-done.7
  152.0 15.0 %all_to_all.31 = f32[16,88,128]{2,1,0:T(8,128)S(1)} all-to-all(f32[16,88,128]{2,1,0:T(8,128)S(1)} %broadcast_in_dim.4), channel_id=1, replica_groups=mesh['far'=4,'near'=4,'y'=4,'core'=2,'x'=4] {'y','x'}, dimensions={0} | all-to-all | bytes 1441792 | tf_op jit(solution)/shard_map/all_to_all | solution.py:154
  167.0 5.6 %collective-permute-start.8 = (f32[4,4,88,128]{3,2,1,0:T(8,128)S(1)}, f32[4,4,88,128]{3,2,1,0:T(8,128)S(1)}, u32[]{:S(2)}, u32[]{:S(2)}) collective-permute-start(f32[4,4,88,128]{3,2,1,0:T(8,128)S(1)} %bitcast.62), channel_id=1, source_target_pairs={{0,4},{4,0},{1,5},{5,1},{2,6},{6,2},{3,7},{7,3},{8,12},{12,8},{9,1... | collective-permute-start | bytes 2162696 | tf_op jit(solution)/shard_map/ppermute | solution.py:223
  172.7 1.6 collective-permute-done.8
  174.4 0.8 fusion.22
  175.2 1.3 fusion.21
  176.6 0.2 pad_maximum_fusion.2
  176.7 0.7 fusion.3
  177.5 0.3 fusion.29
  177.8 0.4 fusion.4
  178.1 0.3 fusion.30
  178.5 2.3 %collective-permute-start.9 = (f32[352,256]{1,0:T(8,128)S(1)}, f32[352,256]{1,0:T(8,128)S(1)}, u32[]{:S(2)}, u32[]{:S(2)}) collective-permute-start(f32[352,256]{1,0:T(8,128)S(1)} %pad_maximum_fusion.4), channel_id=1, source_target_pairs={{0,4},{4,0},{1,5},{5,1},{2,6},{6,2},{3,7},{7,3},{8,12},{12,8},{9,1... | collective-permute-start | bytes 1081352 | tf_op jit(solution)/shard_map/ppermute | solution.py:213
  180.8 1.3 collective-permute-done.9
  182.1 9.9 %all_to_all.32 = f32[4,88,256]{2,1,0:T(8,128)S(1)} all-to-all(f32[4,88,256]{2,1,0:T(8,128)S(1)} %bitcast.66), channel_id=1, replica_groups=mesh['far'=4,'near'=4,'y'=4,'core'=2,'x'=4] {'y'}, dimensions={0} | all-to-all | bytes 720896 | tf_op jit(solution)/shard_map/all_to_all | solution.py:214
  192.0 3.6 %collective-permute-start.10 = (f32[88,256]{1,0:T(8,128)S(1)}, f32[88,256]{1,0:T(8,128)S(1)}, u32[]{:S(2)}, u32[]{:S(2)}) collective-permute-start(f32[88,256]{1,0:T(8,128)S(1)} %reduce_sum.39), channel_id=1, source_target_pairs={{0,32},{32,64},{64,96},{96,0},{1,33},{33,65},{65,97},{97,1},{2,34}... | collective-permute-start | bytes 270344 | tf_op jit(solution)/shard_map/ppermute | solution.py:215
  195.7 3.0 %collective-permute-start.11 = (f32[88,256]{1,0:T(8,128)S(1)}, f32[88,256]{1,0:T(8,128)S(1)}, u32[]{:S(2)}, u32[]{:S(2)}) collective-permute-start(f32[88,256]{1,0:T(8,128)S(1)} %reduce_sum.39), channel_id=1, source_target_pairs={{0,64},{32,96},{64,0},{96,32},{1,65},{33,97},{65,1},{97,33},{2,66}... | collective-permute-start | bytes 270344 | tf_op jit(solution)/shard_map/ppermute | solution.py:215
  198.7 2.9 %collective-permute-start.12 = (f32[88,256]{1,0:T(8,128)S(1)}, f32[88,256]{1,0:T(8,128)S(1)}, u32[]{:S(2)}, u32[]{:S(2)}) collective-permute-start(f32[88,256]{1,0:T(8,128)S(1)} %reduce_sum.39), channel_id=1, source_target_pairs={{0,96},{32,0},{64,32},{96,64},{1,97},{33,1},{65,33},{97,65},{2,98}... | collective-permute-start | bytes 270344 | tf_op jit(solution)/shard_map/ppermute | solution.py:215
  201.6 2.6 %collective-permute-done.11 = f32[88,256]{1,0:T(8,128)S(1)} collective-permute-done((f32[88,256]{1,0:T(8,128)S(1)}, f32[88,256]{1,0:T(8,128)S(1)}, u32[]{:S(2)}, u32[]{:S(2)}) %collective-permute-start.11) | collective-permute-done | bytes 90144 | tf_op jit(solution)/shard_map/ppermute | solution.py:215
  204.2 1.3 collective-permute-done.12
  205.6 0.8 broadcast_in_dim.5
  206.3 4.8 %all-to-all-start.5 = ((f32[8,88,128]{2,1,0:T(8,128)}), f32[8,88,128]{2,1,0:T(8,128)S(1)}, u32[]{:S(2)}, u32[]{:S(2)}) async-start(f32[8,88,128]{2,1,0:T(8,128)} %broadcast_in_dim.5), calls=%async_computation.5 | async-start | bytes 720896 | tf_op jit(solution)/shard_map/all_to_all | solution.py:154
  211.1 0.1 constant_dynamic-slice_fusion.4
  211.2 0.7 copy.25
  212.0 6.9 %all-to-all-done.5 = f32[8,88,128]{2,1,0:T(8,128)S(1)} async-done(((f32[8,88,128]{2,1,0:T(8,128)}), f32[8,88,128]{2,1,0:T(8,128)S(1)}, u32[]{:S(2)}, u32[]{:S(2)}) %all-to-all-start.5) | async-done | bytes 360480 | tf_op jit(solution)/shard_map/all_to_all | solution.py:154
  218.9 0.2 copy.24
  219.0 0.8 copy.29
  (40 shorter events, 1.2 us)
Async XLA Ops:
  0.6 14.2 %copy-start.3 = (s32[4096]{0:T(1024)S(1)}, s32[4096]{0:T(1024)}, u32[]{:S(2)}) copy-start(s32[4096]{0:T(1024)} %param.11) | copy-start | bytes 49156
  4.5 12.7 %collective-permute-start = (f32[2048,256]{1,0:T(8,128)S(1)}, f32[2048,256]{1,0:T(8,128)}, u32[]{:S(2)}, u32[]{:S(2)}) collective-permute-start(f32[2048,256]{1,0:T(8,128)S(1)} %shard_map.104.own_ref), channel_id=1, source_target_pairs={{0,4},{4,0},{1,5},{5,1},{2,6},{6,2},{3,7},{7,3},{8,12},{12,8},{9,1... | collective-permute-start | bytes 6291464 | tf_op jit(solution)/shard_map/ppermute | solution.py:175
  22.4 3.8 %copy-start = (f32[352,256]{1,0:T(8,128)S(1)}, f32[352,256]{1,0:T(8,128)}, u32[]{:S(2)}) copy-start(f32[352,256]{1,0:T(8,128)} %param.14) | copy-start | bytes 1081348
  22.4 3.8 %copy-start.1 = (s32[352,256]{1,0:T(8,128)S(1)}, s32[352,256]{1,0:T(8,128)}, u32[]{:S(2)}) copy-start(s32[352,256]{1,0:T(8,128)} %param.12) | copy-start | bytes 1081348
  22.4 5.8 %copy-start.2 = (f32[32,352]{1,0:T(8,128)S(1)}, f32[32,352]{1,0:T(8,128)}, u32[]{:S(2)}) copy-start(f32[32,352]{1,0:T(8,128)} %param.13) | copy-start | bytes 135172
  22.4 29.8 %all-to-all-start = ((f32[4,1024,128]{2,1,0:T(8,128)}), f32[4,1024,128]{2,1,0:T(8,128)S(1)}, u32[]{:S(2)}, u32[]{:S(2)}) async-start(f32[4,1024,128]{2,1,0:T(8,128)} %bitcast.61), calls=%async_computation | async-start | bytes 4194304 | tf_op jit(solution)/shard_map/all_to_all | solution.py:183
  26.3 23.2 %collective-permute-start.1 = (f32[352,256]{1,0:T(8,128)S(1)}, f32[352,256]{1,0:T(8,128)S(1)}, u32[]{:S(2)}, u32[]{:S(2)}) collective-permute-start(f32[352,256]{1,0:T(8,128)S(1)} %convert_multiply_fusion), channel_id=1, source_target_pairs={{0,2},{1,3},{2,0},{3,1},{4,6},{5,7},{6,4},{7,5},{8,10},{9,11},{10,... | collective-permute-start | bytes 1081352 | tf_op jit(solution)/shard_map/ppermute | solution.py:172
  53.2 32.4 %all-to-all-start.1 = ((f32[16,64,128]{2,1,0:T(8,128)}), f32[16,64,128]{2,1,0:T(8,128)S(1)}, u32[]{:S(2)}, u32[]{:S(2)}) async-start(f32[16,64,128]{2,1,0:T(8,128)} %bitcast.7), calls=%async_computation.1 | async-start | bytes 1048576 | tf_op jit(solution)/shard_map/all_to_all | solution.py:189
  63.0 10.3 %collective-permute-start.3 = (f32[352,256]{1,0:T(8,128)S(1)}, f32[352,256]{1,0:T(8,128)S(1)}, u32[]{:S(2)}, u32[]{:S(2)}) collective-permute-start(f32[352,256]{1,0:T(8,128)S(1)} %convert_multiply_fusion), channel_id=1, source_target_pairs={{0,3},{1,0},{2,1},{3,2},{4,7},{5,4},{6,5},{7,6},{8,11},{9,8},{10,9... | collective-permute-start | bytes 1081352 | tf_op jit(solution)/shard_map/ppermute | solution.py:172
  67.4 10.9 %collective-permute-start.2 = (f32[352,256]{1,0:T(8,128)S(1)}, f32[352,256]{1,0:T(8,128)S(1)}, u32[]{:S(2)}, u32[]{:S(2)}) collective-permute-start(f32[352,256]{1,0:T(8,128)S(1)} %convert_multiply_fusion), channel_id=1, source_target_pairs={{0,1},{1,2},{2,3},{3,0},{4,5},{5,6},{6,7},{7,4},{8,9},{9,10},{10,1... | collective-permute-start | bytes 1081352 | tf_op jit(solution)/shard_map/ppermute | solution.py:172
  118.9 9.6 %collective-permute-start.4 = (f32[352,256]{1,0:T(8,128)S(1)}, f32[352,256]{1,0:T(8,128)S(1)}, u32[]{:S(2)}, u32[]{:S(2)}) collective-permute-start(f32[352,256]{1,0:T(8,128)S(1)} %pad_maximum_fusion.3), channel_id=1, source_target_pairs={{0,4},{4,0},{1,5},{5,1},{2,6},{6,2},{3,7},{7,3},{8,12},{12,8},{9,1... | collective-permute-start | bytes 1081352 | tf_op jit(solution)/shard_map/ppermute | solution.py:213
  138.4 10.9 %collective-permute-start.5 = (f32[88,256]{1,0:T(8,128)S(1)}, f32[88,256]{1,0:T(8,128)S(1)}, u32[]{:S(2)}, u32[]{:S(2)}) collective-permute-start(f32[88,256]{1,0:T(8,128)S(1)} %reduce_sum.38), channel_id=1, source_target_pairs={{0,32},{32,64},{64,96},{96,0},{1,33},{33,65},{65,97},{97,1},{2,34}... | collective-permute-start | bytes 270344 | tf_op jit(solution)/shard_map/ppermute | solution.py:215
  142.6 7.1 %collective-permute-start.6 = (f32[88,256]{1,0:T(8,128)S(1)}, f32[88,256]{1,0:T(8,128)S(1)}, u32[]{:S(2)}, u32[]{:S(2)}) collective-permute-start(f32[88,256]{1,0:T(8,128)S(1)} %reduce_sum.38), channel_id=1, source_target_pairs={{0,64},{32,96},{64,0},{96,32},{1,65},{33,97},{65,1},{97,33},{2,66}... | collective-permute-start | bytes 270344 | tf_op jit(solution)/shard_map/ppermute | solution.py:215
  146.2 5.7 %collective-permute-start.7 = (f32[88,256]{1,0:T(8,128)S(1)}, f32[88,256]{1,0:T(8,128)S(1)}, u32[]{:S(2)}, u32[]{:S(2)}) collective-permute-start(f32[88,256]{1,0:T(8,128)S(1)} %reduce_sum.38), channel_id=1, source_target_pairs={{0,96},{32,0},{64,32},{96,64},{1,97},{33,1},{65,33},{97,65},{2,98}... | collective-permute-start | bytes 270344 | tf_op jit(solution)/shard_map/ppermute | solution.py:215
  167.0 7.2 %collective-permute-start.8 = (f32[4,4,88,128]{3,2,1,0:T(8,128)S(1)}, f32[4,4,88,128]{3,2,1,0:T(8,128)S(1)}, u32[]{:S(2)}, u32[]{:S(2)}) collective-permute-start(f32[4,4,88,128]{3,2,1,0:T(8,128)S(1)} %bitcast.62), channel_id=1, source_target_pairs={{0,4},{4,0},{1,5},{5,1},{2,6},{6,2},{3,7},{7,3},{8,12},{12,8},{9,1... | collective-permute-start | bytes 2162696 | tf_op jit(solution)/shard_map/ppermute | solution.py:223
  178.5 3.6 %collective-permute-start.9 = (f32[352,256]{1,0:T(8,128)S(1)}, f32[352,256]{1,0:T(8,128)S(1)}, u32[]{:S(2)}, u32[]{:S(2)}) collective-permute-start(f32[352,256]{1,0:T(8,128)S(1)} %pad_maximum_fusion.4), channel_id=1, source_target_pairs={{0,4},{4,0},{1,5},{5,1},{2,6},{6,2},{3,7},{7,3},{8,12},{12,8},{9,1... | collective-permute-start | bytes 1081352 | tf_op jit(solution)/shard_map/ppermute | solution.py:213
  192.0 9.6 %collective-permute-start.10 = (f32[88,256]{1,0:T(8,128)S(1)}, f32[88,256]{1,0:T(8,128)S(1)}, u32[]{:S(2)}, u32[]{:S(2)}) collective-permute-start(f32[88,256]{1,0:T(8,128)S(1)} %reduce_sum.39), channel_id=1, source_target_pairs={{0,32},{32,64},{64,96},{96,0},{1,33},{33,65},{65,97},{97,1},{2,34}... | collective-permute-start | bytes 270344 | tf_op jit(solution)/shard_map/ppermute | solution.py:215
  195.7 8.5 %collective-permute-start.11 = (f32[88,256]{1,0:T(8,128)S(1)}, f32[88,256]{1,0:T(8,128)S(1)}, u32[]{:S(2)}, u32[]{:S(2)}) collective-permute-start(f32[88,256]{1,0:T(8,128)S(1)} %reduce_sum.39), channel_id=1, source_target_pairs={{0,64},{32,96},{64,0},{96,32},{1,65},{33,97},{65,1},{97,33},{2,66}... | collective-permute-start | bytes 270344 | tf_op jit(solution)/shard_map/ppermute | solution.py:215
  198.7 6.8 %collective-permute-start.12 = (f32[88,256]{1,0:T(8,128)S(1)}, f32[88,256]{1,0:T(8,128)S(1)}, u32[]{:S(2)}, u32[]{:S(2)}) collective-permute-start(f32[88,256]{1,0:T(8,128)S(1)} %reduce_sum.39), channel_id=1, source_target_pairs={{0,96},{32,0},{64,32},{96,64},{1,97},{33,1},{65,33},{97,65},{2,98}... | collective-permute-start | bytes 270344 | tf_op jit(solution)/shard_map/ppermute | solution.py:215
  206.3 12.5 %all-to-all-start.5 = ((f32[8,88,128]{2,1,0:T(8,128)}), f32[8,88,128]{2,1,0:T(8,128)S(1)}, u32[]{:S(2)}, u32[]{:S(2)}) async-start(f32[8,88,128]{2,1,0:T(8,128)} %broadcast_in_dim.5), calls=%async_computation.5 | async-start | bytes 720896 | tf_op jit(solution)/shard_map/all_to_all | solution.py:154

commit v7 on v5

--- a/solution.py
+++ b/solution.py
@@ -212,7 +212,7 @@
 
         both = half(mine) + lax.ppermute(half(theirs), "core", swap)
         both = jnp.sum(lax.all_to_all(both.reshape(n_y, k // n_y, 2 * SHARE), "y", 0, 0), axis=0)
-        both = both + sum(lax.ppermute(both, "near", shift("near", by)) for by in range(1, n_near))
+        both = jnp.sum(everywhere(both, "near", n_near), axis=0)
         piece = lax.dynamic_slice(templates, (at_y * (k // n_y), at_x * bins + mine), (k // n_y, SHARE))
         piece = piece * ratio(both[:, :SHARE], both[:, SHARE:])
         if round_index == ITERS - 1:

time: 221 us -> 223 us (level)
  starting transfers between devices: 72 us -> 58 us
  blocking collectives: 87.3 us -> 99.6 us
  waiting for transfers between devices: 35.9 us -> 38.7 us
    ppermute x6 -> x0, starting transfers between devices: 20.4 us -> none  [body(): lax.ppermute(both, 'near', shift('near', by))]
    all_to_all x1 -> x2, blocking collectives: 15 us -> 27.3 us  [everywhere(): lax.all_to_all(jnp.broadcast_to(value[None], (count, *value.shape)), axes...]
    all_to_all x1 -> x2, waiting for transfers between devices: 6.9 us -> 16.1 us  [everywhere(): lax.all_to_all(jnp.broadcast_to(value[None], (count, *value.shape)), axes...]
    ppermute x6 -> x0, waiting for transfers between devices: 6.47 us -> none  [body(): lax.ppermute(both, 'near', shift('near', by))]
    all_to_all x1 -> x2, starting transfers between devices: 4.78 us -> 10.8 us  [everywhere(): lax.all_to_all(jnp.broadcast_to(value[None], (count, *value.shape)), axes...]
  transfers between devices with their start and end apart: 16 -> 11, of which waited for: 13 -> 10; matrix products, arithmetic and copies ran while one was open for 2% -> 2% of each run, Pallas kernels for 0% -> 0%
where the time goes in v7:
time: 223 us; the launch traced here: 222 us
  blocking collectives  99.6 us (45%)
  starting transfers between devices  58 us (26%)
  waiting for transfers between devices  38.7 us (17%)
  Pallas kernels  9.13 us (4%)
  matrix products  7.4 us (3%)
  local copies, waits for them, and re-layouts  5.58 us (3%)
    all_to_all x2, blocking collectives, everywhere(): lax.all_to_all(jnp.broadcast_to(value[None], (count, *value.shape)), axes...  27.3 us
    all_gather x1, blocking collectives, body(): activations = lax.all_gather(w_init, 'far', tiled=True)  21.2 us
    all_gather x1, blocking collectives, body(): sketch_own = lax.all_gather(sketch, 'far', tiled=True)  21.1 us
    all_to_all x2, blocking collectives, body(): lax.all_to_all(both.reshape(n_y, k // n_y, 2 * SHARE), 'y', 0, 0)  19.7 us
    all_to_all x2, waiting for transfers between devices, everywhere(): lax.all_to_all(jnp.broadcast_to(value[None], (count, *value.shape)), axes...  16.1 us
    all_to_all x2, starting transfers between devices, everywhere(): lax.all_to_all(jnp.broadcast_to(value[None], (count, *value.shape)), axes...  10.8 us
    ppermute x2, starting transfers between devices, body(): both = half(mine) + lax.ppermute(half(theirs), 'core', swap)  10.6 us
    all_gather x1, blocking collectives, body(): sketch = lax.all_gather(sketch_own, 'x', axis=1, tiled=True)  10.2 us
  transfers between devices with their start and end apart: 11, of which 10 were waited for; matrix products, arithmetic and copies ran while one was open for 2% of the time, Pallas kernels for 0%

profile of v7, /device:TPU:1, one launch (start us, length us, event | category | flops | bytes accessed | tf_op | source)
XLA Modules:
  0.0 221.7 jit_solution(10334212971507140380)
XLA Ops:
  0.6 3.8 %shard_map.104.own_ref = f32[2048,256]{1,0:T(8,128)S(1)} custom-call(s32[1,2048]{1,0:T(1,128)} %bitcast.82, f32[2048,256]{1,0:T(8,128)} %rows_ref.1, bf16[256,256]{1,0:T(8,128)(2,1)} %constant.101.clone.fine_ref), custom_call_target="tpu_custom_call" | custom-call | tf_op jit(solution)/shard_map/pallas_call | solution.py:81
  4.5 8.8 %collective-permute-start = (f32[2048,256]{1,0:T(8,128)S(1)}, f32[2048,256]{1,0:T(8,128)}, u32[]{:S(2)}, u32[]{:S(2)}) collective-permute-start(f32[2048,256]{1,0:T(8,128)S(1)} %shard_map.104.own_ref), channel_id=1, source_target_pairs={{0,4},{4,0},{1,5},{5,1},{2,6},{6,2},{3,7},{7,3},{8,12},{12,8},{9,1... | collective-permute-start | bytes 6291464 | tf_op jit(solution)/shard_map/ppermute | solution.py:175
  13.3 0.7 fusion.19
  14.0 0.7 fusion.18
  14.7 0.1 broadcast_multiply_fusion.1
  14.8 0.1 mul.68.to_ref
  14.8 0.1 reshape.51
  15.0 0.1 reshape.52.rows_ref
  15.1 2.1 collective-permute-done.other_ref
  17.2 5.3 %shard_map.105 = f32[4096,128]{1,0:T(8,128)} custom-call(f32[1]{0:T(128)} %bitcast.sign_ref, f32[64]{0:T(128)S(1)} %mul.68.to_ref, s32[2048]{0:T(1024)S(1)} %reshape.52.rows_ref, f32[2048,256]{1,0:T(8,128)S(1)} %shard_map.104.own_ref, f32[2048,256]{1,0:T(8,128)} %collective-permute-done.other_ref), custom_call_target="tpu_custom_call" | custom-call | tf_op jit(solution)/shard_map/pallas_call | solution.py:130
  22.5 0.0 copy-start.1
  22.5 3.8 %all-to-all-start = ((f32[4,1024,128]{2,1,0:T(8,128)}), f32[4,1024,128]{2,1,0:T(8,128)S(1)}, u32[]{:S(2)}, u32[]{:S(2)}) async-start(f32[4,1024,128]{2,1,0:T(8,128)} %bitcast.61), calls=%async_computation | async-start | bytes 4194304 | tf_op jit(solution)/shard_map/all_to_all | solution.py:183
  26.3 1.9 collective-permute-start.1
  28.3 21.2 %all_gather.9 = f32[128,352]{1,0:T(8,128)S(1)} all-gather(f32[32,352]{1,0:T(8,128)S(1)} %copy-done.2), channel_id=1, replica_groups=mesh['far'=4,'near'=4,'y'=4,'core'=2,'x'=4] {'far'}, dimensions={0}, use_global_device_ids=true | all-gather | bytes 225280 | tf_op jit(solution)/shard_map/all_gather | solution.py:186
  49.5 2.8 %all-to-all-done = f32[4,1024,128]{2,1,0:T(8,128)S(1)} async-done(((f32[4,1024,128]{2,1,0:T(8,128)}), f32[4,1024,128]{2,1,0:T(8,128)S(1)}, u32[]{:S(2)}, u32[]{:S(2)}) %all-to-all-start) | async-done | bytes 2097184 | tf_op jit(solution)/shard_map/all_to_all | solution.py:183
  52.3 0.9 reduce_sum.54
  53.3 9.8 %all-to-all-start.1 = ((f32[16,64,128]{2,1,0:T(8,128)}), f32[16,64,128]{2,1,0:T(8,128)S(1)}, u32[]{:S(2)}, u32[]{:S(2)}) async-start(f32[16,64,128]{2,1,0:T(8,128)} %bitcast.7), calls=%async_computation.1 | async-start | bytes 1048576 | tf_op jit(solution)/shard_map/all_to_all | solution.py:189
  63.1 4.4 %collective-permute-start.3 = (f32[352,256]{1,0:T(8,128)S(1)}, f32[352,256]{1,0:T(8,128)S(1)}, u32[]{:S(2)}, u32[]{:S(2)}) collective-permute-start(f32[352,256]{1,0:T(8,128)S(1)} %convert_multiply_fusion), channel_id=1, source_target_pairs={{0,3},{1,0},{2,1},{3,2},{4,7},{5,4},{6,5},{7,6},{8,11},{9,8},{10,9... | collective-permute-start | bytes 1081352 | tf_op jit(solution)/shard_map/ppermute | solution.py:172
  67.5 1.9 collective-permute-start.2
  69.5 0.1 copy.27
  69.6 3.7 %collective-permute-done.3 = f32[352,256]{1,0:T(8,128)S(1)} collective-permute-done((f32[352,256]{1,0:T(8,128)S(1)}, f32[352,256]{1,0:T(8,128)S(1)}, u32[]{:S(2)}, u32[]{:S(2)}) %collective-permute-start.3) | collective-permute-done | bytes 360480 | tf_op jit(solution)/shard_map/ppermute | solution.py:172
  73.4 5.0 %collective-permute-done.2 = f32[352,256]{1,0:T(8,128)S(1)} collective-permute-done((f32[352,256]{1,0:T(8,128)S(1)}, f32[352,256]{1,0:T(8,128)S(1)}, u32[]{:S(2)}, u32[]{:S(2)}) %collective-permute-start.2) | collective-permute-done | bytes 360480 | tf_op jit(solution)/shard_map/ppermute | solution.py:172
  78.4 0.1 pad_maximum_fusion
  78.5 0.1 dynamic-slice_bitcast_fusion.3
  78.7 1.3 fusion.20
  80.0 0.2 pad_maximum_fusion.1
  80.2 0.7 fusion.25
  80.9 4.8 %all-to-all-done.1 = f32[16,64,128]{2,1,0:T(8,128)S(1)} async-done(((f32[16,64,128]{2,1,0:T(8,128)}), f32[16,64,128]{2,1,0:T(8,128)S(1)}, u32[]{:S(2)}, u32[]{:S(2)}) %all-to-all-start.1) | async-done | bytes 524320 | tf_op jit(solution)/shard_map/all_to_all | solution.py:189
  85.7 21.1 %all_gather.10 = f32[128,256]{1,0:T(8,128)S(1)} all-gather(f32[32,256]{1,0:T(8,128)S(1)} %div.22), channel_id=1, replica_groups=mesh['far'=4,'near'=4,'y'=4,'core'=2,'x'=4] {'far'}, dimensions={0}, use_global_device_ids=true | all-gather | bytes 163840 | tf_op jit(solution)/shard_map/all_gather | solution.py:198
  106.8 10.2 %all_gather.11 = f32[128,1024]{1,0:T(8,128)S(1)} all-gather(f32[128,256]{1,0:T(8,128)S(1)} %all_gather.10), channel_id=1, replica_groups=mesh['far'=4,'near'=4,'y'=4,'core'=2,'x'=4] {'x'}, dimensions={1}, use_global_device_ids=true | all-gather | bytes 655360 | tf_op jit(solution)/shard_map/all_gather | solution.py:199
  117.0 0.7 fusion.26
  117.8 0.1 sqrt_multiply_fusion
  117.9 0.3 fusion.27
  118.2 0.4 fusion.6
  118.5 0.3 fusion.28
  119.0 8.3 %collective-permute-start.4 = (f32[352,256]{1,0:T(8,128)S(1)}, f32[352,256]{1,0:T(8,128)S(1)}, u32[]{:S(2)}, u32[]{:S(2)}) collective-permute-start(f32[352,256]{1,0:T(8,128)S(1)} %pad_maximum_fusion.3), channel_id=1, source_target_pairs={{0,4},{4,0},{1,5},{5,1},{2,6},{6,2},{3,7},{7,3},{8,12},{12,8},{9,1... | collective-permute-start | bytes 1081352 | tf_op jit(solution)/shard_map/ppermute | solution.py:213
  127.3 1.3 collective-permute-done.4
  128.6 0.1 maximum_add_fusion
  128.6 9.9 %all_to_all.40 = f32[4,88,256]{2,1,0:T(8,128)S(1)} all-to-all(f32[4,88,256]{2,1,0:T(8,128)S(1)} %bitcast.65), channel_id=1, replica_groups=mesh['far'=4,'near'=4,'y'=4,'core'=2,'x'=4] {'y'}, dimensions={0} | all-to-all | bytes 720896 | tf_op jit(solution)/shard_map/all_to_all | solution.py:214
  138.5 0.8 broadcast_in_dim.8
  139.3 4.9 %all-to-all-start.3 = ((f32[4,88,256]{2,1,0:T(8,128)}), f32[4,88,256]{2,1,0:T(8,128)S(1)}, u32[]{:S(2)}, u32[]{:S(2)}) async-start(f32[4,88,256]{2,1,0:T(8,128)} %broadcast_in_dim.8), calls=%async_computation.3 | async-start | bytes 720896 | tf_op jit(solution)/shard_map/all_to_all | solution.py:154
  144.2 9.2 %all-to-all-done.3 = f32[4,88,256]{2,1,0:T(8,128)S(1)} async-done(((f32[4,88,256]{2,1,0:T(8,128)}), f32[4,88,256]{2,1,0:T(8,128)S(1)}, u32[]{:S(2)}, u32[]{:S(2)}) %all-to-all-start.3) | async-done | bytes 360480 | tf_op jit(solution)/shard_map/all_to_all | solution.py:154
  153.5 14.6 %all_to_all.41 = f32[16,88,128]{2,1,0:T(8,128)S(1)} all-to-all(f32[16,88,128]{2,1,0:T(8,128)S(1)} %broadcast_in_dim.9), channel_id=1, replica_groups=mesh['far'=4,'near'=4,'y'=4,'core'=2,'x'=4] {'y','x'}, dimensions={0} | all-to-all | bytes 1441792 | tf_op jit(solution)/shard_map/all_to_all | solution.py:154
  168.2 6.0 %collective-permute-start.5 = (f32[4,4,88,128]{3,2,1,0:T(8,128)S(1)}, f32[4,4,88,128]{3,2,1,0:T(8,128)S(1)}, u32[]{:S(2)}, u32[]{:S(2)}) collective-permute-start(f32[4,4,88,128]{3,2,1,0:T(8,128)S(1)} %bitcast.62), channel_id=1, source_target_pairs={{0,4},{4,0},{1,5},{5,1},{2,6},{6,2},{3,7},{7,3},{8,12},{12,8},{9,1... | collective-permute-start | bytes 2162696 | tf_op jit(solution)/shard_map/ppermute | solution.py:223
  174.2 1.6 collective-permute-done.5
  176.0 0.8 fusion.22
  176.7 1.3 fusion.21
  178.1 0.2 pad_maximum_fusion.2
  178.3 0.7 fusion.3
  179.0 0.3 fusion.29
  179.3 0.4 fusion.4
  179.6 0.3 fusion.30
  179.9 0.1 constant_dynamic-slice_fusion.2
  180.0 2.3 %collective-permute-start.6 = (f32[352,256]{1,0:T(8,128)S(1)}, f32[352,256]{1,0:T(8,128)S(1)}, u32[]{:S(2)}, u32[]{:S(2)}) collective-permute-start(f32[352,256]{1,0:T(8,128)S(1)} %pad_maximum_fusion.4), channel_id=1, source_target_pairs={{0,4},{4,0},{1,5},{5,1},{2,6},{6,2},{3,7},{7,3},{8,12},{12,8},{9,1... | collective-permute-start | bytes 1081352 | tf_op jit(solution)/shard_map/ppermute | solution.py:213
  182.3 1.3 collective-permute-done.6
  183.6 9.9 %all_to_all.42 = f32[4,88,256]{2,1,0:T(8,128)S(1)} all-to-all(f32[4,88,256]{2,1,0:T(8,128)S(1)} %bitcast.66), channel_id=1, replica_groups=mesh['far'=4,'near'=4,'y'=4,'core'=2,'x'=4] {'y'}, dimensions={0} | all-to-all | bytes 720896 | tf_op jit(solution)/shard_map/all_to_all | solution.py:214
  193.6 12.7 %all_to_all.43 = f32[4,88,256]{2,1,0:T(8,128)S(1)} all-to-all(f32[4,88,256]{2,1,0:T(8,128)S(1)} %broadcast_in_dim.10), channel_id=1, replica_groups=mesh['far'=4,'near'=4,'y'=4,'core'=2,'x'=4] {'near'}, dimensions={0} | all-to-all | bytes 720896 | tf_op jit(solution)/shard_map/all_to_all | solution.py:154
  206.3 0.8 broadcast_in_dim.11
  207.1 5.9 %all-to-all-start.7 = ((f32[8,88,128]{2,1,0:T(8,128)}), f32[8,88,128]{2,1,0:T(8,128)S(1)}, u32[]{:S(2)}, u32[]{:S(2)}) async-start(f32[8,88,128]{2,1,0:T(8,128)} %broadcast_in_dim.11), calls=%async_computation.7 | async-start | bytes 720896 | tf_op jit(solution)/shard_map/all_to_all | solution.py:154
  213.0 0.1 constant_dynamic-slice_fusion.4
  213.1 0.7 copy.29
  213.9 6.9 %all-to-all-done.7 = f32[8,88,128]{2,1,0:T(8,128)S(1)} async-done(((f32[8,88,128]{2,1,0:T(8,128)}), f32[8,88,128]{2,1,0:T(8,128)S(1)}, u32[]{:S(2)}, u32[]{:S(2)}) %all-to-all-start.7) | async-done | bytes 360480 | tf_op jit(solution)/shard_map/all_to_all | solution.py:154
  220.8 0.2 copy.28
  220.9 0.8 copy.33
  (33 shorter events, 0.8 us)
Async XLA Ops:
  0.6 14.2 %copy-start.3 = (s32[4096]{0:T(1024)S(1)}, s32[4096]{0:T(1024)}, u32[]{:S(2)}) copy-start(s32[4096]{0:T(1024)} %param.11) | copy-start | bytes 49156
  4.5 12.7 %collective-permute-start = (f32[2048,256]{1,0:T(8,128)S(1)}, f32[2048,256]{1,0:T(8,128)}, u32[]{:S(2)}, u32[]{:S(2)}) collective-permute-start(f32[2048,256]{1,0:T(8,128)S(1)} %shard_map.104.own_ref), channel_id=1, source_target_pairs={{0,4},{4,0},{1,5},{5,1},{2,6},{6,2},{3,7},{7,3},{8,12},{12,8},{9,1... | collective-permute-start | bytes 6291464 | tf_op jit(solution)/shard_map/ppermute | solution.py:175
  22.5 3.8 %copy-start = (f32[352,256]{1,0:T(8,128)S(1)}, f32[352,256]{1,0:T(8,128)}, u32[]{:S(2)}) copy-start(f32[352,256]{1,0:T(8,128)} %param.14) | copy-start | bytes 1081348
  22.5 3.8 %copy-start.1 = (s32[352,256]{1,0:T(8,128)S(1)}, s32[352,256]{1,0:T(8,128)}, u32[]{:S(2)}) copy-start(s32[352,256]{1,0:T(8,128)} %param.12) | copy-start | bytes 1081348
  22.5 5.8 %copy-start.2 = (f32[32,352]{1,0:T(8,128)S(1)}, f32[32,352]{1,0:T(8,128)}, u32[]{:S(2)}) copy-start(f32[32,352]{1,0:T(8,128)} %param.13) | copy-start | bytes 135172
  22.5 29.8 %all-to-all-start = ((f32[4,1024,128]{2,1,0:T(8,128)}), f32[4,1024,128]{2,1,0:T(8,128)S(1)}, u32[]{:S(2)}, u32[]{:S(2)}) async-start(f32[4,1024,128]{2,1,0:T(8,128)} %bitcast.61), calls=%async_computation | async-start | bytes 4194304 | tf_op jit(solution)/shard_map/all_to_all | solution.py:183
  26.3 23.2 %collective-permute-start.1 = (f32[352,256]{1,0:T(8,128)S(1)}, f32[352,256]{1,0:T(8,128)S(1)}, u32[]{:S(2)}, u32[]{:S(2)}) collective-permute-start(f32[352,256]{1,0:T(8,128)S(1)} %convert_multiply_fusion), channel_id=1, source_target_pairs={{0,2},{1,3},{2,0},{3,1},{4,6},{5,7},{6,4},{7,5},{8,10},{9,11},{10,... | collective-permute-start | bytes 1081352 | tf_op jit(solution)/shard_map/ppermute | solution.py:172
  53.3 32.4 %all-to-all-start.1 = ((f32[16,64,128]{2,1,0:T(8,128)}), f32[16,64,128]{2,1,0:T(8,128)S(1)}, u32[]{:S(2)}, u32[]{:S(2)}) async-start(f32[16,64,128]{2,1,0:T(8,128)} %bitcast.7), calls=%async_computation.1 | async-start | bytes 1048576 | tf_op jit(solution)/shard_map/all_to_all | solution.py:189
  63.1 10.3 %collective-permute-start.3 = (f32[352,256]{1,0:T(8,128)S(1)}, f32[352,256]{1,0:T(8,128)S(1)}, u32[]{:S(2)}, u32[]{:S(2)}) collective-permute-start(f32[352,256]{1,0:T(8,128)S(1)} %convert_multiply_fusion), channel_id=1, source_target_pairs={{0,3},{1,0},{2,1},{3,2},{4,7},{5,4},{6,5},{7,6},{8,11},{9,8},{10,9... | collective-permute-start | bytes 1081352 | tf_op jit(solution)/shard_map/ppermute | solution.py:172
  67.5 10.9 %collective-permute-start.2 = (f32[352,256]{1,0:T(8,128)S(1)}, f32[352,256]{1,0:T(8,128)S(1)}, u32[]{:S(2)}, u32[]{:S(2)}) collective-permute-start(f32[352,256]{1,0:T(8,128)S(1)} %convert_multiply_fusion), channel_id=1, source_target_pairs={{0,1},{1,2},{2,3},{3,0},{4,5},{5,6},{6,7},{7,4},{8,9},{9,10},{10,1... | collective-permute-start | bytes 1081352 | tf_op jit(solution)/shard_map/ppermute | solution.py:172
  119.0 9.6 %collective-permute-start.4 = (f32[352,256]{1,0:T(8,128)S(1)}, f32[352,256]{1,0:T(8,128)S(1)}, u32[]{:S(2)}, u32[]{:S(2)}) collective-permute-start(f32[352,256]{1,0:T(8,128)S(1)} %pad_maximum_fusion.3), channel_id=1, source_target_pairs={{0,4},{4,0},{1,5},{5,1},{2,6},{6,2},{3,7},{7,3},{8,12},{12,8},{9,1... | collective-permute-start | bytes 1081352 | tf_op jit(solution)/shard_map/ppermute | solution.py:213
  139.3 14.1 %all-to-all-start.3 = ((f32[4,88,256]{2,1,0:T(8,128)}), f32[4,88,256]{2,1,0:T(8,128)S(1)}, u32[]{:S(2)}, u32[]{:S(2)}) async-start(f32[4,88,256]{2,1,0:T(8,128)} %broadcast_in_dim.8), calls=%async_computation.3 | async-start | bytes 720896 | tf_op jit(solution)/shard_map/all_to_all | solution.py:154
  168.2 7.6 %collective-permute-start.5 = (f32[4,4,88,128]{3,2,1,0:T(8,128)S(1)}, f32[4,4,88,128]{3,2,1,0:T(8,128)S(1)}, u32[]{:S(2)}, u32[]{:S(2)}) collective-permute-start(f32[4,4,88,128]{3,2,1,0:T(8,128)S(1)} %bitcast.62), channel_id=1, source_target_pairs={{0,4},{4,0},{1,5},{5,1},{2,6},{6,2},{3,7},{7,3},{8,12},{12,8},{9,1... | collective-permute-start | bytes 2162696 | tf_op jit(solution)/shard_map/ppermute | solution.py:223
  180.0 3.6 %collective-permute-start.6 = (f32[352,256]{1,0:T(8,128)S(1)}, f32[352,256]{1,0:T(8,128)S(1)}, u32[]{:S(2)}, u32[]{:S(2)}) collective-permute-start(f32[352,256]{1,0:T(8,128)S(1)} %pad_maximum_fusion.4), channel_id=1, source_target_pairs={{0,4},{4,0},{1,5},{5,1},{2,6},{6,2},{3,7},{7,3},{8,12},{12,8},{9,1... | collective-permute-start | bytes 1081352 | tf_op jit(solution)/shard_map/ppermute | solution.py:213
  207.1 13.7 %all-to-all-start.7 = ((f32[8,88,128]{2,1,0:T(8,128)}), f32[8,88,128]{2,1,0:T(8,128)S(1)}, u32[]{:S(2)}, u32[]{:S(2)}) async-start(f32[8,88,128]{2,1,0:T(8,128)} %broadcast_in_dim.11), calls=%async_computation.7 | async-start | bytes 720896 | tf_op jit(solution)/shard_map/all_to_all | solution.py:154
